TPU v7x, 128 devices: a whole 4x4x4 slice. The times are simulated.
128 devices in a mesh: dom: 64 (over y, x, z), seed: 2 (over core).
Axes of the slice: x: 4, y: 4, z: 4, core: 2. Of those that a mesh axis runs over, the one named last changes fastest.
Arguments:
- rank_in: float32 [128, 1048576], P('seed', 'dom'), as said below
- band_tiles: bfloat16 [8192, 3, 128, 128], P('dom'), as said below
- off_tiles: bfloat16 [32768, 128, 128], P('dom'), as said below
- tile_src: int32 [64, 512], P('dom'), may hold values from 0 to 8191, as said below
- tile_row: int32 [64, 512], P('dom'), may hold values from 0 to 127
- tile_count: int32 [64], P('dom'), may hold values from 256 to 512, as said below
- seed_ids: int32 [128], P('seed'), may hold values from 0 to 1048575
- dangling: int32 [1048576], P('dom'), may hold values 0 or 1
Outputs:
- rank_out: float32 [128, 1048576], P('seed', 'dom')
- change: float32 [3, 128], P(None, 'seed')
- total_change: float32 [3], replicated
- seed_score: float32 [128], P('seed')
Inputs may be any that keep to these rules, and one draw needn't show every extreme that they name: `rank_in`: positive. `band_tiles`: nonnegative transition weights. `off_tiles`: nonnegative transition weights. `tile_src`: every source block is held by another index of dom than the tile; the live tiles of one index of dom read at most 2 distinct blocks held by any one other index. The first tile_count[g] slots of index g are live, the rest are padding.
All inputs are finite; a program needn't handle non-finite values. No bound on the sum of `dangling` on one device may be relied on, other than what follows from the above.
Results may differ from a plain program's by a relative error of at most 0.0003.
Values may be sent and summed in bfloat16 or wider, within the bound.
No kernel may reach another device: no remote copies, remote signals or barrier semaphores. Data moves between devices by JAX's collectives and lax.ppermute only.
A program may use at most 192 MiB of HBM per device.

v0:
```python
import jax
import jax.numpy as jnp
from jax import lax
from jax.sharding import PartitionSpec as P

CAP = 2
ITERS = 3


DAMP = 0.85


def extended(cells, sides, width):
    for axis, dim in sides:
        count = lax.axis_size(axis)
        ends = count - 1
        head = lax.slice_in_dim(cells, 0, width, axis=dim)
        tail = lax.slice_in_dim(cells, cells.shape[dim] - width, cells.shape[dim], axis=dim)
        cells = jnp.concatenate(
            [
                lax.ppermute(tail, axis, [(i, (i + 1) % count) for i in range(ends)]),
                cells,
                lax.ppermute(head, axis, [((i + 1) % count, i) for i in range(ends)]),
            ],
            axis=dim,
        )
    return cells


def plan_requests(tile_src, tile_count, blocks):
    peer_count = lax.axis_size("dom")
    slot_count = tile_src.shape[1]
    source_ids = tile_src[0]
    live_slots = jnp.arange(slot_count, dtype=jnp.int32) < tile_count[0]
    all_blocks = jnp.arange(blocks * peer_count, dtype=jnp.int32)
    hit_table = jnp.logical_and(source_ids[:, None] == all_blocks[None, :], live_slots[:, None])
    needed = (
        (jnp.sum(hit_table.astype(jnp.int32), axis=0) > 0)
        .astype(jnp.int32)
        .reshape(peer_count, blocks)
    )
    slot_table = jnp.cumsum(needed, axis=1) - 1
    slot_match = needed[:, :, None] * (
        slot_table[:, :, None] == jnp.arange(CAP, dtype=jnp.int32)[None, None, :]
    ).astype(jnp.int32)
    request = jnp.sum(slot_match * jnp.arange(blocks, dtype=jnp.int32)[None, :, None], axis=1)
    wanted = lax.all_to_all(request, "dom", split_axis=0, concat_axis=0, tiled=True)
    holders = source_ids // blocks
    tile_slot = holders * CAP + jnp.take(slot_table.reshape(-1), source_ids)
    tile_slot = jnp.maximum(tile_slot, 0)
    return (wanted, tile_slot, live_slots)


def gather_requested(source, wanted):
    seed_cols, blocks, block_width = source.shape
    peer_count, slots_per = wanted.shape
    outgoing = jnp.take(source, wanted.reshape(-1), axis=1).reshape(
        seed_cols, peer_count, slots_per, block_width
    )
    fetched = lax.all_to_all(outgoing, "dom", split_axis=1, concat_axis=1, tiled=True)
    return fetched.reshape(seed_cols, peer_count * slots_per, block_width)


def on_device(rank_in, band_tiles, off_tiles, tile_src, tile_row, tile_count, seed_ids, dangling):
    blocks = band_tiles.shape[0]
    block_width = band_tiles.shape[2]
    seed_cols = rank_in.shape[0]
    peer_count = lax.axis_size("dom")
    groups = lax.axis_size("seed")
    vertices = blocks * block_width * peer_count
    wanted, tile_slot, live_slots = plan_requests(tile_src, tile_count, blocks)
    tile_rows = jnp.where(live_slots, tile_row[0], blocks)
    first_vertex = lax.axis_index("dom") * (blocks * block_width)
    vertex_ids = first_vertex + jnp.arange(blocks * block_width, dtype=jnp.int32)
    seed_mask = (seed_ids[:, None] == vertex_ids[None, :]).astype(jnp.float32)
    restart = (1.0 - DAMP) * seed_mask
    dead_ends = dangling.astype(jnp.float32)
    keep_share = 1.0 - dead_ends
    rank_now = rank_in
    history = []
    own_total = jnp.zeros((seed_cols,), jnp.float32)
    for iteration in range(ITERS):
        mass_term = jnp.sum(rank_now * dead_ends[None, :], axis=1)
        dead_mass = lax.psum(mass_term, "dom")
        source = (
            (rank_now * keep_share[None, :])
            .astype(jnp.bfloat16)
            .reshape(seed_cols, blocks, block_width)
        )
        padded = extended(source, (("dom", 1),), 1)
        fetched = gather_requested(source, wanted)
        stacked = jnp.stack(
            [padded[:, 0:blocks], padded[:, 1 : blocks + 1], padded[:, 2 : blocks + 2]], axis=2
        )
        banded = jnp.einsum(
            "sbkj,bkij->bsi", stacked, band_tiles, preferred_element_type=jnp.float32
        )
        operands = jnp.take(fetched, tile_slot, axis=1)
        products = jnp.einsum(
            "stj,tij->tsi", operands, off_tiles, preferred_element_type=jnp.float32
        )
        remote = jax.ops.segment_sum(products, tile_rows, num_segments=blocks + 1)[:blocks]
        linked = jnp.transpose(banded + remote, (1, 0, 2)).reshape(seed_cols, blocks * block_width)
        updated = DAMP * (linked + dead_mass[:, None] / vertices) + restart
        gap_here = jnp.sum(jnp.abs(updated - rank_now), axis=1)
        if iteration + 1 < ITERS:
            moved_total = lax.psum(gap_here, "dom")
        else:
            own_here = jnp.sum(updated * seed_mask, axis=1)
            moved_total, own_total = lax.psum((gap_here, own_here), "dom")
        history.append(moved_total / vertices)
        rank_now = updated
    change = jnp.stack(history)
    total_change = lax.psum(jnp.sum(change, axis=1), "seed") / (seed_cols * groups)
    return (rank_now, change, total_change, own_total)


def solution(mesh):
    return jax.shard_map(
        on_device,
        mesh=mesh,
        in_specs=(
            P("seed", "dom"),
            P("dom", None, None, None),
            P("dom", None, None),
            P("dom", None),
            P("dom", None),
            P("dom"),
            P("seed"),
            P("dom"),
        ),
        out_specs=(P("seed", "dom"), P(None, "seed"), P(), P("seed")),
        check_vma=False,
    )
```

profile of v0, /device:TPU:1, one launch (start us, length us, event | category | flops | bytes accessed | tf_op | source)
XLA Modules:
  0.0 1224.1 jit_solution(12480250764925267797)
XLA Ops:
  1.3 5.1 convert_reduce_fusion
  7.6 12.0 all-to-all-start
  34.6 8.3 all-to-all-start.1
  51.0 154.3 %psum.56 = f32[64]{0:T(128)S(1)} all-reduce(f32[64]{0:T(128)S(1)} %get-tuple-element.23), channel_id=1, replica_groups=mesh['dom'=64,'seed'=2] {'dom'}, use_global_device_ids=true, to_apply=%region_5.8 | all-reduce | flops 64 | bytes 512 | tf_op jit(solution)/shard_map/psum | solution.py:84
  212.8 13.5 %gather_fusion.2 = bf16[512,64,128]{2,1,0:T(8,128)(2,1)} fusion(bf16[64,128,128]{2,0,1:T(8,128)(2,1)S(1)} %bitcast.125, s32[1024]{0:T(1024)S(1)} %pad_clamp_fusion), kind=kCustom, calls=%fused_computation.1.clone | custom fusion | bytes 16779264 | tf_op jit(solution)/shard_map/jit(_take)/gather | solution.py:98
  226.2 20.4 %fusion.9 = f32[512,64,128]{2,1,0:T(8,128)} fusion(bf16[512,128,128]{2,1,0:T(8,128)(2,1)} %param.14, bf16[512,64,128]{2,1,0:T(8,128)(2,1)} %gather_fusion.2, pred[512]{0:T(512)(128)(4,1)S(1)} %get-tuple-element.15), kind=kOutput, calls=%fused_computation.21 | convolution fusion | flops 1077936128 | bytes 41943552 | tf_op jit(solution)/shard_map/stj,tij->tsi/dot_general | solution.py:99
  249.1 83.5 %scatter_fusion = f32[129,64,128]{2,1,0:T(8,128)} fusion(f32[129,64,128]{2,1,0:T(8,128)} %broadcast.296.clone, s32[512]{0:T(512)S(1)} %bitcast.137, f32[512,64,128]{2,1,0:T(8,128)} %fusion.9), kind=kCustom, calls=%fused_computation.7 | custom fusion | flops 4194304 | bytes 50333696 | tf_op jit(solution)/shard_map/scatter-add | solution.py:102
  332.6 12.0 multiply_reduce_fusion.1
  349.9 4.7 all-to-all-start.2
  359.4 154.3 %psum.57 = f32[64]{0:T(128)S(1)} all-reduce(f32[64]{0:T(128)S(1)} %get-tuple-element.17), channel_id=1, replica_groups=mesh['dom'=64,'seed'=2] {'dom'}, use_global_device_ids=true, to_apply=%region_8.11 | all-reduce | flops 64 | bytes 512 | tf_op jit(solution)/shard_map/psum | solution.py:84
  513.8 4.6 fusion.60
  518.3 13.5 %gather_fusion.4 = bf16[512,64,128]{2,1,0:T(8,128)(2,1)} fusion(bf16[64,128,128]{2,0,1:T(8,128)(2,1)S(1)} %bitcast.127, s32[1024]{0:T(1024)S(1)} %pad_clamp_fusion), kind=kCustom, calls=%fused_computation.4.clone | custom fusion | bytes 16779264 | tf_op jit(solution)/shard_map/jit(_take)/gather | solution.py:98
  531.8 20.4 %fusion.7 = f32[512,64,128]{2,1,0:T(8,128)} fusion(bf16[512,128,128]{2,1,0:T(8,128)(2,1)} %param.14, bf16[512,64,128]{2,1,0:T(8,128)(2,1)} %gather_fusion.4, pred[512]{0:T(512)(128)(4,1)S(1)} %get-tuple-element.15), kind=kOutput, calls=%fused_computation.19 | convolution fusion | flops 1077936128 | bytes 41943552 | tf_op jit(solution)/shard_map/stj,tij->tsi/dot_general | solution.py:99
  554.7 83.5 %scatter_fusion.1 = f32[129,64,128]{2,1,0:T(8,128)} fusion(f32[129,64,128]{2,1,0:T(8,128)} %broadcast.296.clone.1, s32[512]{0:T(512)S(1)} %bitcast.138, f32[512,64,128]{2,1,0:T(8,128)} %fusion.7), kind=kCustom, calls=%fused_computation.8 | custom fusion | flops 4194304 | bytes 50333696 | tf_op jit(solution)/shard_map/scatter-add | solution.py:102
  638.2 12.0 multiply_reduce_fusion
  655.5 4.7 all-to-all-start.3
  665.1 154.3 %psum.58 = f32[64]{0:T(128)S(1)} all-reduce(f32[64]{0:T(128)S(1)} %get-tuple-element.21), channel_id=1, replica_groups=mesh['dom'=64,'seed'=2] {'dom'}, use_global_device_ids=true, to_apply=%region_11.14 | all-reduce | flops 64 | bytes 512 | tf_op jit(solution)/shard_map/psum | solution.py:84
  824.0 13.5 %gather_fusion.6 = bf16[512,64,128]{2,1,0:T(8,128)(2,1)} fusion(bf16[64,128,128]{2,0,1:T(8,128)(2,1)S(1)} %bitcast.126, s32[1024]{0:T(1024)S(1)} %pad_clamp_fusion), kind=kCustom, calls=%fused_computation.5.clone | custom fusion | bytes 16779264 | tf_op jit(solution)/shard_map/jit(_take)/gather | solution.py:98
  837.4 20.4 %fusion.5 = f32[512,64,128]{2,1,0:T(8,128)} fusion(bf16[512,128,128]{2,1,0:T(8,128)(2,1)} %param.14, bf16[512,64,128]{2,1,0:T(8,128)(2,1)} %gather_fusion.6, pred[512]{0:T(512)(128)(4,1)S(1)} %get-tuple-element.15), kind=kOutput, calls=%fused_computation.17 | convolution fusion | flops 1077936128 | bytes 41943552 | tf_op jit(solution)/shard_map/stj,tij->tsi/dot_general | solution.py:99
  860.3 83.5 %scatter_fusion.2 = f32[129,64,128]{2,1,0:T(8,128)} fusion(f32[129,64,128]{2,1,0:T(8,128)} %broadcast.296, s32[512]{0:T(512)S(1)} %bitcast.139, f32[512,64,128]{2,1,0:T(8,128)} %fusion.5), kind=kCustom, calls=%fused_computation.9 | custom fusion | flops 4194304 | bytes 50333696 | tf_op jit(solution)/shard_map/scatter-add | solution.py:102
  943.9 14.2 %fusion.36 = (f32[64]{0:T(128)S(1)}, f32[64]{0:T(128)S(1)}, f32[64]{0:T(128)S(1)}, f32[128,64,128]{2,1,0:T(8,128)}) fusion(f32[64]{0:T(128)S(1)} %broadcast_multiply_fusion.1, s32[128,128]{1,0:T(8,128)S(1)} %add_add_fusion, s32[64]{0:T(128)S(1)} %copy-done.7, f32[64,128,128]{2,0,1:T(8,128)} %get-tuple-element.45, f32[64]{0:T(128)S(1)} %broadcast_multiply_fusion.3, ...), kind=kOutput, calls=%fused_computation.54 | convolution fusion | flops 829423424 | bytes 35718656 | tf_op jit(solution)/shard_map/sbkj,bkij->bsi/dot_general | solution.py:95
  958.1 7.0 fusion.35
  965.0 144.8 %all-reduce = (f32[64]{0:T(128)S(1)}, f32[64]{0:T(128)S(1)}, f32[64]{0:T(128)S(1)}, f32[64]{0:T(128)}) all-reduce(f32[64]{0:T(128)S(1)} %get-tuple-element.7, f32[64]{0:T(128)S(1)} %get-tuple-element.8, f32[64]{0:T(128)S(1)} %get-tuple-element.36, f32[64]{0:T(128)S(1)} %get-tuple-element.6), channel_id=1, replica_groups=mesh['dom'=64,'seed'=2] {'dom'}, use_global_device_ids=true, to_apply=%region_17.20 | all-reduce | flops 256 | bytes 2048 | tf_op jit(solution)/shard_map/psum | solution.py:110
  1110.5 112.9 %psum.62 = f32[3]{0:T(128)S(1)} all-reduce(f32[3]{0:T(128)S(1)} %get-tuple-element.13), channel_id=1, replica_groups=mesh['dom'=64,'seed'=2] {'seed'}, use_global_device_ids=true, to_apply=%region_19.22 | all-reduce | flops 3 | bytes 24 | tf_op jit(solution)/shard_map/psum | solution.py:114
  (79 shorter events, 65.2 us)
Async XLA Ops:
  7.6 20.3 %all-to-all-start = ((s32[64,1,2]{2,1,0:T(1,128)}), s32[64,1,2]{2,1,0:T(1,128)S(1)}, u32[]{:S(2)}, u32[]{:S(2)}) async-start(s32[64,1,2]{2,1,0:T(1,128)} %copy.53), calls=%async_computation | async-start | bytes 65536 | tf_op jit(solution)/shard_map/all_to_all | solution.py:47
  26.1 8.5 copy-start
  31.4 16.4 %copy-start.5 = (s32[1,512]{1,0:T(1,128)S(1)}, s32[1,512]{1,0:T(1,128)}, u32[]{:S(2)}) copy-start(s32[1,512]{1,0:T(1,128)} %param.15) | copy-start | bytes 6148
  34.6 170.8 %copy-start.6 = (s32[1,512]{1,0:T(1,128)S(1)}, s32[1,512]{1,0:T(1,128)}, u32[]{:S(2)}) copy-start(s32[1,512]{1,0:T(1,128)} %param.16) | copy-start | bytes 6148
  34.6 178.2 %all-to-all-start.1 = ((bf16[64,64,2,128]{3,0,2,1:T(8,128)(2,1)}), bf16[64,64,2,128]{3,0,2,1:T(8,128)(2,1)S(1)}, u32[]{:S(2)}, u32[]{:S(2)}) async-start(bf16[64,64,2,128]{3,0,2,1:T(8,128)(2,1)} %bitcast.133), calls=%async_computation.1 | async-start | bytes 4194304 | tf_op jit(solution)/shard_map/all_to_all | solution.py:60
  43.6 166.9 %collective-permute-start = (bf16[64,1,128]{2,0,1:T(8,128)(2,1)S(1)}, bf16[64,1,128]{2,0,1:T(8,128)(2,1)S(1)}, u32[]{:S(2)}, u32[]{:S(2)}) collective-permute-start(bf16[64,1,128]{2,0,1:T(8,128)(2,1)S(1)} %get-tuple-element.34), channel_id=1, source_target_pairs={{0,2},{2,4},{4,6},{6,8},{8,10},{10,12},{12,14},{14,16},{16,18},{18... | collective-permute-start | bytes 49160 | tf_op jit(solution)/shard_map/ppermute | solution.py:21
  46.5 164.0 %collective-permute-start.1 = (bf16[64,1,128]{2,0,1:T(8,128)(2,1)S(1)}, bf16[64,1,128]{2,0,1:T(8,128)(2,1)S(1)}, u32[]{:S(2)}, u32[]{:S(2)}) collective-permute-start(bf16[64,1,128]{2,0,1:T(8,128)(2,1)S(1)} %get-tuple-element.35), channel_id=1, source_target_pairs={{2,0},{4,2},{6,4},{8,6},{10,8},{12,10},{14,12},{16,14},{18,16},{20... | collective-permute-start | bytes 49160 | tf_op jit(solution)/shard_map/ppermute | solution.py:23
  205.4 5.0 copy-start.1
  249.1 83.5 %copy-start.7 = (s32[64]{0:T(128)S(1)}, s32[64]{0:T(128)}, u32[]{:S(2)}) copy-start(s32[64]{0:T(128)} %param.18) | copy-start | bytes 772
  344.6 5.3 copy-start.4
  349.9 168.5 %all-to-all-start.2 = ((bf16[64,64,2,128]{3,0,2,1:T(8,128)(2,1)}), bf16[64,64,2,128]{3,0,2,1:T(8,128)(2,1)S(1)}, u32[]{:S(2)}, u32[]{:S(2)}) async-start(bf16[64,64,2,128]{3,0,2,1:T(8,128)(2,1)} %bitcast.135), calls=%async_computation.2 | async-start | bytes 4194304 | tf_op jit(solution)/shard_map/all_to_all | solution.py:60
  355.3 158.4 %collective-permute-start.2 = (bf16[64,1,128]{2,0,1:T(8,128)(2,1)S(1)}, bf16[64,1,128]{2,0,1:T(8,128)(2,1)S(1)}, u32[]{:S(2)}, u32[]{:S(2)}) collective-permute-start(bf16[64,1,128]{2,0,1:T(8,128)(2,1)S(1)} %get-tuple-element.30), channel_id=1, source_target_pairs={{0,2},{2,4},{4,6},{6,8},{8,10},{10,12},{12,14},{14,16},{16,18},{18... | collective-permute-start | bytes 49160 | tf_op jit(solution)/shard_map/ppermute | solution.py:21
  358.1 155.6 %collective-permute-start.3 = (bf16[64,1,128]{2,0,1:T(8,128)(2,1)S(1)}, bf16[64,1,128]{2,0,1:T(8,128)(2,1)S(1)}, u32[]{:S(2)}, u32[]{:S(2)}) collective-permute-start(bf16[64,1,128]{2,0,1:T(8,128)(2,1)S(1)} %get-tuple-element.31), channel_id=1, source_target_pairs={{2,0},{4,2},{6,4},{8,6},{10,8},{12,10},{14,12},{16,14},{18,16},{20... | collective-permute-start | bytes 49160 | tf_op jit(solution)/shard_map/ppermute | solution.py:23
  650.2 5.4 copy-start.2
  655.5 168.4 %all-to-all-start.3 = ((bf16[64,64,2,128]{3,0,2,1:T(8,128)(2,1)}), bf16[64,64,2,128]{3,0,2,1:T(8,128)(2,1)S(1)}, u32[]{:S(2)}, u32[]{:S(2)}) async-start(bf16[64,64,2,128]{3,0,2,1:T(8,128)(2,1)} %bitcast.134), calls=%async_computation.3 | async-start | bytes 4194304 | tf_op jit(solution)/shard_map/all_to_all | solution.py:60
  661.0 158.4 %collective-permute-start.4 = (bf16[64,1,128]{2,0,1:T(8,128)(2,1)S(1)}, bf16[64,1,128]{2,0,1:T(8,128)(2,1)S(1)}, u32[]{:S(2)}, u32[]{:S(2)}) collective-permute-start(bf16[64,1,128]{2,0,1:T(8,128)(2,1)S(1)} %get-tuple-element.26), channel_id=1, source_target_pairs={{0,2},{2,4},{4,6},{6,8},{8,10},{10,12},{12,14},{14,16},{16,18},{18... | collective-permute-start | bytes 49160 | tf_op jit(solution)/shard_map/ppermute | solution.py:21
  663.8 155.6 %collective-permute-start.5 = (bf16[64,1,128]{2,0,1:T(8,128)(2,1)S(1)}, bf16[64,1,128]{2,0,1:T(8,128)(2,1)S(1)}, u32[]{:S(2)}, u32[]{:S(2)}) collective-permute-start(bf16[64,1,128]{2,0,1:T(8,128)(2,1)S(1)} %get-tuple-element.27), channel_id=1, source_target_pairs={{2,0},{4,2},{6,4},{8,6},{10,8},{12,10},{14,12},{16,14},{18,16},{20... | collective-permute-start | bytes 49160 | tf_op jit(solution)/shard_map/ppermute | solution.py:23
  860.3 83.5 %copy-start.3 = (bf16[64,128,128]{2,0,1:T(8,128)(2,1)S(1)}, bf16[64,128,128]{2,0,1:T(8,128)(2,1)}, u32[]{:S(2)}) copy-start(bf16[64,128,128]{2,0,1:T(8,128)(2,1)} %copy-done.2) | copy-start | bytes 6291460
where the time goes:
time: 1230 us; the launch traced here: 1220 us
  blocking collectives  721 us (59%)
  other arithmetic  292 us (24%)
  matrix products  99.4 us (8%)
  local copies, waits for them, and re-layouts  66.6 us (5%)
  starting transfers between devices  42 us (3%)
    psum x3, blocking collectives, on_device(): dead_mass = lax.psum(mass_term, 'dom')  463 us
    scatter-add x3, other arithmetic, on_device(): jax.ops.segment_sum(products, tile_rows, num_segments=blocks + 1)[:blocks]  250 us
    psum x1, blocking collectives, on_device(): moved_total, own_total = lax.psum((gap_here, own_here), 'dom')  145 us
    psum x1, blocking collectives, on_device(): lax.psum(jnp.sum(change, axis=1), 'seed') / (seed_cols * groups)  113 us
    dot_general x3, matrix products, on_device(): jnp.einsum('stj,tij->tsi', operands, off_tiles, preferred_element_type=jn...  61.3 us
    gather x3, local copies, waits for them, and re-layouts, on_device(): operands = jnp.take(fetched, tile_slot, axis=1)  40.4 us
    dot_general x3, matrix products, on_device(): jnp.einsum('sbkj,bkij->bsi', stacked, band_tiles, preferred_element_type=...  38.1 us
  transfers between devices with their start and end apart: 10, of which 1 were waited for; matrix products, arithmetic and copies ran while one was open for 2% of the time, Pallas kernels for 0%

commit v1 on v0

v1 whole, which is shorter than its diff:
```python
import functools

import jax
import jax.numpy as jnp
from jax import lax
from jax.experimental import pallas as pl
from jax.experimental.pallas import tpu as pltpu
from jax.sharding import PartitionSpec as P

CAP = 2
ITERS = 3
DAMP = 0.85

BF16 = jnp.bfloat16
F32 = jnp.float32
I32 = jnp.int32
VMEM = pltpu.VMEM
NT = (((1,), (1,)), ((), ()))
SLAB = 8
PARAMS = pltpu.CompilerParams(vmem_limit_bytes=52 << 20)


def vmem():
    return pl.BlockSpec(memory_space=pltpu.VMEM)


def smem():
    return pl.BlockSpec(memory_space=pltpu.SMEM)


def anywhere():
    return pl.BlockSpec(memory_space=pl.ANY)


def shaped(shape, dtype):
    return jax.ShapeDtypeStruct(shape, dtype)


def dot_nt(x, w):
    return lax.dot_general(x, w, NT, preferred_element_type=F32)


def plan_kernel(peers, blocks, count_ref, src_ref, row_ref, request_ref, slot_ref, target_ref):
    slots = src_ref.shape[1]
    ids = src_ref[...]
    live = lax.broadcasted_iota(I32, (1, slots), 1) < count_ref[0]
    holder = ids // blocks
    inside = (ids - holder * blocks).astype(F32)
    peer = lax.broadcasted_iota(I32, (peers, slots), 0)
    held = jnp.broadcast_to(holder, (peers, slots)) == peer
    asked = jnp.logical_and(held, jnp.broadcast_to(live, (peers, slots)))
    block_of = jnp.broadcast_to(inside, (peers, slots))
    low = jnp.min(jnp.where(asked, block_of, float(blocks - 1)), axis=1, keepdims=True)
    high = jnp.max(jnp.where(asked, block_of, 0.0), axis=1, keepdims=True)
    lane = lax.broadcasted_iota(I32, request_ref.shape, 1)
    request_ref[...] = jnp.where(lane == 0, low, high).astype(I32)
    low_of = jnp.sum(jnp.where(held, low, 0.0), axis=0, keepdims=True)
    slot_ref[...] = holder * CAP + jnp.where(inside == low_of, 0, 1)
    target_ref[...] = jnp.where(live, row_ref[...], blocks)


def plan(tile_count, tile_src, tile_row, peers, blocks):
    slots = tile_src.shape[1]
    return pl.pallas_call(
        functools.partial(plan_kernel, peers, blocks),
        out_shape=(shaped((peers, 128), I32), shaped((1, slots), I32), shaped((1, slots), I32)),
        in_specs=[smem(), vmem(), vmem()],
        out_specs=(vmem(), vmem(), vmem()),
        name="plan",
    )(tile_count, tile_src, tile_row)


def eye(rows):
    return lax.broadcasted_iota(I32, (rows, 128), 0) == lax.broadcasted_iota(I32, (rows, 128), 1)


def to_row(column):
    return jnp.sum(jnp.where(eye(column.shape[0]), column, 0.0), axis=0, keepdims=True)


def to_column(row, seeds):
    return jnp.sum(jnp.where(eye(seeds), row, 0.0), axis=1, keepdims=True)


def mass_slab(mass):
    row = to_row(jnp.sum(mass, axis=1, keepdims=True))
    high = row.astype(BF16).astype(F32)
    rest = row - high
    middle = rest.astype(BF16).astype(F32)
    low = rest - middle
    at = lax.broadcasted_iota(I32, (SLAB, 128), 0)
    slab = jnp.where(at == 0, high, jnp.where(at == 1, middle, jnp.where(at == 2, low, 0.0)))
    return slab.astype(BF16)


def prep_kernel(rank_hbm, dangling_ref, source_ref, slab_ref, head_ref, tail_ref, rank, sem):
    blocks, seeds, width = source_ref.shape
    chunks = sem.shape[0]
    per = blocks // chunks

    def fetch(c):
        cols = pl.ds(c * per * width, per * width)
        return pltpu.make_async_copy(rank_hbm.at[:, cols], rank.at[:, cols], sem.at[c])

    for c in range(chunks):
        fetch(c).start()
    mass = jnp.zeros((seeds, width), F32)
    for c in range(chunks):
        fetch(c).wait()
        for b in range(c * per, (c + 1) * per):
            old = rank[:, b * width : (b + 1) * width]
            dead = jnp.broadcast_to(dangling_ref[b : b + 1, :], (seeds, width)) != 0
            kept = jnp.where(dead, 0.0, old)
            mass += old - kept
            source_ref[b] = kept.astype(BF16)
    slab_ref[...] = mass_slab(mass)
    head_ref[...] = source_ref[0]
    tail_ref[...] = source_ref[blocks - 1]


def prep(rank, dangling, blocks):
    seeds = rank.shape[0]
    width = rank.shape[1] // blocks
    edge = shaped((seeds, width), BF16)
    return pl.pallas_call(
        prep_kernel,
        out_shape=(shaped((blocks, seeds, width), BF16), shaped((SLAB, 128), BF16), edge, edge),
        in_specs=[anywhere(), vmem()],
        out_specs=(vmem(),) * 4,
        scratch_shapes=[VMEM(rank.shape, F32), pltpu.SemaphoreType.DMA((8,))],
        compiler_params=PARAMS,
        name="prep",
    )(rank, dangling)


def pack(wanted, source, slab, message, out_hbm, sem):
    peers, _, _ = message.shape
    seeds = source.shape[1]
    parts = sem.shape[0]
    per = peers // parts

    def send(c):
        span = pl.ds(c * per, per)
        return pltpu.make_async_copy(message.at[span], out_hbm.at[span], sem.at[c])

    for c in range(parts):

        def one(p, carry):
            for k in range(CAP):
                message[p, k * seeds : (k + 1) * seeds, :] = source[wanted[p, k]]
            message[p, CAP * seeds :, :] = slab
            return carry

        lax.fori_loop(c * per, (c + 1) * per, one, 0, unroll=4)
        send(c).start()
    for c in range(parts):
        send(c).wait()


def pack_kernel(wanted_ref, source_ref, slab_ref, out_hbm, message, sem):
    pack(wanted_ref, source_ref, slab_ref[...], message, out_hbm, sem)


def pack_first(wanted, source, slab, peers):
    _, seeds, width = source.shape
    shape = (peers, CAP * seeds + SLAB, width)
    return pl.pallas_call(
        pack_kernel,
        out_shape=shaped(shape, BF16),
        in_specs=[smem(), vmem(), vmem()],
        out_specs=anywhere(),
        scratch_shapes=[VMEM(shape, BF16), pltpu.SemaphoreType.DMA((4,))],
        compiler_params=PARAMS,
        name="pack",
    )(wanted, source, slab)


def band_kernel(source_hbm, left_ref, right_ref, tiles_hbm, out_hbm, source, tiles, banded, sem, source_sem, out_sem):
    blocks, seeds, width = banded.shape
    chunks = sem.shape[0]
    per = blocks // chunks

    def fetch(c):
        span = pl.ds(c * per, per)
        return pltpu.make_async_copy(tiles_hbm.at[span], tiles.at[span], sem.at[c])

    def flush(c):
        span = pl.ds(c * per, per)
        return pltpu.make_async_copy(banded.at[span], out_hbm.at[span], out_sem.at[c])

    own = pltpu.make_async_copy(source_hbm, source.at[pl.ds(1, blocks)], source_sem)
    own.start()
    for c in range(chunks):
        fetch(c).start()
    source[0] = left_ref[...]
    source[blocks + 1] = right_ref[...]
    own.wait()
    for c in range(chunks):
        fetch(c).wait()
        for b in range(c * per, (c + 1) * per):
            x = jnp.concatenate([source[b], source[b + 1], source[b + 2]], axis=1)
            w = jnp.concatenate([tiles[b, 0], tiles[b, 1], tiles[b, 2]], axis=1)
            banded[b] = dot_nt(x, w)
        flush(c).start()
    for c in range(chunks):
        flush(c).wait()


def band(source, left, right, tiles):
    blocks, seeds, width = source.shape
    return pl.pallas_call(
        band_kernel,
        out_shape=shaped((blocks, seeds, width), F32),
        in_specs=[anywhere(), vmem(), vmem(), anywhere()],
        out_specs=anywhere(),
        scratch_shapes=[
            VMEM((blocks + 2, seeds, width), BF16),
            VMEM(tiles.shape, BF16),
            VMEM((blocks, seeds, width), F32),
            pltpu.SemaphoreType.DMA((8,)),
            pltpu.SemaphoreType.DMA,
            pltpu.SemaphoreType.DMA((8,)),
        ],
        compiler_params=PARAMS,
        name="band",
    )(source, left, right, tiles)


UNROLL = 32


def finish_kernel(last, vertices, *refs):
    (first_ref, count_ref, slot_ref, target_ref, wanted_ref, seed_ref, dangling_ref) = refs[:7]
    fetched_hbm, banded_hbm, rank_hbm, tiles_hbm = refs[7:11]
    if last:
        next_hbm, stats_ref = refs[11:13]
        scratch = refs[13:]
    else:
        next_hbm, stats_ref, source, head_ref, tail_ref, message_hbm, message, send_sem = refs[11:19]
        scratch = refs[19:]
    fetched, tiles, acc, rank, nxt, sem, tile_sem, rank_sem, out_sem = scratch
    blocks = acc.shape[0] - 1
    seeds, width = acc.shape[1:]
    peers = fetched.shape[0]
    chunks = tile_sem.shape[0]
    per = tiles.shape[0] // chunks
    parts = rank_sem.shape[0]
    span = blocks // parts

    def tile_copy(c):
        at = pl.ds(c * per, per)
        return pltpu.make_async_copy(tiles_hbm.at[at], tiles.at[at], tile_sem.at[c])

    def rank_copy(c):
        cols = pl.ds(c * span * width, span * width)
        return pltpu.make_async_copy(rank_hbm.at[:, cols], rank.at[:, cols], rank_sem.at[c])

    def rank_store(c):
        cols = pl.ds(c * span * width, span * width)
        return pltpu.make_async_copy(nxt.at[:, cols], next_hbm.at[:, cols], out_sem.at[c])

    got = pltpu.make_async_copy(fetched_hbm, fetched, sem.at[0])
    base = pltpu.make_async_copy(banded_hbm, acc.at[pl.ds(0, blocks)], sem.at[1])
    got.start()
    base.start()
    for c in range(chunks):
        tile_copy(c).start()
    for c in range(parts):
        rank_copy(c).start()
    got.wait()
    slabs = fetched[:, CAP * seeds :, :].astype(F32)
    mass_row = jnp.sum(jnp.sum(slabs, axis=0), axis=0, keepdims=True)
    share = jnp.broadcast_to(to_column(mass_row, seeds) / vertices, (seeds, width))
    acc[blocks] = jnp.zeros((seeds, width), F32)
    zero = jnp.zeros((seeds, width), BF16)
    base.wait()

    def operand(t):
        slot = slot_ref[0, t]
        at = pl.multiple_of((slot % CAP) * seeds, seeds)
        return fetched[slot // CAP, pl.ds(at, seeds), :]

    def group(g, carry):
        first = g * UNROLL
        products = []
        for u in range(0, UNROLL, 2):
            one, two = first + u, first + u + 1
            x = jnp.concatenate(
                [
                    jnp.concatenate([operand(one), zero], axis=1),
                    jnp.concatenate([zero, operand(two)], axis=1),
                ],
                axis=0,
            )
            y = dot_nt(x, jnp.concatenate([tiles[one], tiles[two]], axis=1))
            products += [y[:seeds], y[seeds:]]
        for u in range(UNROLL):
            row = target_ref[0, first + u]
            acc[row] = acc[row] + products[u]
        return carry

    groups = per // UNROLL
    used = (count_ref[0] + UNROLL - 1) // UNROLL

    def chunk(c, carry):
        tile_copy(c).wait()
        lax.fori_loop(c * groups, jnp.clip(used, c * groups, (c + 1) * groups), group, 0)
        return carry

    lax.fori_loop(0, chunks, chunk, 0)

    away = jnp.broadcast_to(seed_ref[...] - first_ref[0], (seeds, width)) - lax.broadcasted_iota(
        I32, (seeds, width), 1
    )

    def update(b, carry):
        gap, other = carry
        cols = pl.ds(pl.multiple_of(b * width, width), width)
        old = rank[:, cols]
        at_seed = away == b * width
        new = DAMP * (acc[b] + share) + jnp.where(at_seed, 1.0 - DAMP, 0.0)
        nxt[:, cols] = new
        gap = gap + jnp.abs(new - old)
        if last:
            return gap, other + jnp.where(at_seed, new, 0.0)
        dead = jnp.broadcast_to(dangling_ref[pl.ds(b, 1), :], (seeds, width)) != 0
        kept = jnp.where(dead, 0.0, new)
        source[b] = kept.astype(BF16)
        return gap, other + (new - kept)

    carry = (jnp.zeros((seeds, width), F32), jnp.zeros((seeds, width), F32))
    for c in range(parts):
        rank_copy(c).wait()
        carry = lax.fori_loop(c * span, (c + 1) * span, update, carry, unroll=8)
        rank_store(c).start()
    gap, other = carry
    gap_row = to_row(jnp.sum(gap, axis=1, keepdims=True))
    if last:
        own_row = to_row(jnp.sum(other, axis=1, keepdims=True))
        stats_ref[0:1, :] = gap_row
        stats_ref[1:2, :] = own_row
    else:
        stats_ref[0:1, :] = gap_row
        stats_ref[1:2, :] = jnp.zeros((1, 128), F32)
        head_ref[...] = source[0]
        tail_ref[...] = source[blocks - 1]
        pack(wanted_ref, source, mass_slab(other), message, message_hbm, send_sem)
    for c in range(parts):
        rank_store(c).wait()


def finish(last, vertices, first, count, slot, target, wanted, seeds_at, dangling, fetched, banded, rank, tiles):
    blocks, seeds, width = banded.shape
    out_shape = [shaped(rank.shape, F32), shaped((2, 128), F32)]
    out_specs = [anywhere(), vmem()]
    extra = []
    if not last:
        edge = shaped((seeds, width), BF16)
        out_shape += [shaped((blocks, seeds, width), BF16), edge, edge, shaped(fetched.shape, BF16)]
        out_specs += [vmem(), vmem(), vmem(), anywhere()]
        extra = [VMEM(fetched.shape, BF16), pltpu.SemaphoreType.DMA((4,))]
    return pl.pallas_call(
        functools.partial(finish_kernel, last, vertices),
        out_shape=tuple(out_shape),
        in_specs=[smem()] * 5 + [vmem()] * 2 + [anywhere()] * 4,
        out_specs=tuple(out_specs),
        scratch_shapes=extra
        + [
            VMEM(fetched.shape, BF16),
            VMEM(tiles.shape, BF16),
            VMEM((blocks + 1, seeds, width), F32),
            VMEM(rank.shape, F32),
            VMEM(rank.shape, F32),
            pltpu.SemaphoreType.DMA((2,)),
            pltpu.SemaphoreType.DMA((8,)),
            pltpu.SemaphoreType.DMA((8,)),
            pltpu.SemaphoreType.DMA((8,)),
        ],
        compiler_params=PARAMS,
        name="finish",
    )(first, count, slot, target, wanted, seeds_at, dangling, fetched, banded, rank, tiles)


def stats_kernel(seeds, vertices, group_ref, got_ref, change_ref, total_ref, own_ref):
    got = got_ref[...]
    odd = lax.broadcasted_iota(I32, got.shape, 0) % 2 == 1
    one = jnp.sum(jnp.where(odd, got, 0.0), axis=0, keepdims=True)
    zero = jnp.sum(jnp.where(odd, 0.0, got), axis=0, keepdims=True)
    mine = jnp.where(group_ref[0] == 1, one, zero)
    both = one + zero
    for i in range(ITERS):
        lanes = slice(i * seeds, (i + 1) * seeds)
        change_ref[i : i + 1, :] = mine[:, lanes] / vertices
        total_ref[:, i : i + 1] = jnp.sum(both[:, lanes] / vertices, axis=1, keepdims=True) / (2 * seeds)
    own_ref[...] = mine[:, ITERS * seeds :]


def on_device(rank_in, band_tiles, off_tiles, tile_src, tile_row, tile_count, seed_ids, dangling):
    blocks, _, width, _ = band_tiles.shape
    seeds = rank_in.shape[0]
    peers = lax.axis_size("dom")
    groups = lax.axis_size("seed")
    vertices = blocks * width * peers
    first = (lax.axis_index("dom") * (blocks * width)).astype(I32).reshape(1)
    group = lax.axis_index("seed").astype(I32).reshape(1)
    dangling = dangling.reshape(blocks, width)
    seeds_at = seed_ids.reshape(seeds, 1)

    request, slot, target = plan(tile_count, tile_src, tile_row, peers, blocks)
    wanted = lax.all_to_all(request, "dom", split_axis=0, concat_axis=0, tiled=True)
    source, slab, head, tail = prep(rank_in, dangling, blocks)
    message = pack_first(wanted, source, slab, peers)
    rank = rank_in
    rows = []
    for iteration in range(ITERS):
        last = iteration + 1 == ITERS
        fetched = lax.all_to_all(message, "dom", split_axis=0, concat_axis=0, tiled=True)
        left = lax.ppermute(tail, "dom", [(i, i + 1) for i in range(peers - 1)])
        right = lax.ppermute(head, "dom", [(i + 1, i) for i in range(peers - 1)])
        banded = band(source, left, right, band_tiles)
        done = finish(
            last, vertices, first, tile_count, slot, target, wanted, seeds_at, dangling, fetched, banded, rank, off_tiles
        )
        rank, stats = done[:2]
        rows.append(stats[0:1, :seeds])
        if not last:
            source, head, tail, message = done[2:]
    rows.append(stats[1:2, :seeds])
    line = jnp.concatenate(rows, axis=1)
    got = lax.all_to_all(
        jnp.broadcast_to(line, (peers * groups, line.shape[1])),
        ("dom", "seed"),
        split_axis=0,
        concat_axis=0,
        tiled=True,
    )
    change, total, own = pl.pallas_call(
        functools.partial(stats_kernel, seeds, vertices),
        out_shape=(shaped((ITERS, seeds), F32), shaped((1, ITERS), F32), shaped((1, seeds), F32)),
        in_specs=[smem(), vmem()],
        out_specs=(vmem(),) * 3,
        name="stats",
    )(group, got)
    return (rank, change, total.reshape(ITERS), own.reshape(seeds))


def solution(mesh):
    return jax.shard_map(
        on_device,
        mesh=mesh,
        in_specs=(
            P("seed", "dom"),
            P("dom", None, None, None),
            P("dom", None, None),
            P("dom", None),
            P("dom", None),
            P("dom"),
            P("seed"),
            P("dom"),
        ),
        out_specs=(P("seed", "dom"), P(None, "seed"), P(), P("seed")),
        check_vma=False,
    )
```

time: 1230 us -> 251 us (0.20)
  blocking collectives: 721 us -> 0 us
  other arithmetic: 292 us -> 0.08 us
  Pallas kernels: 0 us -> 105 us
  matrix products: 99.4 us -> 0 us
  local copies, waits for them, and re-layouts: 66.6 us -> 6.63 us
  waiting for transfers between devices: 1.77 us -> 49.5 us
  starting transfers between devices: 42 us -> 87.3 us
    psum x5 -> x0, blocking collectives: 721 us -> none  [the longest x3 463 us: on_device(): dead_mass = lax.psum(mass_term, 'dom')]
    scatter-add x3 -> x0, other arithmetic: 250 us -> none  [on_device(): jax.ops.segment_sum(products, tile_rows, num_segments=blocks + 1)[:blocks]]
    pallas_call x0 -> x10, Pallas kernels: none -> 105 us  [the longest x3 59.6 us: finish(): pl.pallas_call(functools.partial(finish_kernel, last, vertices), out_shap...]
    dot_general x6 -> x0, matrix products: 99.4 us -> none  [the longest x3 61.3 us: on_device(): jnp.einsum('stj,tij->tsi', operands, off_tiles, preferred_element_type=jn...]
    gather x7 -> x0, local copies, waits for them, and re-layouts: 50 us -> none  [the longest x3 40.4 us: on_device(): operands = jnp.take(fetched, tile_slot, axis=1)]
    all_to_all x4 -> x5, starting transfers between devices: 29.6 us -> 74.5 us  [the longest x3 42.3 us: on_device(): lax.all_to_all(message, 'dom', split_axis=0, concat_axis=0, tiled=True)]
    ppermute x6, waiting for transfers between devices: 0.02 us -> 26.8 us  [the longest x3 20.2 us: on_device(): right = lax.ppermute(head, 'dom', [(i + 1, i) for i in range(peers - 1)])]
    all_to_all x4 -> x5, waiting for transfers between devices: 1.76 us -> 22.6 us  [the longest x1 9.82 us: on_device(): lax.all_to_all(jnp.broadcast_to(line, (peers * groups, line.shape[1])), (...]
  transfers between devices with their start and end apart: 10 -> 11, of which waited for: 1 -> 8; matrix products, arithmetic and copies ran while one was open for 2% -> 0% of each run, Pallas kernels for 0% -> 16%
where the time goes in v1:
time: 251 us; the launch traced here: 250 us
  Pallas kernels  105 us (42%)
  starting transfers between devices  87.3 us (35%)
  waiting for transfers between devices  49.5 us (20%)
  local copies, waits for them, and re-layouts  6.63 us (3%)
    pallas_call x3, Pallas kernels, finish(): pl.pallas_call(functools.partial(finish_kernel, last, vertices), out_shap...  59.6 us
    all_to_all x3, starting transfers between devices, on_device(): lax.all_to_all(message, 'dom', split_axis=0, concat_axis=0, tiled=True)  42.3 us
    pallas_call x3, Pallas kernels, band(): pl.pallas_call(band_kernel, out_shape=shaped((blocks, seeds, width), F32)...  35.6 us
    ppermute x3, waiting for transfers between devices, on_device(): right = lax.ppermute(head, 'dom', [(i + 1, i) for i in range(peers - 1)])  20.2 us
    all_to_all x1, starting transfers between devices, on_device(): lax.all_to_all(jnp.broadcast_to(line, (peers * groups, line.shape[1])), (...  20.2 us
    all_to_all x1, starting transfers between devices, on_device(): lax.all_to_all(request, 'dom', split_axis=0, concat_axis=0, tiled=True)  12 us
    all_to_all x1, waiting for transfers between devices, on_device(): lax.all_to_all(jnp.broadcast_to(line, (peers * groups, line.shape[1])), (...  9.82 us
    all_to_all x3, waiting for transfers between devices, on_device(): lax.all_to_all(message, 'dom', split_axis=0, concat_axis=0, tiled=True)  8.95 us
  transfers between devices with their start and end apart: 11, of which 8 were waited for; matrix products, arithmetic and copies ran while one was open for 0% of the time, Pallas kernels for 16%

profile of v1, /device:TPU:1, one launch (start us, length us, event | category | flops | bytes accessed | tf_op | source)
XLA Modules:
  0.0 249.9 jit_solution(8281857856411306345)
XLA Ops:
  2.7 12.0 %all-to-all-start = ((s32[64,1,128]{2,1,0:T(1,128)}), s32[64,1,128]{2,1,0:T(1,128)S(1)}, u32[]{:S(2)}, u32[]{:S(2)}) async-start(s32[64,1,128]{2,1,0:T(1,128)} %bitcast.23), calls=%async_computation | async-start | bytes 65536 | tf_op jit(solution)/shard_map/all_to_all | solution.py:410
  15.5 3.6 %prep.1 = (bf16[128,64,128]{2,1,0:T(8,128)(2,1)}, bf16[8,128]{1,0:T(8,128)(2,1)S(1)}, bf16[64,128]{1,0:T(8,128)(2,1)S(1)}, bf16[64,128]{1,0:T(8,128)(2,1)S(1)}) custom-call(f32[64,16384]{1,0:T(8,128)} %refs_9_.1, s32[128,128]{1,0:T(8,128)S(1)} %bitcast.14), custom_call_target="tpu_custom_call" | custom-call | tf_op jit(solution)/shard_map/prep/pallas_call | solution.py:125
  19.2 3.9 %all-to-all-done = s32[64,1,128]{2,1,0:T(1,128)S(1)} async-done(((s32[64,1,128]{2,1,0:T(1,128)}), s32[64,1,128]{2,1,0:T(1,128)S(1)}, u32[]{:S(2)}, u32[]{:S(2)}) %all-to-all-start) | async-done | bytes 32800 | tf_op jit(solution)/shard_map/all_to_all | solution.py:410
  23.0 3.1 %pack.1 = bf16[64,136,128]{2,1,0:T(8,128)(2,1)} custom-call(s32[64,128]{1,0:T(8,128)S(1)} %bitcast.18, bf16[128,64,128]{2,1,0:T(8,128)(2,1)} %get-tuple-element.31.source_ref.source_hbm, bf16[8,128]{1,0:T(8,128)(2,1)S(1)} %get-tuple-element.32.slab_ref), custom_call_target="tpu_custom_call" | custom-call | tf_op jit(solution)/shard_map/pack/pallas_call | solution.py:167
  26.1 5.9 %all-to-all-start.1 = ((bf16[64,136,128]{2,1,0:T(8,128)(2,1)}), bf16[64,136,128]{2,1,0:T(8,128)(2,1)S(1)}, u32[]{:S(2)}, u32[]{:S(2)}) async-start(bf16[64,136,128]{2,1,0:T(8,128)(2,1)} %pack.1), calls=%async_computation.1 | async-start | bytes 4456448 | tf_op jit(solution)/shard_map/all_to_all | solution.py:417
  32.1 2.9 %collective-permute-start = (bf16[64,128]{1,0:T(8,128)(2,1)S(1)}, bf16[64,128]{1,0:T(8,128)(2,1)S(1)}, u32[]{:S(2)}, u32[]{:S(2)}) collective-permute-start(bf16[64,128]{1,0:T(8,128)(2,1)S(1)} %get-tuple-element.33), channel_id=1, source_target_pairs={{0,2},{2,4},{4,6},{6,8},{8,10},{10,12},{12,14},{14,16},{16,18},{18... | collective-permute-start | bytes 49160 | tf_op jit(solution)/shard_map/ppermute | solution.py:418
  36.4 6.6 %collective-permute-done.left_ref = bf16[64,128]{1,0:T(8,128)(2,1)S(1)} collective-permute-done((bf16[64,128]{1,0:T(8,128)(2,1)S(1)}, bf16[64,128]{1,0:T(8,128)(2,1)S(1)}, u32[]{:S(2)}, u32[]{:S(2)}) %collective-permute-start) | collective-permute-done | bytes 16416 | tf_op jit(solution)/shard_map/ppermute | solution.py:418
  43.0 11.9 %band.3.refs_8_ = f32[128,64,128]{2,1,0:T(8,128)} custom-call(bf16[128,64,128]{2,1,0:T(8,128)(2,1)} %get-tuple-element.31.source_ref.source_hbm, bf16[64,128]{1,0:T(8,128)(2,1)S(1)} %collective-permute-done.left_ref, bf16[64,128]{1,0:T(8,128)(2,1)S(1)} %collective-permute-done.1.right_ref, bf16[128,3,128,128]{3,2,1,0:T(8,128)(2,1)} %tiles_hbm.5), custom_call_target="tpu_custom_call" | custom-call | tf_op jit(solution)/shard_map/band/pallas_call | solution.py:211
  54.9 5.7 %all-to-all-done.1.refs_7_ = bf16[64,136,128]{2,1,0:T(8,128)(2,1)S(1)} async-done(((bf16[64,136,128]{2,1,0:T(8,128)(2,1)}), bf16[64,136,128]{2,1,0:T(8,128)(2,1)S(1)}, u32[]{:S(2)}, u32[]{:S(2)}) %all-to-all-start.1) | async-done | bytes 2228256 | tf_op jit(solution)/shard_map/all_to_all | solution.py:417
  62.0 20.7 %finish.3 = (f32[64,16384]{1,0:T(8,128)}, f32[2,128]{1,0:T(2,128)S(1)}, bf16[128,64,128]{2,1,0:T(8,128)(2,1)}, bf16[64,128]{1,0:T(8,128)(2,1)S(1)}, bf16[64,128]...) custom-call(s32[1]{0:T(128)} %bitcast.refs_0_, s32[1]{0:T(128)S(6)} %copy.22.count_ref.refs_1_, s32[1,512]{1,0:T(1,128)S(1)} %copy-done.2, ...), custom_call_target="tpu_custom_call" | custom-call | tf_op jit(solution)/shard_map/finish/pallas_call | solution.py:362
  82.7 18.5 %all-to-all-start.2 = ((bf16[64,136,128]{2,1,0:T(8,128)(2,1)}), bf16[64,136,128]{2,1,0:T(8,128)(2,1)S(1)}, u32[]{:S(2)}, u32[]{:S(2)}) async-start(bf16[64,136,128]{2,1,0:T(8,128)(2,1)} %get-tuple-element.35), calls=%async_computation.2 | async-start | bytes 4456448 | tf_op jit(solution)/shard_map/all_to_all | solution.py:417
  101.1 2.9 %collective-permute-start.2 = (bf16[64,128]{1,0:T(8,128)(2,1)S(1)}, bf16[64,128]{1,0:T(8,128)(2,1)S(1)}, u32[]{:S(2)}, u32[]{:S(2)}) collective-permute-start(bf16[64,128]{1,0:T(8,128)(2,1)S(1)} %get-tuple-element.37), channel_id=1, source_target_pairs={{0,2},{2,4},{4,6},{6,8},{8,10},{10,12},{12,14},{14,16},{16,18},{18... | collective-permute-start | bytes 49160 | tf_op jit(solution)/shard_map/ppermute | solution.py:418
  105.6 10.3 %collective-permute-done.3.right_ref = bf16[64,128]{1,0:T(8,128)(2,1)S(1)} collective-permute-done((bf16[64,128]{1,0:T(8,128)(2,1)S(1)}, bf16[64,128]{1,0:T(8,128)(2,1)S(1)}, u32[]{:S(2)}, u32[]{:S(2)}) %collective-permute-start.3) | collective-permute-done | bytes 16416 | tf_op jit(solution)/shard_map/ppermute | solution.py:419
  115.8 11.9 %band.4.refs_8_ = f32[128,64,128]{2,1,0:T(8,128)} custom-call(bf16[128,64,128]{2,1,0:T(8,128)(2,1)} %get-tuple-element.36.source_hbm, bf16[64,128]{1,0:T(8,128)(2,1)S(1)} %collective-permute-done.2.left_ref, bf16[64,128]{1,0:T(8,128)(2,1)S(1)} %collective-permute-done.3.right_ref, bf16[128,3,128,128]{3,2,1,0:T(8,128)(2,1)} %tiles_hbm.5), custom_call_target="tpu_custom_call" | custom-call | tf_op jit(solution)/shard_map/band/pallas_call | solution.py:211
  127.7 1.7 all-to-all-done.2.refs_7_
  130.9 20.7 %finish.4 = (f32[64,16384]{1,0:T(8,128)}, f32[2,128]{1,0:T(2,128)S(1)}, bf16[128,64,128]{2,1,0:T(8,128)(2,1)}, bf16[64,128]{1,0:T(8,128)(2,1)S(1)}, bf16[64,128]...) custom-call(s32[1]{0:T(128)} %bitcast.refs_0_, s32[1]{0:T(128)S(6)} %copy.22.count_ref.refs_1_, s32[1,512]{1,0:T(1,128)S(1)} %copy-done.2, ...), custom_call_target="tpu_custom_call" | custom-call | tf_op jit(solution)/shard_map/finish/pallas_call | solution.py:362
  151.5 17.9 %all-to-all-start.3 = ((bf16[64,136,128]{2,1,0:T(8,128)(2,1)}), bf16[64,136,128]{2,1,0:T(8,128)(2,1)S(1)}, u32[]{:S(2)}, u32[]{:S(2)}) async-start(bf16[64,136,128]{2,1,0:T(8,128)(2,1)} %get-tuple-element.40), calls=%async_computation.3 | async-start | bytes 4456448 | tf_op jit(solution)/shard_map/all_to_all | solution.py:417
  169.5 2.9 %collective-permute-start.4 = (bf16[64,128]{1,0:T(8,128)(2,1)S(1)}, bf16[64,128]{1,0:T(8,128)(2,1)S(1)}, u32[]{:S(2)}, u32[]{:S(2)}) collective-permute-start(bf16[64,128]{1,0:T(8,128)(2,1)S(1)} %get-tuple-element.42), channel_id=1, source_target_pairs={{0,2},{2,4},{4,6},{6,8},{8,10},{10,12},{12,14},{14,16},{16,18},{18... | collective-permute-start | bytes 49160 | tf_op jit(solution)/shard_map/ppermute | solution.py:418
  173.7 9.9 %collective-permute-done.5.right_ref = bf16[64,128]{1,0:T(8,128)(2,1)S(1)} collective-permute-done((bf16[64,128]{1,0:T(8,128)(2,1)S(1)}, bf16[64,128]{1,0:T(8,128)(2,1)S(1)}, u32[]{:S(2)}, u32[]{:S(2)}) %collective-permute-start.5) | collective-permute-done | bytes 16416 | tf_op jit(solution)/shard_map/ppermute | solution.py:419
  183.7 11.9 %band.5.refs_8_ = f32[128,64,128]{2,1,0:T(8,128)} custom-call(bf16[128,64,128]{2,1,0:T(8,128)(2,1)} %get-tuple-element.41.source_hbm, bf16[64,128]{1,0:T(8,128)(2,1)S(1)} %collective-permute-done.4.left_ref, bf16[64,128]{1,0:T(8,128)(2,1)S(1)} %collective-permute-done.5.right_ref, bf16[128,3,128,128]{3,2,1,0:T(8,128)(2,1)} %tiles_hbm.5), custom_call_target="tpu_custom_call" | custom-call | tf_op jit(solution)/shard_map/band/pallas_call | solution.py:211
  198.6 18.2 %finish.5 = (f32[64,16384]{1,0:T(8,128)}, f32[2,128]{1,0:T(2,128)S(1)}) custom-call(s32[1]{0:T(128)} %bitcast.refs_0_, s32[1]{0:T(128)S(6)} %copy.22.count_ref.refs_1_, s32[1,512]{1,0:T(1,128)S(1)} %copy-done.2, s32[1,512]{1,0:T(1,128)S(1)} %copy-done.3, s32[64,128]{1,0:T(8,128)S(1)} %bitcast.21, s32[64,1]{1,0:T(8,128)S(1)} %copy.18.refs_5_, ...), custom_call_target="tpu_custom_call" | custom-call | tf_op jit(solution)/shard_map/finish/pallas_call | solution.py:362
  217.6 20.2 %all-to-all-start.4 = ((f32[128,1,256]{2,1,0:T(1,128)}), f32[128,1,256]{2,1,0:T(1,128)S(1)}, u32[]{:S(2)}, u32[]{:S(2)}) async-start(f32[128,1,256]{2,1,0:T(1,128)} %broadcast_in_dim.2), calls=%async_computation.4 | async-start | bytes 262144 | tf_op jit(solution)/shard_map/all_to_all | solution.py:430
  237.8 9.8 %all-to-all-done.4 = f32[128,1,256]{2,1,0:T(1,128)S(1)} async-done(((f32[128,1,256]{2,1,0:T(1,128)}), f32[128,1,256]{2,1,0:T(1,128)S(1)}, u32[]{:S(2)}, u32[]{:S(2)}) %all-to-all-start.4) | async-done | bytes 131104 | tf_op jit(solution)/shard_map/all_to_all | solution.py:430
  248.3 1.6 stats.1
  (31 shorter events, 13.8 us)
Async XLA Ops:
  2.7 20.3 %all-to-all-start = ((s32[64,1,128]{2,1,0:T(1,128)}), s32[64,1,128]{2,1,0:T(1,128)S(1)}, u32[]{:S(2)}, u32[]{:S(2)}) async-start(s32[64,1,128]{2,1,0:T(1,128)} %bitcast.23), calls=%async_computation | async-start | bytes 65536 | tf_op jit(solution)/shard_map/all_to_all | solution.py:410
  14.7 0.8 copy-start
  23.0 13.3 %copy-start.7 = (s32[64]{0:T(128)S(1)}, s32[64]{0:T(128)}, u32[]{:S(2)}) copy-start(s32[64]{0:T(128)} %param.14) | copy-start | bytes 772
  26.1 34.4 %all-to-all-start.1 = ((bf16[64,136,128]{2,1,0:T(8,128)(2,1)}), bf16[64,136,128]{2,1,0:T(8,128)(2,1)S(1)}, u32[]{:S(2)}, u32[]{:S(2)}) async-start(bf16[64,136,128]{2,1,0:T(8,128)(2,1)} %pack.1), calls=%async_computation.1 | async-start | bytes 4456448 | tf_op jit(solution)/shard_map/all_to_all | solution.py:417
  32.1 11.0 %collective-permute-start = (bf16[64,128]{1,0:T(8,128)(2,1)S(1)}, bf16[64,128]{1,0:T(8,128)(2,1)S(1)}, u32[]{:S(2)}, u32[]{:S(2)}) collective-permute-start(bf16[64,128]{1,0:T(8,128)(2,1)S(1)} %get-tuple-element.33), channel_id=1, source_target_pairs={{0,2},{2,4},{4,6},{6,8},{8,10},{10,12},{12,14},{14,16},{16,18},{18... | collective-permute-start | bytes 49160 | tf_op jit(solution)/shard_map/ppermute | solution.py:418
  35.0 8.0 %collective-permute-start.1 = (bf16[64,128]{1,0:T(8,128)(2,1)S(1)}, bf16[64,128]{1,0:T(8,128)(2,1)S(1)}, u32[]{:S(2)}, u32[]{:S(2)}) collective-permute-start(bf16[64,128]{1,0:T(8,128)(2,1)S(1)} %get-tuple-element.34), channel_id=1, source_target_pairs={{2,0},{4,2},{6,4},{8,6},{10,8},{12,10},{14,12},{16,14},{18,16},{20... | collective-permute-start | bytes 49160 | tf_op jit(solution)/shard_map/ppermute | solution.py:419
  36.4 25.6 %copy-start.1 = (s32[16384]{0:T(1024)S(1)}, s32[16384]{0:T(1024)}, u32[]{:S(2)}) copy-start(s32[16384]{0:T(1024)} %param.15) | copy-start | bytes 196612
  36.4 25.6 %copy-start.2 = (s32[1,512]{1,0:T(1,128)S(1)}, s32[1,512]{1,0:T(1,128)}, u32[]{:S(2)}) copy-start(s32[1,512]{1,0:T(1,128)} %get-tuple-element.28.refs_2_) | copy-start | bytes 6148
  36.4 25.6 %copy-start.3 = (s32[1,512]{1,0:T(1,128)S(1)}, s32[1,512]{1,0:T(1,128)}, u32[]{:S(2)}) copy-start(s32[1,512]{1,0:T(1,128)} %get-tuple-element.29.refs_3_) | copy-start | bytes 6148
  60.6 1.4 copy-start.4
  82.7 46.7 %all-to-all-start.2 = ((bf16[64,136,128]{2,1,0:T(8,128)(2,1)}), bf16[64,136,128]{2,1,0:T(8,128)(2,1)S(1)}, u32[]{:S(2)}, u32[]{:S(2)}) async-start(bf16[64,136,128]{2,1,0:T(8,128)(2,1)} %get-tuple-element.35), calls=%async_computation.2 | async-start | bytes 4456448 | tf_op jit(solution)/shard_map/all_to_all | solution.py:417
  101.1 4.4 %collective-permute-start.2 = (bf16[64,128]{1,0:T(8,128)(2,1)S(1)}, bf16[64,128]{1,0:T(8,128)(2,1)S(1)}, u32[]{:S(2)}, u32[]{:S(2)}) collective-permute-start(bf16[64,128]{1,0:T(8,128)(2,1)S(1)} %get-tuple-element.37), channel_id=1, source_target_pairs={{0,2},{2,4},{4,6},{6,8},{8,10},{10,12},{12,14},{14,16},{16,18},{18... | collective-permute-start | bytes 49160 | tf_op jit(solution)/shard_map/ppermute | solution.py:418
  104.1 11.8 %collective-permute-start.3 = (bf16[64,128]{1,0:T(8,128)(2,1)S(1)}, bf16[64,128]{1,0:T(8,128)(2,1)S(1)}, u32[]{:S(2)}, u32[]{:S(2)}) collective-permute-start(bf16[64,128]{1,0:T(8,128)(2,1)S(1)} %get-tuple-element.38), channel_id=1, source_target_pairs={{2,0},{4,2},{6,4},{8,6},{10,8},{12,10},{14,12},{16,14},{18,16},{20... | collective-permute-start | bytes 49160 | tf_op jit(solution)/shard_map/ppermute | solution.py:419
  129.4 1.4 copy-start.6
  151.5 45.6 %all-to-all-start.3 = ((bf16[64,136,128]{2,1,0:T(8,128)(2,1)}), bf16[64,136,128]{2,1,0:T(8,128)(2,1)S(1)}, u32[]{:S(2)}, u32[]{:S(2)}) async-start(bf16[64,136,128]{2,1,0:T(8,128)(2,1)} %get-tuple-element.40), calls=%async_computation.3 | async-start | bytes 4456448 | tf_op jit(solution)/shard_map/all_to_all | solution.py:417
  169.5 4.2 %collective-permute-start.4 = (bf16[64,128]{1,0:T(8,128)(2,1)S(1)}, bf16[64,128]{1,0:T(8,128)(2,1)S(1)}, u32[]{:S(2)}, u32[]{:S(2)}) collective-permute-start(bf16[64,128]{1,0:T(8,128)(2,1)S(1)} %get-tuple-element.42), channel_id=1, source_target_pairs={{0,2},{2,4},{4,6},{6,8},{8,10},{10,12},{12,14},{14,16},{16,18},{18... | collective-permute-start | bytes 49160 | tf_op jit(solution)/shard_map/ppermute | solution.py:418
  172.4 11.3 %collective-permute-start.5 = (bf16[64,128]{1,0:T(8,128)(2,1)S(1)}, bf16[64,128]{1,0:T(8,128)(2,1)S(1)}, u32[]{:S(2)}, u32[]{:S(2)}) collective-permute-start(bf16[64,128]{1,0:T(8,128)(2,1)S(1)} %get-tuple-element.43), channel_id=1, source_target_pairs={{2,0},{4,2},{6,4},{8,6},{10,8},{12,10},{14,12},{16,14},{18,16},{20... | collective-permute-start | bytes 49160 | tf_op jit(solution)/shard_map/ppermute | solution.py:419
  197.1 1.4 copy-start.5
  217.6 30.0 %all-to-all-start.4 = ((f32[128,1,256]{2,1,0:T(1,128)}), f32[128,1,256]{2,1,0:T(1,128)S(1)}, u32[]{:S(2)}, u32[]{:S(2)}) async-start(f32[128,1,256]{2,1,0:T(1,128)} %broadcast_in_dim.2), calls=%async_computation.4 | async-start | bytes 262144 | tf_op jit(solution)/shard_map/all_to_all | solution.py:430

commit v2 on v1

--- a/solution.py
+++ b/solution.py
@@ -17,7 +17,9 @@
 VMEM = pltpu.VMEM
 NT = (((1,), (1,)), ((), ()))
 SLAB = 8
-PARAMS = pltpu.CompilerParams(vmem_limit_bytes=52 << 20)
+PARAMS = pltpu.CompilerParams(vmem_limit_bytes=44 << 20)
+MIDDLE = pltpu.CompilerParams(vmem_limit_bytes=24 << 20)
+SMALL = pltpu.CompilerParams(vmem_limit_bytes=16 << 20)
 
 
 def vmem():
@@ -28,8 +30,16 @@
     return pl.BlockSpec(memory_space=pltpu.SMEM)
 
 
-def anywhere():
-    return pl.BlockSpec(memory_space=pl.ANY)
+def hbm():
+    return pl.BlockSpec(memory_space=pltpu.HBM)
+
+
+def in_hbm(shape, dtype):
+    return pltpu.HBM(shape, dtype)
+
+
+def off_chip(x):
+    return pltpu.with_memory_space_constraint(x, pltpu.HBM)
 
 
 def shaped(shape, dtype):
@@ -125,16 +135,16 @@
     return pl.pallas_call(
         prep_kernel,
         out_shape=(shaped((blocks, seeds, width), BF16), shaped((SLAB, 128), BF16), edge, edge),
-        in_specs=[anywhere(), vmem()],
+        in_specs=[hbm(), vmem()],
         out_specs=(vmem(),) * 4,
         scratch_shapes=[VMEM(rank.shape, F32), pltpu.SemaphoreType.DMA((8,))],
-        compiler_params=PARAMS,
+        compiler_params=SMALL,
         name="prep",
-    )(rank, dangling)
+    )(off_chip(rank), dangling)
 
 
 def pack(wanted, source, slab, message, out_hbm, sem):
-    peers, _, _ = message.shape
+    peers = message.shape[0]
     seeds = source.shape[1]
     parts = sem.shape[0]
     per = peers // parts
@@ -143,15 +153,14 @@
         span = pl.ds(c * per, per)
         return pltpu.make_async_copy(message.at[span], out_hbm.at[span], sem.at[c])
 
+    def one(p, carry):
+        for k in range(CAP):
+            message[p, k * seeds : (k + 1) * seeds, :] = source[wanted[p, k]]
+        message[p, CAP * seeds :, :] = slab
+        return carry
+
     for c in range(parts):
-
-        def one(p, carry):
-            for k in range(CAP):
-                message[p, k * seeds : (k + 1) * seeds, :] = source[wanted[p, k]]
-            message[p, CAP * seeds :, :] = slab
-            return carry
-
-        lax.fori_loop(c * per, (c + 1) * per, one, 0, unroll=4)
+        lax.fori_loop(c * per, (c + 1) * per, one, 0, unroll=8)
         send(c).start()
     for c in range(parts):
         send(c).wait()
@@ -166,16 +175,16 @@
     shape = (peers, CAP * seeds + SLAB, width)
     return pl.pallas_call(
         pack_kernel,
-        out_shape=shaped(shape, BF16),
+        out_shape=in_hbm(shape, BF16),
         in_specs=[smem(), vmem(), vmem()],
-        out_specs=anywhere(),
+        out_specs=hbm(),
         scratch_shapes=[VMEM(shape, BF16), pltpu.SemaphoreType.DMA((4,))],
-        compiler_params=PARAMS,
+        compiler_params=SMALL,
         name="pack",
     )(wanted, source, slab)
 
 
-def band_kernel(source_hbm, left_ref, right_ref, tiles_hbm, out_hbm, source, tiles, banded, sem, source_sem, out_sem):
+def band_kernel(source_hbm, tiles_hbm, out_hbm, source, tiles, banded, sem, source_sem, out_sem):
     blocks, seeds, width = banded.shape
     chunks = sem.shape[0]
     per = blocks // chunks
@@ -188,17 +197,18 @@
         span = pl.ds(c * per, per)
         return pltpu.make_async_copy(banded.at[span], out_hbm.at[span], out_sem.at[c])
 
-    own = pltpu.make_async_copy(source_hbm, source.at[pl.ds(1, blocks)], source_sem)
+    own = pltpu.make_async_copy(source_hbm, source, source_sem)
     own.start()
     for c in range(chunks):
         fetch(c).start()
-    source[0] = left_ref[...]
-    source[blocks + 1] = right_ref[...]
+    zero = jnp.zeros((seeds, width), BF16)
     own.wait()
     for c in range(chunks):
         fetch(c).wait()
         for b in range(c * per, (c + 1) * per):
-            x = jnp.concatenate([source[b], source[b + 1], source[b + 2]], axis=1)
+            before = source[b - 1] if b > 0 else zero
+            after = source[b + 1] if b + 1 < blocks else zero
+            x = jnp.concatenate([before, source[b], after], axis=1)
             w = jnp.concatenate([tiles[b, 0], tiles[b, 1], tiles[b, 2]], axis=1)
             banded[b] = dot_nt(x, w)
         flush(c).start()
@@ -206,74 +216,78 @@
         flush(c).wait()
 
 
-def band(source, left, right, tiles):
-    blocks, seeds, width = source.shape
+def band(source, tiles):
     return pl.pallas_call(
         band_kernel,
-        out_shape=shaped((blocks, seeds, width), F32),
-        in_specs=[anywhere(), vmem(), vmem(), anywhere()],
-        out_specs=anywhere(),
+        out_shape=in_hbm(source.shape, F32),
+        in_specs=[hbm(), hbm()],
+        out_specs=hbm(),
         scratch_shapes=[
-            VMEM((blocks + 2, seeds, width), BF16),
+            VMEM(source.shape, BF16),
             VMEM(tiles.shape, BF16),
-            VMEM((blocks, seeds, width), F32),
+            VMEM(source.shape, F32),
             pltpu.SemaphoreType.DMA((8,)),
             pltpu.SemaphoreType.DMA,
             pltpu.SemaphoreType.DMA((8,)),
         ],
-        compiler_params=PARAMS,
+        compiler_params=MIDDLE,
         name="band",
-    )(source, left, right, tiles)
+    )(off_chip(source), off_chip(tiles))
 
 
 UNROLL = 32
+AHEAD = 6
 
 
 def finish_kernel(last, vertices, *refs):
-    (first_ref, count_ref, slot_ref, target_ref, wanted_ref, seed_ref, dangling_ref) = refs[:7]
-    fetched_hbm, banded_hbm, rank_hbm, tiles_hbm = refs[7:11]
+    (first_ref, count_ref, slot_ref, target_ref, wanted_ref) = refs[:5]
+    (seed_ref, dangling_ref, left_ref, right_ref, fetched) = refs[5:10]
+    banded_hbm, rank_hbm, tiles_hbm, band_hbm = refs[10:14]
     if last:
-        next_hbm, stats_ref = refs[11:13]
-        scratch = refs[13:]
+        next_hbm, stats_ref = refs[14:16]
+        scratch = refs[16:]
     else:
-        next_hbm, stats_ref, source, head_ref, tail_ref, message_hbm, message, send_sem = refs[11:19]
-        scratch = refs[19:]
-    fetched, tiles, acc, rank, nxt, sem, tile_sem, rank_sem, out_sem = scratch
-    blocks = acc.shape[0] - 1
-    seeds, width = acc.shape[1:]
-    peers = fetched.shape[0]
-    chunks = tile_sem.shape[0]
-    per = tiles.shape[0] // chunks
-    parts = rank_sem.shape[0]
+        next_hbm, stats_ref, source_hbm, head_ref, tail_ref, message_hbm = refs[14:20]
+        source, message, source_sem, send_sem = refs[20:24]
+        scratch = refs[24:]
+    tiles, acc, banded, rank, edges, edge_sem, tile_sem, load_sem, out_sem = scratch
+    blocks, seeds, width = banded.shape
+    parts = out_sem.shape[0]
     span = blocks // parts
 
-    def tile_copy(c):
-        at = pl.ds(c * per, per)
-        return pltpu.make_async_copy(tiles_hbm.at[at], tiles.at[at], tile_sem.at[c])
-
-    def rank_copy(c):
-        cols = pl.ds(c * span * width, span * width)
-        return pltpu.make_async_copy(rank_hbm.at[:, cols], rank.at[:, cols], rank_sem.at[c])
+    def edge_copy(k):
+        at = band_hbm.at[0, 0] if k == 0 else band_hbm.at[blocks - 1, 2]
+        return pltpu.make_async_copy(at, edges.at[k], edge_sem.at[k])
+
+    def tile_copy(g):
+        at = pl.ds(g * UNROLL, UNROLL)
+        return pltpu.make_async_copy(tiles_hbm.at[at], tiles.at[at], tile_sem.at[g])
 
     def rank_store(c):
         cols = pl.ds(c * span * width, span * width)
-        return pltpu.make_async_copy(nxt.at[:, cols], next_hbm.at[:, cols], out_sem.at[c])
-
-    got = pltpu.make_async_copy(fetched_hbm, fetched, sem.at[0])
-    base = pltpu.make_async_copy(banded_hbm, acc.at[pl.ds(0, blocks)], sem.at[1])
-    got.start()
-    base.start()
-    for c in range(chunks):
-        tile_copy(c).start()
-    for c in range(parts):
-        rank_copy(c).start()
-    got.wait()
-    slabs = fetched[:, CAP * seeds :, :].astype(F32)
-    mass_row = jnp.sum(jnp.sum(slabs, axis=0), axis=0, keepdims=True)
+        return pltpu.make_async_copy(rank.at[:, cols], next_hbm.at[:, cols], out_sem.at[c])
+
+    def source_store(c):
+        at = pl.ds(c * span, span)
+        return pltpu.make_async_copy(source.at[at], source_hbm.at[at], source_sem.at[c])
+
+    used = (count_ref[0] + UNROLL - 1) // UNROLL
+    for k in range(2):
+        edge_copy(k).start()
+    for g in range(AHEAD):
+
+        @pl.when(g < used)
+        def _():
+            tile_copy(g).start()
+
+    mass_row = jnp.sum(jnp.sum(fetched[:, CAP * seeds :, :].astype(F32), axis=0), axis=0, keepdims=True)
     share = jnp.broadcast_to(to_column(mass_row, seeds) / vertices, (seeds, width))
-    acc[blocks] = jnp.zeros((seeds, width), F32)
     zero = jnp.zeros((seeds, width), BF16)
-    base.wait()
+    acc[...] = jnp.zeros_like(acc)
+    for k in range(2):
+        edge_copy(k).wait()
+    acc[0] = dot_nt(left_ref[...], edges[0])
+    acc[blocks - 1] = acc[blocks - 1] + dot_nt(right_ref[...], edges[1])
 
     def operand(t):
         slot = slot_ref[0, t]
@@ -281,6 +295,12 @@
         return fetched[slot // CAP, pl.ds(at, seeds), :]
 
     def group(g, carry):
+        tile_copy(g).wait()
+
+        @pl.when(g + AHEAD < used)
+        def _():
+            tile_copy(g + AHEAD).start()
+
         first = g * UNROLL
         products = []
         for u in range(0, UNROLL, 2):
@@ -299,15 +319,17 @@
             acc[row] = acc[row] + products[u]
         return carry
 
-    groups = per // UNROLL
-    used = (count_ref[0] + UNROLL - 1) // UNROLL
-
-    def chunk(c, carry):
-        tile_copy(c).wait()
-        lax.fori_loop(c * groups, jnp.clip(used, c * groups, (c + 1) * groups), group, 0)
-        return carry
-
-    lax.fori_loop(0, chunks, chunk, 0)
+    early = jnp.minimum(used, 4)
+    lax.fori_loop(0, early, group, 0)
+    loads = (
+        pltpu.make_async_copy(banded_hbm, banded, load_sem.at[0]),
+        pltpu.make_async_copy(rank_hbm, rank, load_sem.at[1]),
+    )
+    for load in loads:
+        load.start()
+    lax.fori_loop(early, used, group, 0)
+    for load in loads:
+        load.wait()
 
     away = jnp.broadcast_to(seed_ref[...] - first_ref[0], (seeds, width)) - lax.broadcasted_iota(
         I32, (seeds, width), 1
@@ -318,8 +340,8 @@
         cols = pl.ds(pl.multiple_of(b * width, width), width)
         old = rank[:, cols]
         at_seed = away == b * width
-        new = DAMP * (acc[b] + share) + jnp.where(at_seed, 1.0 - DAMP, 0.0)
-        nxt[:, cols] = new
+        new = DAMP * (banded[b] + acc[b] + share) + jnp.where(at_seed, 1.0 - DAMP, 0.0)
+        rank[:, cols] = new
         gap = gap + jnp.abs(new - old)
         if last:
             return gap, other + jnp.where(at_seed, new, 0.0)
@@ -330,55 +352,62 @@
 
     carry = (jnp.zeros((seeds, width), F32), jnp.zeros((seeds, width), F32))
     for c in range(parts):
-        rank_copy(c).wait()
         carry = lax.fori_loop(c * span, (c + 1) * span, update, carry, unroll=8)
         rank_store(c).start()
+        if not last:
+            source_store(c).start()
     gap, other = carry
-    gap_row = to_row(jnp.sum(gap, axis=1, keepdims=True))
-    if last:
-        own_row = to_row(jnp.sum(other, axis=1, keepdims=True))
-        stats_ref[0:1, :] = gap_row
-        stats_ref[1:2, :] = own_row
-    else:
-        stats_ref[0:1, :] = gap_row
-        stats_ref[1:2, :] = jnp.zeros((1, 128), F32)
+    if not last:
+        pack(wanted_ref, source, mass_slab(other), message, message_hbm, send_sem)
         head_ref[...] = source[0]
         tail_ref[...] = source[blocks - 1]
-        pack(wanted_ref, source, mass_slab(other), message, message_hbm, send_sem)
+        stats_ref[1:2, :] = jnp.zeros((1, 128), F32)
+    else:
+        stats_ref[1:2, :] = to_row(jnp.sum(other, axis=1, keepdims=True))
+    stats_ref[0:1, :] = to_row(jnp.sum(gap, axis=1, keepdims=True))
     for c in range(parts):
         rank_store(c).wait()
-
-
-def finish(last, vertices, first, count, slot, target, wanted, seeds_at, dangling, fetched, banded, rank, tiles):
+        if not last:
+            source_store(c).wait()
+
+
+def finish(last, vertices, *operands):
+    fetched, banded, rank, tiles = operands[9:13]
+    operands = operands[:10] + tuple(off_chip(x) for x in operands[10:])
     blocks, seeds, width = banded.shape
-    out_shape = [shaped(rank.shape, F32), shaped((2, 128), F32)]
-    out_specs = [anywhere(), vmem()]
-    extra = []
+    out_shape = [in_hbm(rank.shape, F32), shaped((2, 128), F32)]
+    out_specs = [hbm(), vmem()]
+    scratch = []
     if not last:
         edge = shaped((seeds, width), BF16)
-        out_shape += [shaped((blocks, seeds, width), BF16), edge, edge, shaped(fetched.shape, BF16)]
-        out_specs += [vmem(), vmem(), vmem(), anywhere()]
-        extra = [VMEM(fetched.shape, BF16), pltpu.SemaphoreType.DMA((4,))]
+        out_shape += [in_hbm((blocks, seeds, width), BF16), edge, edge, in_hbm(fetched.shape, BF16)]
+        out_specs += [hbm(), vmem(), vmem(), hbm()]
+        scratch = [
+            VMEM((blocks, seeds, width), BF16),
+            VMEM(fetched.shape, BF16),
+            pltpu.SemaphoreType.DMA((8,)),
+            pltpu.SemaphoreType.DMA((4,)),
+        ]
     return pl.pallas_call(
         functools.partial(finish_kernel, last, vertices),
         out_shape=tuple(out_shape),
-        in_specs=[smem()] * 5 + [vmem()] * 2 + [anywhere()] * 4,
+        in_specs=[smem()] * 5 + [vmem()] * 5 + [hbm()] * 4,
         out_specs=tuple(out_specs),
-        scratch_shapes=extra
+        scratch_shapes=scratch
         + [
-            VMEM(fetched.shape, BF16),
             VMEM(tiles.shape, BF16),
             VMEM((blocks + 1, seeds, width), F32),
+            VMEM((blocks, seeds, width), F32),
             VMEM(rank.shape, F32),
-            VMEM(rank.shape, F32),
+            VMEM((2, width, width), BF16),
             pltpu.SemaphoreType.DMA((2,)),
-            pltpu.SemaphoreType.DMA((8,)),
-            pltpu.SemaphoreType.DMA((8,)),
+            pltpu.SemaphoreType.DMA((tiles.shape[0] // UNROLL,)),
+            pltpu.SemaphoreType.DMA((2,)),
             pltpu.SemaphoreType.DMA((8,)),
         ],
         compiler_params=PARAMS,
         name="finish",
-    )(first, count, slot, target, wanted, seeds_at, dangling, fetched, banded, rank, tiles)
+    )(*operands)
 
 
 def stats_kernel(seeds, vertices, group_ref, got_ref, change_ref, total_ref, own_ref):
@@ -417,9 +446,24 @@
         fetched = lax.all_to_all(message, "dom", split_axis=0, concat_axis=0, tiled=True)
         left = lax.ppermute(tail, "dom", [(i, i + 1) for i in range(peers - 1)])
         right = lax.ppermute(head, "dom", [(i + 1, i) for i in range(peers - 1)])
-        banded = band(source, left, right, band_tiles)
+        banded = band(source, band_tiles)
         done = finish(
-            last, vertices, first, tile_count, slot, target, wanted, seeds_at, dangling, fetched, banded, rank, off_tiles
+            last,
+            vertices,
+            first,
+            tile_count,
+            slot,
+            target,
+            wanted,
+            seeds_at,
+            dangling,
+            left,
+            right,
+            fetched,
+            banded,
+            rank,
+            off_tiles,
+            band_tiles,
         )
         rank, stats = done[:2]
         rows.append(stats[0:1, :seeds])

time: 251 us -> 196 us (0.78)
  starting transfers between devices: 87.3 us -> 58.8 us
  Pallas kernels: 105 us -> 83.5 us
  local copies, waits for them, and re-layouts: 6.63 us -> 2.37 us
    all_to_all x3, waiting for transfers between devices: 8.95 us -> 31.6 us  [on_device(): lax.all_to_all(message, 'dom', split_axis=0, concat_axis=0, tiled=True)]
    pallas_call x3, Pallas kernels: 59.6 us -> 38.6 us  [finish(): pl.pallas_call(functools.partial(finish_kernel, last, vertices), out_shap...]
    all_to_all x3, starting transfers between devices: 42.3 us -> 24.1 us  [on_device(): lax.all_to_all(message, 'dom', split_axis=0, concat_axis=0, tiled=True)]
    ppermute x3, waiting for transfers between devices: 20.2 us -> 3.16 us  [on_device(): right = lax.ppermute(head, 'dom', [(i + 1, i) for i in range(peers - 1)])]
    all_to_all x1, starting transfers between devices: 20.2 us -> 9.97 us  [on_device(): lax.all_to_all(jnp.broadcast_to(line, (peers * groups, line.shape[1])), (...]
    ppermute x3, waiting for transfers between devices: 6.61 us -> 0.01 us  [on_device(): left = lax.ppermute(tail, 'dom', [(i, i + 1) for i in range(peers - 1)])]
    unnamed x17 -> x13, local copies, waits for them, and re-layouts: 5.8 us -> 1.53 us
  transfers between devices with their start and end apart: 11 -> 11, of which waited for: 8 -> 6; matrix products, arithmetic and copies ran while one was open for 0% -> 0% of each run, Pallas kernels for 16% -> 20%
where the time goes in v2:
time: 196 us
  Pallas kernels  83.5 us (43%)
  starting transfers between devices  58.8 us (30%)
  waiting for transfers between devices  49.7 us (25%)
  local copies, waits for them, and re-layouts  2.37 us (1%)
    pallas_call x3, Pallas kernels, finish(): pl.pallas_call(functools.partial(finish_kernel, last, vertices), out_shap...  38.6 us
    pallas_call x3, Pallas kernels, band(): pl.pallas_call(band_kernel, out_shape=in_hbm(source.shape, F32), in_specs...  37 us
    all_to_all x3, waiting for transfers between devices, on_device(): lax.all_to_all(message, 'dom', split_axis=0, concat_axis=0, tiled=True)  31.6 us
    all_to_all x3, starting transfers between devices, on_device(): lax.all_to_all(message, 'dom', split_axis=0, concat_axis=0, tiled=True)  24.1 us
    all_to_all x1, starting transfers between devices, on_device(): lax.all_to_all(request, 'dom', split_axis=0, concat_axis=0, tiled=True)  12 us
    all_to_all x1, starting transfers between devices, on_device(): lax.all_to_all(jnp.broadcast_to(line, (peers * groups, line.shape[1])), (...  9.97 us
    all_to_all x1, waiting for transfers between devices, on_device(): lax.all_to_all(jnp.broadcast_to(line, (peers * groups, line.shape[1])), (...  9.82 us
    ppermute x3, starting transfers between devices, on_device(): left = lax.ppermute(tail, 'dom', [(i, i + 1) for i in range(peers - 1)])  8.75 us
  transfers between devices with their start and end apart: 11, of which 6 were waited for; matrix products, arithmetic and copies ran while one was open for 0% of the time, Pallas kernels for 20%

profile of v2, /device:TPU:1, one launch (start us, length us, event | category | flops | bytes accessed | tf_op | source)
XLA Modules:
  0.0 196.0 jit_solution(1463471395285149848)
XLA Ops:
  2.7 12.0 %all-to-all-start = ((s32[64,1,128]{2,1,0:T(1,128)}), s32[64,1,128]{2,1,0:T(1,128)S(1)}, u32[]{:S(2)}, u32[]{:S(2)}) async-start(s32[64,1,128]{2,1,0:T(1,128)} %bitcast.23), calls=%async_computation | async-start | bytes 65536 | tf_op jit(solution)/shard_map/all_to_all | solution.py:439
  15.5 2.4 %prep.1 = (bf16[128,64,128]{2,1,0:T(8,128)(2,1)S(1)}, bf16[8,128]{1,0:T(8,128)(2,1)S(1)}, bf16[64,128]{1,0:T(8,128)(2,1)S(1)}, bf16[64,128]{1,0:T(8,128)(2,1)S(1)}) custom-call(f32[64,16384]{1,0:T(8,128)} %refs_11_.1, s32[128,128]{1,0:T(8,128)S(1)} %bitcast.14), custom_call_target="tpu_custom_call" | custom-call | tf_op jit(solution)/shard_map/prep/pallas_call | solution.py:135
  17.9 5.1 %all-to-all-done = s32[64,1,128]{2,1,0:T(1,128)S(1)} async-done(((s32[64,1,128]{2,1,0:T(1,128)}), s32[64,1,128]{2,1,0:T(1,128)S(1)}, u32[]{:S(2)}, u32[]{:S(2)}) %all-to-all-start) | async-done | bytes 32800 | tf_op jit(solution)/shard_map/all_to_all | solution.py:439
  23.0 2.5 %pack.1 = bf16[64,136,128]{2,1,0:T(8,128)(2,1)} custom-call(s32[64,128]{1,0:T(8,128)S(1)} %bitcast.18, bf16[128,64,128]{2,1,0:T(8,128)(2,1)S(1)} %get-tuple-element.33.source_ref.source_hbm, bf16[8,128]{1,0:T(8,128)(2,1)S(1)} %get-tuple-element.34.slab_ref), custom_call_target="tpu_custom_call" | custom-call | tf_op jit(solution)/shard_map/pack/pallas_call | solution.py:176
  25.6 4.7 %all-to-all-start.1 = ((bf16[64,136,128]{2,1,0:T(8,128)(2,1)}), bf16[64,136,128]{2,1,0:T(8,128)(2,1)S(1)}, u32[]{:S(2)}, u32[]{:S(2)}) async-start(bf16[64,136,128]{2,1,0:T(8,128)(2,1)} %pack.1), calls=%async_computation.1 | async-start | bytes 4456448 | tf_op jit(solution)/shard_map/all_to_all | solution.py:446
  30.3 2.9 %collective-permute-start = (bf16[64,128]{1,0:T(8,128)(2,1)S(1)}, bf16[64,128]{1,0:T(8,128)(2,1)S(1)}, u32[]{:S(2)}, u32[]{:S(2)}) collective-permute-start(bf16[64,128]{1,0:T(8,128)(2,1)S(1)} %get-tuple-element.31), channel_id=1, source_target_pairs={{0,2},{2,4},{4,6},{6,8},{8,10},{10,12},{12,14},{14,16},{16,18},{18... | collective-permute-start | bytes 49160 | tf_op jit(solution)/shard_map/ppermute | solution.py:447
  34.7 12.3 %band.3.refs_10_ = f32[128,64,128]{2,1,0:T(8,128)} custom-call(bf16[128,64,128]{2,1,0:T(8,128)(2,1)} %copy-done, bf16[128,3,128,128]{3,2,1,0:T(8,128)(2,1)} %refs_13_.5), custom_call_target="tpu_custom_call" | custom-call | tf_op jit(solution)/shard_map/band/pallas_call | solution.py:220
  47.0 11.6 %all-to-all-done.1.refs_9_ = bf16[64,136,128]{2,1,0:T(8,128)(2,1)S(1)} async-done(((bf16[64,136,128]{2,1,0:T(8,128)(2,1)}), bf16[64,136,128]{2,1,0:T(8,128)(2,1)S(1)}, u32[]{:S(2)}, u32[]{:S(2)}) %all-to-all-start.1) | async-done | bytes 2228256 | tf_op jit(solution)/shard_map/all_to_all | solution.py:446
  58.6 13.3 %finish.3 = (f32[64,16384]{1,0:T(8,128)}, f32[2,128]{1,0:T(2,128)S(1)}, bf16[128,64,128]{2,1,0:T(8,128)(2,1)}, bf16[64,128]{1,0:T(8,128)(2,1)S(1)}, bf16[64,128]...) custom-call(s32[1]{0:T(128)} %bitcast.refs_0_, s32[1]{0:T(128)S(6)} %copy.22.count_ref.refs_1_, s32[1,512]{1,0:T(1,128)S(1)} %copy-done.3, ...), custom_call_target="tpu_custom_call" | custom-call | tf_op jit(solution)/shard_map/finish/pallas_call | solution.py:391
  71.9 9.5 %all-to-all-start.2 = ((bf16[64,136,128]{2,1,0:T(8,128)(2,1)}), bf16[64,136,128]{2,1,0:T(8,128)(2,1)S(1)}, u32[]{:S(2)}, u32[]{:S(2)}) async-start(bf16[64,136,128]{2,1,0:T(8,128)(2,1)} %get-tuple-element.37), calls=%async_computation.2 | async-start | bytes 4456448 | tf_op jit(solution)/shard_map/all_to_all | solution.py:446
  81.4 2.9 %collective-permute-start.2 = (bf16[64,128]{1,0:T(8,128)(2,1)S(1)}, bf16[64,128]{1,0:T(8,128)(2,1)S(1)}, u32[]{:S(2)}, u32[]{:S(2)}) collective-permute-start(bf16[64,128]{1,0:T(8,128)(2,1)S(1)} %get-tuple-element.35), channel_id=1, source_target_pairs={{0,2},{2,4},{4,6},{6,8},{8,10},{10,12},{12,14},{14,16},{16,18},{18... | collective-permute-start | bytes 49160 | tf_op jit(solution)/shard_map/ppermute | solution.py:447
  84.3 1.5 collective-permute-start.3
  85.8 12.3 %band.4.refs_10_ = f32[128,64,128]{2,1,0:T(8,128)} custom-call(bf16[128,64,128]{2,1,0:T(8,128)(2,1)} %get-tuple-element.38.source_hbm, bf16[128,3,128,128]{3,2,1,0:T(8,128)(2,1)} %refs_13_.5), custom_call_target="tpu_custom_call" | custom-call | tf_op jit(solution)/shard_map/band/pallas_call | solution.py:220
  98.2 11.4 %all-to-all-done.2.refs_9_ = bf16[64,136,128]{2,1,0:T(8,128)(2,1)S(1)} async-done(((bf16[64,136,128]{2,1,0:T(8,128)(2,1)}), bf16[64,136,128]{2,1,0:T(8,128)(2,1)S(1)}, u32[]{:S(2)}, u32[]{:S(2)}) %all-to-all-start.2) | async-done | bytes 2228256 | tf_op jit(solution)/shard_map/all_to_all | solution.py:446
  109.6 13.3 %finish.4 = (f32[64,16384]{1,0:T(8,128)}, f32[2,128]{1,0:T(2,128)S(1)}, bf16[128,64,128]{2,1,0:T(8,128)(2,1)}, bf16[64,128]{1,0:T(8,128)(2,1)S(1)}, bf16[64,128]...) custom-call(s32[1]{0:T(128)} %bitcast.refs_0_, s32[1]{0:T(128)S(6)} %copy.22.count_ref.refs_1_, s32[1,512]{1,0:T(1,128)S(1)} %copy-done.3, ...), custom_call_target="tpu_custom_call" | custom-call | tf_op jit(solution)/shard_map/finish/pallas_call | solution.py:391
  122.9 9.9 %all-to-all-start.3 = ((bf16[64,136,128]{2,1,0:T(8,128)(2,1)}), bf16[64,136,128]{2,1,0:T(8,128)(2,1)S(1)}, u32[]{:S(2)}, u32[]{:S(2)}) async-start(bf16[64,136,128]{2,1,0:T(8,128)(2,1)} %get-tuple-element.42), calls=%async_computation.3 | async-start | bytes 4456448 | tf_op jit(solution)/shard_map/all_to_all | solution.py:446
  132.8 2.9 %collective-permute-start.4 = (bf16[64,128]{1,0:T(8,128)(2,1)S(1)}, bf16[64,128]{1,0:T(8,128)(2,1)S(1)}, u32[]{:S(2)}, u32[]{:S(2)}) collective-permute-start(bf16[64,128]{1,0:T(8,128)(2,1)S(1)} %get-tuple-element.40), channel_id=1, source_target_pairs={{0,2},{2,4},{4,6},{6,8},{8,10},{10,12},{12,14},{14,16},{16,18},{18... | collective-permute-start | bytes 49160 | tf_op jit(solution)/shard_map/ppermute | solution.py:447
  137.0 12.3 %band.5.refs_10_ = f32[128,64,128]{2,1,0:T(8,128)} custom-call(bf16[128,64,128]{2,1,0:T(8,128)(2,1)} %get-tuple-element.43.source_hbm, bf16[128,3,128,128]{3,2,1,0:T(8,128)(2,1)} %refs_13_.5), custom_call_target="tpu_custom_call" | custom-call | tf_op jit(solution)/shard_map/band/pallas_call | solution.py:220
  149.3 3.2 %collective-permute-done.5.refs_8_ = bf16[64,128]{1,0:T(8,128)(2,1)S(1)} collective-permute-done((bf16[64,128]{1,0:T(8,128)(2,1)S(1)}, bf16[64,128]{1,0:T(8,128)(2,1)S(1)}, u32[]{:S(2)}, u32[]{:S(2)}) %collective-permute-start.5) | collective-permute-done | bytes 16416 | tf_op jit(solution)/shard_map/ppermute | solution.py:448
  152.5 8.6 %all-to-all-done.3.refs_9_ = bf16[64,136,128]{2,1,0:T(8,128)(2,1)S(1)} async-done(((bf16[64,136,128]{2,1,0:T(8,128)(2,1)}), bf16[64,136,128]{2,1,0:T(8,128)(2,1)S(1)}, u32[]{:S(2)}, u32[]{:S(2)}) %all-to-all-start.3) | async-done | bytes 2228256 | tf_op jit(solution)/shard_map/all_to_all | solution.py:446
  161.1 12.0 %finish.5 = (f32[64,16384]{1,0:T(8,128)}, f32[2,128]{1,0:T(2,128)S(1)}) custom-call(s32[1]{0:T(128)} %bitcast.refs_0_, s32[1]{0:T(128)S(6)} %copy.22.count_ref.refs_1_, s32[1,512]{1,0:T(1,128)S(1)} %copy-done.3, s32[1,512]{1,0:T(1,128)S(1)} %copy-done.4, s32[64,128]{1,0:T(8,128)S(1)} %bitcast.21, s32[64,1]{1,0:T(8,128)S(1)} %copy.18.refs_5_, ...), custom_call_target="tpu_custom_call" | custom-call | tf_op jit(solution)/shard_map/finish/pallas_call | solution.py:391
  173.9 10.0 %all-to-all-start.4 = ((f32[128,1,256]{2,1,0:T(1,128)}), f32[128,1,256]{2,1,0:T(1,128)S(1)}, u32[]{:S(2)}, u32[]{:S(2)}) async-start(f32[128,1,256]{2,1,0:T(1,128)} %broadcast_in_dim.2), calls=%async_computation.4 | async-start | bytes 262144 | tf_op jit(solution)/shard_map/all_to_all | solution.py:474
  183.9 9.8 %all-to-all-done.4 = f32[128,1,256]{2,1,0:T(1,128)S(1)} async-done(((f32[128,1,256]{2,1,0:T(1,128)}), f32[128,1,256]{2,1,0:T(1,128)S(1)}, u32[]{:S(2)}, u32[]{:S(2)}) %all-to-all-start.4) | async-done | bytes 131104 | tf_op jit(solution)/shard_map/all_to_all | solution.py:474
  194.4 1.6 stats.1
  (27 shorter events, 6.5 us)
Async XLA Ops:
  2.7 20.3 %all-to-all-start = ((s32[64,1,128]{2,1,0:T(1,128)}), s32[64,1,128]{2,1,0:T(1,128)S(1)}, u32[]{:S(2)}, u32[]{:S(2)}) async-start(s32[64,1,128]{2,1,0:T(1,128)} %bitcast.23), calls=%async_computation | async-start | bytes 65536 | tf_op jit(solution)/shard_map/all_to_all | solution.py:439
  14.7 0.8 copy-start.1
  17.9 7.6 %copy-start = (bf16[128,64,128]{2,1,0:T(8,128)(2,1)}, bf16[128,64,128]{2,1,0:T(8,128)(2,1)S(1)}, u32[]{:S(2)}) copy-start(bf16[128,64,128]{2,1,0:T(8,128)(2,1)S(1)} %get-tuple-element.33.source_ref.source_hbm) | copy-start | bytes 6291460
  23.0 11.5 %copy-start.5 = (s32[64]{0:T(128)S(1)}, s32[64]{0:T(128)}, u32[]{:S(2)}) copy-start(s32[64]{0:T(128)} %param.14) | copy-start | bytes 772
  25.6 33.1 %all-to-all-start.1 = ((bf16[64,136,128]{2,1,0:T(8,128)(2,1)}), bf16[64,136,128]{2,1,0:T(8,128)(2,1)S(1)}, u32[]{:S(2)}, u32[]{:S(2)}) async-start(bf16[64,136,128]{2,1,0:T(8,128)(2,1)} %pack.1), calls=%async_computation.1 | async-start | bytes 4456448 | tf_op jit(solution)/shard_map/all_to_all | solution.py:446
  30.3 16.7 %collective-permute-start = (bf16[64,128]{1,0:T(8,128)(2,1)S(1)}, bf16[64,128]{1,0:T(8,128)(2,1)S(1)}, u32[]{:S(2)}, u32[]{:S(2)}) collective-permute-start(bf16[64,128]{1,0:T(8,128)(2,1)S(1)} %get-tuple-element.31), channel_id=1, source_target_pairs={{0,2},{2,4},{4,6},{6,8},{8,10},{10,12},{12,14},{14,16},{16,18},{18... | collective-permute-start | bytes 49160 | tf_op jit(solution)/shard_map/ppermute | solution.py:447
  33.2 13.8 %collective-permute-start.1 = (bf16[64,128]{1,0:T(8,128)(2,1)S(1)}, bf16[64,128]{1,0:T(8,128)(2,1)S(1)}, u32[]{:S(2)}, u32[]{:S(2)}) collective-permute-start(bf16[64,128]{1,0:T(8,128)(2,1)S(1)} %get-tuple-element.32), channel_id=1, source_target_pairs={{2,0},{4,2},{6,4},{8,6},{10,8},{12,10},{14,12},{16,14},{18,16},{20... | collective-permute-start | bytes 49160 | tf_op jit(solution)/shard_map/ppermute | solution.py:448
  34.6 24.0 %copy-start.2 = (s32[16384]{0:T(1024)S(1)}, s32[16384]{0:T(1024)}, u32[]{:S(2)}) copy-start(s32[16384]{0:T(1024)} %param.15) | copy-start | bytes 196612
  34.6 24.0 %copy-start.3 = (s32[1,512]{1,0:T(1,128)S(1)}, s32[1,512]{1,0:T(1,128)}, u32[]{:S(2)}) copy-start(s32[1,512]{1,0:T(1,128)} %get-tuple-element.28.refs_2_) | copy-start | bytes 6148
  34.7 24.0 %copy-start.4 = (s32[1,512]{1,0:T(1,128)S(1)}, s32[1,512]{1,0:T(1,128)}, u32[]{:S(2)}) copy-start(s32[1,512]{1,0:T(1,128)} %get-tuple-element.29.refs_3_) | copy-start | bytes 6148
  71.9 37.6 %all-to-all-start.2 = ((bf16[64,136,128]{2,1,0:T(8,128)(2,1)}), bf16[64,136,128]{2,1,0:T(8,128)(2,1)S(1)}, u32[]{:S(2)}, u32[]{:S(2)}) async-start(bf16[64,136,128]{2,1,0:T(8,128)(2,1)} %get-tuple-element.37), calls=%async_computation.2 | async-start | bytes 4456448 | tf_op jit(solution)/shard_map/all_to_all | solution.py:446
  81.4 16.7 %collective-permute-start.2 = (bf16[64,128]{1,0:T(8,128)(2,1)S(1)}, bf16[64,128]{1,0:T(8,128)(2,1)S(1)}, u32[]{:S(2)}, u32[]{:S(2)}) collective-permute-start(bf16[64,128]{1,0:T(8,128)(2,1)S(1)} %get-tuple-element.35), channel_id=1, source_target_pairs={{0,2},{2,4},{4,6},{6,8},{8,10},{10,12},{12,14},{14,16},{16,18},{18... | collective-permute-start | bytes 49160 | tf_op jit(solution)/shard_map/ppermute | solution.py:447
  84.3 13.8 %collective-permute-start.3 = (bf16[64,128]{1,0:T(8,128)(2,1)S(1)}, bf16[64,128]{1,0:T(8,128)(2,1)S(1)}, u32[]{:S(2)}, u32[]{:S(2)}) collective-permute-start(bf16[64,128]{1,0:T(8,128)(2,1)S(1)} %get-tuple-element.36), channel_id=1, source_target_pairs={{2,0},{4,2},{6,4},{8,6},{10,8},{12,10},{14,12},{16,14},{18,16},{20... | collective-permute-start | bytes 49160 | tf_op jit(solution)/shard_map/ppermute | solution.py:448
  122.9 38.2 %all-to-all-start.3 = ((bf16[64,136,128]{2,1,0:T(8,128)(2,1)}), bf16[64,136,128]{2,1,0:T(8,128)(2,1)S(1)}, u32[]{:S(2)}, u32[]{:S(2)}) async-start(bf16[64,136,128]{2,1,0:T(8,128)(2,1)} %get-tuple-element.42), calls=%async_computation.3 | async-start | bytes 4456448 | tf_op jit(solution)/shard_map/all_to_all | solution.py:446
  132.8 16.6 %collective-permute-start.4 = (bf16[64,128]{1,0:T(8,128)(2,1)S(1)}, bf16[64,128]{1,0:T(8,128)(2,1)S(1)}, u32[]{:S(2)}, u32[]{:S(2)}) collective-permute-start(bf16[64,128]{1,0:T(8,128)(2,1)S(1)} %get-tuple-element.40), channel_id=1, source_target_pairs={{0,2},{2,4},{4,6},{6,8},{8,10},{10,12},{12,14},{14,16},{16,18},{18... | collective-permute-start | bytes 49160 | tf_op jit(solution)/shard_map/ppermute | solution.py:447
  135.7 16.8 %collective-permute-start.5 = (bf16[64,128]{1,0:T(8,128)(2,1)S(1)}, bf16[64,128]{1,0:T(8,128)(2,1)S(1)}, u32[]{:S(2)}, u32[]{:S(2)}) collective-permute-start(bf16[64,128]{1,0:T(8,128)(2,1)S(1)} %get-tuple-element.41), channel_id=1, source_target_pairs={{2,0},{4,2},{6,4},{8,6},{10,8},{12,10},{14,12},{16,14},{18,16},{20... | collective-permute-start | bytes 49160 | tf_op jit(solution)/shard_map/ppermute | solution.py:448
  173.9 19.8 %all-to-all-start.4 = ((f32[128,1,256]{2,1,0:T(1,128)}), f32[128,1,256]{2,1,0:T(1,128)S(1)}, u32[]{:S(2)}, u32[]{:S(2)}) async-start(f32[128,1,256]{2,1,0:T(1,128)} %broadcast_in_dim.2), calls=%async_computation.4 | async-start | bytes 262144 | tf_op jit(solution)/shard_map/all_to_all | solution.py:474

commit v3 on v2

--- a/solution.py
+++ b/solution.py
@@ -18,7 +18,7 @@
 NT = (((1,), (1,)), ((), ()))
 SLAB = 8
 PARAMS = pltpu.CompilerParams(vmem_limit_bytes=44 << 20)
-MIDDLE = pltpu.CompilerParams(vmem_limit_bytes=24 << 20)
+MIDDLE = pltpu.CompilerParams(vmem_limit_bytes=34 << 20)
 SMALL = pltpu.CompilerParams(vmem_limit_bytes=16 << 20)
 
 
@@ -80,12 +80,13 @@
     )(tile_count, tile_src, tile_row)
 
 
-def eye(rows):
-    return lax.broadcasted_iota(I32, (rows, 128), 0) == lax.broadcasted_iota(I32, (rows, 128), 1)
-
-
-def to_row(column):
-    return jnp.sum(jnp.where(eye(column.shape[0]), column, 0.0), axis=0, keepdims=True)
+def eye(rows, start=0):
+    lane = lax.broadcasted_iota(I32, (rows, 128), 1)
+    return lax.broadcasted_iota(I32, (rows, 128), 0) + start == lane
+
+
+def to_row(column, start=0):
+    return jnp.sum(jnp.where(eye(column.shape[0], start), column, 0.0), axis=0, keepdims=True)
 
 
 def to_column(row, seeds):
@@ -184,7 +185,13 @@
     )(wanted, source, slab)
 
 
-def band_kernel(source_hbm, tiles_hbm, out_hbm, source, tiles, banded, sem, source_sem, out_sem):
+def band_kernel(gap_at, rank_hbm, *refs):
+    refs = list(refs)
+    old_hbm = None if gap_at is None else refs.pop(0)
+    tiles_hbm, dangling_ref, out_hbm = refs[:3]
+    refs = refs[3:]
+    gap_ref = None if gap_at is None else refs.pop(0)
+    rank, source, tiles, banded, sem, rank_sem, out_sem = refs[:7]
     blocks, seeds, width = banded.shape
     chunks = sem.shape[0]
     per = blocks // chunks
@@ -197,13 +204,40 @@
         span = pl.ds(c * per, per)
         return pltpu.make_async_copy(banded.at[span], out_hbm.at[span], out_sem.at[c])
 
-    own = pltpu.make_async_copy(source_hbm, source, source_sem)
-    own.start()
+    def fetch_rank(c):
+        cols = pl.ds(c * per * width, per * width)
+        return pltpu.make_async_copy(rank_hbm.at[:, cols], rank.at[:, cols], rank_sem.at[c])
+
+    def fetch_old(c):
+        cols = pl.ds(c * per * width, per * width)
+        return pltpu.make_async_copy(old_hbm.at[:, cols], refs[7].at[:, cols], refs[8].at[c])
+
     for c in range(chunks):
+        fetch_rank(c).start()
+        if gap_at is not None:
+            fetch_old(c).start()
         fetch(c).start()
+
+    gap = jnp.zeros((seeds, width), F32)
+
+    def prepare(c, gap):
+        fetch_rank(c).wait()
+        if gap_at is not None:
+            fetch_old(c).wait()
+        for b in range(c * per, (c + 1) * per):
+            cols = slice(b * width, (b + 1) * width)
+            new = rank[:, cols]
+            dead = jnp.broadcast_to(dangling_ref[b : b + 1, :], (seeds, width)) != 0
+            source[b] = jnp.where(dead, 0.0, new).astype(BF16)
+            if gap_at is not None:
+                gap = gap + jnp.abs(new - refs[7][:, cols])
+        return gap
+
+    gap = prepare(0, gap)
     zero = jnp.zeros((seeds, width), BF16)
-    own.wait()
     for c in range(chunks):
+        if c + 1 < chunks:
+            gap = prepare(c + 1, gap)
         fetch(c).wait()
         for b in range(c * per, (c + 1) * per):
             before = source[b - 1] if b > 0 else zero
@@ -212,45 +246,61 @@
             w = jnp.concatenate([tiles[b, 0], tiles[b, 1], tiles[b, 2]], axis=1)
             banded[b] = dot_nt(x, w)
         flush(c).start()
+    if gap_at is not None:
+        gap_ref[...] = to_row(jnp.sum(gap, axis=1, keepdims=True), gap_at)
     for c in range(chunks):
         flush(c).wait()
 
 
-def band(source, tiles):
+def band(gap_at, rank, old, tiles, dangling):
+    blocks, _, width, _ = tiles.shape
+    seeds = rank.shape[0]
+    shape = (blocks, seeds, width)
+    ranks = [rank] if gap_at is None else [rank, old]
+    out_shape = [in_hbm(shape, F32)]
+    out_specs = [hbm()]
+    extra = []
+    if gap_at is not None:
+        out_shape.append(shaped((1, 128), F32))
+        out_specs.append(vmem())
+        extra = [VMEM(rank.shape, F32), pltpu.SemaphoreType.DMA((8,))]
     return pl.pallas_call(
-        band_kernel,
-        out_shape=in_hbm(source.shape, F32),
-        in_specs=[hbm(), hbm()],
-        out_specs=hbm(),
+        functools.partial(band_kernel, gap_at),
+        out_shape=tuple(out_shape),
+        in_specs=[hbm()] * (len(ranks) + 1) + [vmem()],
+        out_specs=tuple(out_specs),
         scratch_shapes=[
-            VMEM(source.shape, BF16),
+            VMEM(rank.shape, F32),
+            VMEM(shape, BF16),
             VMEM(tiles.shape, BF16),
-            VMEM(source.shape, F32),
+            VMEM(shape, F32),
             pltpu.SemaphoreType.DMA((8,)),
-            pltpu.SemaphoreType.DMA,
             pltpu.SemaphoreType.DMA((8,)),
-        ],
+            pltpu.SemaphoreType.DMA((8,)),
+        ]
+        + extra,
         compiler_params=MIDDLE,
         name="band",
-    )(off_chip(source), off_chip(tiles))
-
-
-UNROLL = 32
+    )(*(off_chip(x) for x in ranks), off_chip(tiles), dangling)
+
+
+UNROLL = 64
+PIECE = 32
 AHEAD = 6
+DEPTH = 8
 
 
 def finish_kernel(last, vertices, *refs):
     (first_ref, count_ref, slot_ref, target_ref, wanted_ref) = refs[:5]
     (seed_ref, dangling_ref, left_ref, right_ref, fetched) = refs[5:10]
-    banded_hbm, rank_hbm, tiles_hbm, band_hbm = refs[10:14]
+    banded_hbm, tiles_hbm, band_hbm = refs[10:13]
     if last:
-        next_hbm, stats_ref = refs[14:16]
-        scratch = refs[16:]
+        rank_hbm, gap_one_ref, gap_two_ref, next_hbm, line_ref, rank_sem = refs[13:19]
+        scratch = refs[19:]
     else:
-        next_hbm, stats_ref, source_hbm, head_ref, tail_ref, message_hbm = refs[14:20]
-        source, message, source_sem, send_sem = refs[20:24]
-        scratch = refs[24:]
-    tiles, acc, banded, rank, edges, edge_sem, tile_sem, load_sem, out_sem = scratch
+        next_hbm, head_ref, tail_ref, message_hbm, source, message, send_sem = refs[13:20]
+        scratch = refs[20:]
+    tiles, acc, banded, rank, edges, edge_sem, tile_sem, base_sem, out_sem = scratch
     blocks, seeds, width = banded.shape
     parts = out_sem.shape[0]
     span = blocks // parts
@@ -260,23 +310,18 @@
         return pltpu.make_async_copy(at, edges.at[k], edge_sem.at[k])
 
     def tile_copy(g):
-        at = pl.ds(g * UNROLL, UNROLL)
+        at = pl.ds(g * PIECE, PIECE)
         return pltpu.make_async_copy(tiles_hbm.at[at], tiles.at[at], tile_sem.at[g])
 
     def rank_store(c):
         cols = pl.ds(c * span * width, span * width)
         return pltpu.make_async_copy(rank.at[:, cols], next_hbm.at[:, cols], out_sem.at[c])
 
-    def source_store(c):
-        at = pl.ds(c * span, span)
-        return pltpu.make_async_copy(source.at[at], source_hbm.at[at], source_sem.at[c])
-
-    used = (count_ref[0] + UNROLL - 1) // UNROLL
-    for k in range(2):
-        edge_copy(k).start()
+    trips = (count_ref[0] + UNROLL - 1) // UNROLL
+    pieces = trips * (UNROLL // PIECE)
     for g in range(AHEAD):
 
-        @pl.when(g < used)
+        @pl.when(g < pieces)
         def _():
             tile_copy(g).start()
 
@@ -284,10 +329,6 @@
     share = jnp.broadcast_to(to_column(mass_row, seeds) / vertices, (seeds, width))
     zero = jnp.zeros((seeds, width), BF16)
     acc[...] = jnp.zeros_like(acc)
-    for k in range(2):
-        edge_copy(k).wait()
-    acc[0] = dot_nt(left_ref[...], edges[0])
-    acc[blocks - 1] = acc[blocks - 1] + dot_nt(right_ref[...], edges[1])
 
     def operand(t):
         slot = slot_ref[0, t]
@@ -295,14 +336,24 @@
         return fetched[slot // CAP, pl.ds(at, seeds), :]
 
     def group(g, carry):
-        tile_copy(g).wait()
-
-        @pl.when(g + AHEAD < used)
-        def _():
-            tile_copy(g + AHEAD).start()
+        for k in range(UNROLL // PIECE):
+            piece = g * (UNROLL // PIECE) + k
+            tile_copy(piece).wait()
+
+            @pl.when(piece + AHEAD < pieces)
+            def _():
+                tile_copy(piece + AHEAD).start()
 
         first = g * UNROLL
-        products = []
+        waiting = []
+
+        def add(most):
+            while len(waiting) > most:
+                t, y = waiting.pop(0)
+                for k in range(2):
+                    row = target_ref[0, t + k]
+                    acc[row] = acc[row] + y[k * seeds : (k + 1) * seeds]
+
         for u in range(0, UNROLL, 2):
             one, two = first + u, first + u + 1
             x = jnp.concatenate(
@@ -312,22 +363,25 @@
                 ],
                 axis=0,
             )
-            y = dot_nt(x, jnp.concatenate([tiles[one], tiles[two]], axis=1))
-            products += [y[:seeds], y[seeds:]]
-        for u in range(UNROLL):
-            row = target_ref[0, first + u]
-            acc[row] = acc[row] + products[u]
+            waiting.append((one, dot_nt(x, jnp.concatenate([tiles[one], tiles[two]], axis=1))))
+            add(DEPTH)
+        add(0)
         return carry
 
-    early = jnp.minimum(used, 4)
+    early = jnp.minimum(trips, 2)
     lax.fori_loop(0, early, group, 0)
-    loads = (
-        pltpu.make_async_copy(banded_hbm, banded, load_sem.at[0]),
-        pltpu.make_async_copy(rank_hbm, rank, load_sem.at[1]),
-    )
+    loads = [pltpu.make_async_copy(banded_hbm, banded, base_sem)]
+    if last:
+        loads.append(pltpu.make_async_copy(rank_hbm, rank, rank_sem))
     for load in loads:
         load.start()
-    lax.fori_loop(early, used, group, 0)
+    for k in range(2):
+        edge_copy(k).start()
+    lax.fori_loop(early, trips, group, 0)
+    for k in range(2):
+        edge_copy(k).wait()
+    acc[0] = acc[0] + dot_nt(left_ref[...], edges[0])
+    acc[blocks - 1] = acc[blocks - 1] + dot_nt(right_ref[...], edges[1])
     for load in loads:
         load.wait()
 
@@ -336,73 +390,76 @@
     )
 
     def update(b, carry):
-        gap, other = carry
         cols = pl.ds(pl.multiple_of(b * width, width), width)
-        old = rank[:, cols]
         at_seed = away == b * width
         new = DAMP * (banded[b] + acc[b] + share) + jnp.where(at_seed, 1.0 - DAMP, 0.0)
+        if last:
+            gap, own = carry
+            gap = gap + jnp.abs(new - rank[:, cols])
+            rank[:, cols] = new
+            return gap, own + jnp.where(at_seed, new, 0.0)
         rank[:, cols] = new
-        gap = gap + jnp.abs(new - old)
-        if last:
-            return gap, other + jnp.where(at_seed, new, 0.0)
         dead = jnp.broadcast_to(dangling_ref[pl.ds(b, 1), :], (seeds, width)) != 0
         kept = jnp.where(dead, 0.0, new)
         source[b] = kept.astype(BF16)
-        return gap, other + (new - kept)
-
-    carry = (jnp.zeros((seeds, width), F32), jnp.zeros((seeds, width), F32))
+        return carry + (new - kept)
+
+    nothing = jnp.zeros((seeds, width), F32)
+    carry = (nothing, nothing) if last else nothing
     for c in range(parts):
         carry = lax.fori_loop(c * span, (c + 1) * span, update, carry, unroll=8)
         rank_store(c).start()
-        if not last:
-            source_store(c).start()
-    gap, other = carry
-    if not last:
-        pack(wanted_ref, source, mass_slab(other), message, message_hbm, send_sem)
+    if last:
+        gap, own = (jnp.sum(x, axis=1, keepdims=True) for x in carry)
+        line = jnp.concatenate(
+            [gap_one_ref[...] + gap_two_ref[...], to_row(gap) + to_row(own, seeds)], axis=1
+        )
+        line_ref[...] = jnp.broadcast_to(line[:, None, :], line_ref.shape)
+    else:
+        pack(wanted_ref, source, mass_slab(carry), message, message_hbm, send_sem)
         head_ref[...] = source[0]
         tail_ref[...] = source[blocks - 1]
-        stats_ref[1:2, :] = jnp.zeros((1, 128), F32)
-    else:
-        stats_ref[1:2, :] = to_row(jnp.sum(other, axis=1, keepdims=True))
-    stats_ref[0:1, :] = to_row(jnp.sum(gap, axis=1, keepdims=True))
     for c in range(parts):
         rank_store(c).wait()
-        if not last:
-            source_store(c).wait()
-
-
-def finish(last, vertices, *operands):
-    fetched, banded, rank, tiles = operands[9:13]
-    operands = operands[:10] + tuple(off_chip(x) for x in operands[10:])
+
+
+def finish(last, vertices, devices, scalars, vectors, arrays, old=(), gaps=()):
+    fetched = vectors[-1]
+    banded, tiles, _ = arrays
     blocks, seeds, width = banded.shape
-    out_shape = [in_hbm(rank.shape, F32), shaped((2, 128), F32)]
-    out_specs = [hbm(), vmem()]
-    scratch = []
-    if not last:
+    shape = (seeds, blocks * width)
+    operands = tuple(scalars) + tuple(vectors) + tuple(off_chip(x) for x in tuple(arrays) + tuple(old)) + tuple(gaps)
+    if last:
+        out_shape = (in_hbm(shape, F32), shaped((devices, 1, 256), F32))
+        out_specs = (hbm(), vmem())
+        scratch = [pltpu.SemaphoreType.DMA]
+    else:
         edge = shaped((seeds, width), BF16)
-        out_shape += [in_hbm((blocks, seeds, width), BF16), edge, edge, in_hbm(fetched.shape, BF16)]
-        out_specs += [hbm(), vmem(), vmem(), hbm()]
+        out_shape = (in_hbm(shape, F32), edge, edge, in_hbm(fetched.shape, BF16))
+        out_specs = (hbm(), vmem(), vmem(), hbm())
         scratch = [
             VMEM((blocks, seeds, width), BF16),
             VMEM(fetched.shape, BF16),
-            pltpu.SemaphoreType.DMA((8,)),
             pltpu.SemaphoreType.DMA((4,)),
         ]
     return pl.pallas_call(
         functools.partial(finish_kernel, last, vertices),
-        out_shape=tuple(out_shape),
-        in_specs=[smem()] * 5 + [vmem()] * 5 + [hbm()] * 4,
-        out_specs=tuple(out_specs),
+        out_shape=out_shape,
+        in_specs=[smem()] * len(scalars)
+        + [vmem()] * len(vectors)
+        + [hbm()] * (len(arrays) + len(old))
+        + [vmem()] * len(gaps),
+        out_specs=out_specs,
         scratch_shapes=scratch
         + [
             VMEM(tiles.shape, BF16),
             VMEM((blocks + 1, seeds, width), F32),
             VMEM((blocks, seeds, width), F32),
-            VMEM(rank.shape, F32),
+            VMEM(shape, F32),
             VMEM((2, width, width), BF16),
             pltpu.SemaphoreType.DMA((2,)),
-            pltpu.SemaphoreType.DMA((tiles.shape[0] // UNROLL,)),
-            pltpu.SemaphoreType.DMA((2,)),
+            pltpu.SemaphoreType.DMA((tiles.shape[0] // PIECE,)),
+            pltpu.SemaphoreType.DMA,
             pltpu.SemaphoreType.DMA((8,)),
         ],
         compiler_params=PARAMS,
@@ -411,16 +468,16 @@
 
 
 def stats_kernel(seeds, vertices, group_ref, got_ref, change_ref, total_ref, own_ref):
-    got = got_ref[...]
-    odd = lax.broadcasted_iota(I32, got.shape, 0) % 2 == 1
-    one = jnp.sum(jnp.where(odd, got, 0.0), axis=0, keepdims=True)
-    zero = jnp.sum(jnp.where(odd, 0.0, got), axis=0, keepdims=True)
-    mine = jnp.where(group_ref[0] == 1, one, zero)
-    both = one + zero
+    devices, _, lanes = got_ref.shape
+    sums = [jnp.zeros((1, lanes), F32), jnp.zeros((1, lanes), F32)]
+    for d in range(devices):
+        sums[d % 2] = sums[d % 2] + got_ref[d]
+    mine = jnp.where(group_ref[0] == 1, sums[1], sums[0])
+    both = sums[0] + sums[1]
     for i in range(ITERS):
-        lanes = slice(i * seeds, (i + 1) * seeds)
-        change_ref[i : i + 1, :] = mine[:, lanes] / vertices
-        total_ref[:, i : i + 1] = jnp.sum(both[:, lanes] / vertices, axis=1, keepdims=True) / (2 * seeds)
+        at = slice(i * seeds, (i + 1) * seeds)
+        change_ref[i : i + 1, :] = mine[:, at] / vertices
+        total_ref[:, i : i + 1] = jnp.sum(both[:, at] / vertices, axis=1, keepdims=True) / (2 * seeds)
     own_ref[...] = mine[:, ITERS * seeds :]
 
 
@@ -428,7 +485,7 @@
     blocks, _, width, _ = band_tiles.shape
     seeds = rank_in.shape[0]
     peers = lax.axis_size("dom")
-    groups = lax.axis_size("seed")
+    devices = peers * lax.axis_size("seed")
     vertices = blocks * width * peers
     first = (lax.axis_index("dom") * (blocks * width)).astype(I32).reshape(1)
     group = lax.axis_index("seed").astype(I32).reshape(1)
@@ -439,45 +496,25 @@
     wanted = lax.all_to_all(request, "dom", split_axis=0, concat_axis=0, tiled=True)
     source, slab, head, tail = prep(rank_in, dangling, blocks)
     message = pack_first(wanted, source, slab, peers)
-    rank = rank_in
-    rows = []
+    old, rank = None, rank_in
+    gaps = []
     for iteration in range(ITERS):
         last = iteration + 1 == ITERS
         fetched = lax.all_to_all(message, "dom", split_axis=0, concat_axis=0, tiled=True)
         left = lax.ppermute(tail, "dom", [(i, i + 1) for i in range(peers - 1)])
         right = lax.ppermute(head, "dom", [(i + 1, i) for i in range(peers - 1)])
-        banded = band(source, band_tiles)
-        done = finish(
-            last,
-            vertices,
-            first,
-            tile_count,
-            slot,
-            target,
-            wanted,
-            seeds_at,
-            dangling,
-            left,
-            right,
-            fetched,
-            banded,
-            rank,
-            off_tiles,
-            band_tiles,
-        )
-        rank, stats = done[:2]
-        rows.append(stats[0:1, :seeds])
-        if not last:
-            source, head, tail, message = done[2:]
-    rows.append(stats[1:2, :seeds])
-    line = jnp.concatenate(rows, axis=1)
-    got = lax.all_to_all(
-        jnp.broadcast_to(line, (peers * groups, line.shape[1])),
-        ("dom", "seed"),
-        split_axis=0,
-        concat_axis=0,
-        tiled=True,
-    )
+        gap_at = (iteration - 1) * seeds if iteration > 0 else None
+        banded, *gap = band(gap_at, rank, old, band_tiles, dangling)
+        gaps += gap
+        scalars = (first, tile_count, slot, target, wanted)
+        vectors = (seeds_at, dangling, left, right, fetched)
+        arrays = (banded, off_tiles, band_tiles)
+        if last:
+            rank, line = finish(last, vertices, devices, scalars, vectors, arrays, (rank,), gaps)
+        else:
+            old = rank
+            rank, head, tail, message = finish(last, vertices, devices, scalars, vectors, arrays)
+    got = lax.all_to_all(line, ("dom", "seed"), split_axis=0, concat_axis=0, tiled=True)
     change, total, own = pl.pallas_call(
         functools.partial(stats_kernel, seeds, vertices),
         out_shape=(shaped((ITERS, seeds), F32), shaped((1, ITERS), F32), shaped((1, seeds), F32)),

time: 196 us -> 187 us (0.954)
  Pallas kernels: 83.5 us -> 70.1 us
  waiting for transfers between devices: 49.7 us -> 55.4 us
    all_to_all x3, waiting for transfers between devices: 31.6 us -> 39.6 us  [on_device(): lax.all_to_all(message, 'dom', split_axis=0, concat_axis=0, tiled=True)]
    pallas_call x3, Pallas kernels: 37 us -> 30 us  [band(): pl.pallas_call(functools.partial(band_kernel, gap_at), out_shape=tuple(ou...]
    pallas_call x3, Pallas kernels: 38.6 us -> 32.1 us  [finish(): pl.pallas_call(functools.partial(finish_kernel, last, vertices), out_shap...]
    all_to_all x3, starting transfers between devices: 24.1 us -> 21.8 us  [on_device(): lax.all_to_all(message, 'dom', split_axis=0, concat_axis=0, tiled=True)]
    ppermute x3, waiting for transfers between devices: 3.16 us -> 0.93 us  [on_device(): right = lax.ppermute(head, 'dom', [(i + 1, i) for i in range(peers - 1)])]
  transfers between devices with their start and end apart: 11 -> 11, of which waited for: 6 -> 6; matrix products, arithmetic and copies ran while one was open for 0% -> 0% of each run, Pallas kernels for 20% -> 17%
where the time goes in v3:
time: 187 us
  Pallas kernels  70.1 us (37%)
  starting transfers between devices  57.9 us (31%)
  waiting for transfers between devices  55.4 us (30%)
    all_to_all x3, waiting for transfers between devices, on_device(): lax.all_to_all(message, 'dom', split_axis=0, concat_axis=0, tiled=True)  39.6 us
    pallas_call x3, Pallas kernels, finish(): pl.pallas_call(functools.partial(finish_kernel, last, vertices), out_shap...  32.1 us
    pallas_call x3, Pallas kernels, band(): pl.pallas_call(functools.partial(band_kernel, gap_at), out_shape=tuple(ou...  30 us
    all_to_all x3, starting transfers between devices, on_device(): lax.all_to_all(message, 'dom', split_axis=0, concat_axis=0, tiled=True)  21.8 us
    all_to_all x1, starting transfers between devices, on_device(): lax.all_to_all(request, 'dom', split_axis=0, concat_axis=0, tiled=True)  12 us
    all_to_all x1, starting transfers between devices, on_device(): lax.all_to_all(line, ('dom', 'seed'), split_axis=0, concat_axis=0, tiled=...  11.1 us
    all_to_all x1, waiting for transfers between devices, on_device(): lax.all_to_all(line, ('dom', 'seed'), split_axis=0, concat_axis=0, tiled=...  9.81 us
    ppermute x3, starting transfers between devices, on_device(): left = lax.ppermute(tail, 'dom', [(i, i + 1) for i in range(peers - 1)])  8.75 us
  transfers between devices with their start and end apart: 11, of which 6 were waited for; matrix products, arithmetic and copies ran while one was open for 0% of the time, Pallas kernels for 17%

profile of v3, /device:TPU:1, one launch (start us, length us, event | category | flops | bytes accessed | tf_op | source)
XLA Modules:
  0.0 186.5 jit_solution(8021695831051614446)
XLA Ops:
  2.7 12.0 %all-to-all-start = ((s32[64,1,128]{2,1,0:T(1,128)}), s32[64,1,128]{2,1,0:T(1,128)S(1)}, u32[]{:S(2)}, u32[]{:S(2)}) async-start(s32[64,1,128]{2,1,0:T(1,128)} %bitcast.21), calls=%async_computation | async-start | bytes 65536 | tf_op jit(solution)/shard_map/all_to_all | solution.py:496
  15.5 2.4 %prep.1 = (bf16[128,64,128]{2,1,0:T(8,128)(2,1)S(1)}, bf16[8,128]{1,0:T(8,128)(2,1)S(1)}, bf16[64,128]{1,0:T(8,128)(2,1)S(1)}, bf16[64,128]{1,0:T(8,128)(2,1)S(1)}) custom-call(f32[64,16384]{1,0:T(8,128)} %refs_0_.3, s32[128,128]{1,0:T(8,128)S(1)} %bitcast.10), custom_call_target="tpu_custom_call" | custom-call | tf_op jit(solution)/shard_map/prep/pallas_call | solution.py:136
  17.9 5.1 %all-to-all-done = s32[64,1,128]{2,1,0:T(1,128)S(1)} async-done(((s32[64,1,128]{2,1,0:T(1,128)}), s32[64,1,128]{2,1,0:T(1,128)S(1)}, u32[]{:S(2)}, u32[]{:S(2)}) %all-to-all-start) | async-done | bytes 32800 | tf_op jit(solution)/shard_map/all_to_all | solution.py:496
  23.0 2.5 %pack.1 = bf16[64,136,128]{2,1,0:T(8,128)(2,1)} custom-call(s32[64,128]{1,0:T(8,128)S(1)} %bitcast.17, bf16[128,64,128]{2,1,0:T(8,128)(2,1)S(1)} %get-tuple-element.33.source_ref, bf16[8,128]{1,0:T(8,128)(2,1)S(1)} %get-tuple-element.34.slab_ref), custom_call_target="tpu_custom_call" | custom-call | tf_op jit(solution)/shard_map/pack/pallas_call | solution.py:177
  25.6 4.7 %all-to-all-start.1 = ((bf16[64,136,128]{2,1,0:T(8,128)(2,1)}), bf16[64,136,128]{2,1,0:T(8,128)(2,1)S(1)}, u32[]{:S(2)}, u32[]{:S(2)}) async-start(bf16[64,136,128]{2,1,0:T(8,128)(2,1)} %pack.1), calls=%async_computation.1 | async-start | bytes 4456448 | tf_op jit(solution)/shard_map/all_to_all | solution.py:503
  30.3 2.9 %collective-permute-start = (bf16[64,128]{1,0:T(8,128)(2,1)S(1)}, bf16[64,128]{1,0:T(8,128)(2,1)S(1)}, u32[]{:S(2)}, u32[]{:S(2)}) collective-permute-start(bf16[64,128]{1,0:T(8,128)(2,1)S(1)} %get-tuple-element.31), channel_id=1, source_target_pairs={{0,2},{2,4},{4,6},{6,8},{8,10},{10,12},{12,14},{14,16},{16,18},{18... | collective-permute-start | bytes 49160 | tf_op jit(solution)/shard_map/ppermute | solution.py:504
  34.7 9.5 %band.3.refs_10_ = f32[128,64,128]{2,1,0:T(8,128)} custom-call(f32[64,16384]{1,0:T(8,128)} %refs_0_.3, bf16[128,3,128,128]{3,2,1,0:T(8,128)(2,1)} %refs_12_.5, s32[128,128]{1,0:T(8,128)S(1)} %bitcast.11), custom_call_target="tpu_custom_call" | custom-call | tf_op jit(solution)/shard_map/band/pallas_call | solution.py:267
  45.1 13.5 %all-to-all-done.1.refs_9_ = bf16[64,136,128]{2,1,0:T(8,128)(2,1)S(1)} async-done(((bf16[64,136,128]{2,1,0:T(8,128)(2,1)}), bf16[64,136,128]{2,1,0:T(8,128)(2,1)S(1)}, u32[]{:S(2)}, u32[]{:S(2)}) %all-to-all-start.1) | async-done | bytes 2228256 | tf_op jit(solution)/shard_map/all_to_all | solution.py:503
  58.6 10.3 %finish.3 = (f32[64,16384]{1,0:T(8,128)}, bf16[64,128]{1,0:T(8,128)(2,1)S(1)}, bf16[64,128]{1,0:T(8,128)(2,1)S(1)}, bf16[64,136,128]{2,1,0:T(8,128)(2,1)}) custom-call(s32[1]{0:T(128)} %bitcast.refs_0_, s32[1]{0:T(128)S(6)} %copy.19.count_ref.refs_1_, s32[1,512]{1,0:T(1,128)S(1)} %copy-done.2, s32[1,512]{1,0:T(1,128)S(1)} %copy-done.3, ...), custom_call_target="tpu_custom_call" | custom-call | tf_op jit(solution)/shard_map/finish/pallas_call | solution.py:445
  69.0 8.6 %all-to-all-start.2 = ((bf16[64,136,128]{2,1,0:T(8,128)(2,1)}), bf16[64,136,128]{2,1,0:T(8,128)(2,1)S(1)}, u32[]{:S(2)}, u32[]{:S(2)}) async-start(bf16[64,136,128]{2,1,0:T(8,128)(2,1)} %get-tuple-element.37), calls=%async_computation.2 | async-start | bytes 4456448 | tf_op jit(solution)/shard_map/all_to_all | solution.py:503
  77.6 2.9 %collective-permute-start.2 = (bf16[64,128]{1,0:T(8,128)(2,1)S(1)}, bf16[64,128]{1,0:T(8,128)(2,1)S(1)}, u32[]{:S(2)}, u32[]{:S(2)}) collective-permute-start(bf16[64,128]{1,0:T(8,128)(2,1)S(1)} %get-tuple-element.35), channel_id=1, source_target_pairs={{0,2},{2,4},{4,6},{6,8},{8,10},{10,12},{12,14},{14,16},{16,18},{18... | collective-permute-start | bytes 49160 | tf_op jit(solution)/shard_map/ppermute | solution.py:504
  80.6 1.5 collective-permute-start.3
  82.0 10.2 %band.4 = (f32[128,64,128]{2,1,0:T(8,128)}, f32[1,128]{1,0:T(1,128)S(1)}) custom-call(f32[64,16384]{1,0:T(8,128)} %get-tuple-element.38.rank_hbm.refs_0_, f32[64,16384]{1,0:T(8,128)} %refs_0_.3, bf16[128,3,128,128]{3,2,1,0:T(8,128)(2,1)} %refs_12_.5, s32[128,128]{1,0:T(8,128)S(1)} %bitcast.13), custom_call_target="tpu_custom_call" | custom-call | tf_op jit(solution)/shard_map/band/pallas_call | solution.py:267
  92.3 13.3 %all-to-all-done.2.refs_9_ = bf16[64,136,128]{2,1,0:T(8,128)(2,1)S(1)} async-done(((bf16[64,136,128]{2,1,0:T(8,128)(2,1)}), bf16[64,136,128]{2,1,0:T(8,128)(2,1)S(1)}, u32[]{:S(2)}, u32[]{:S(2)}) %all-to-all-start.2) | async-done | bytes 2228256 | tf_op jit(solution)/shard_map/all_to_all | solution.py:503
  105.6 10.3 %finish.4 = (f32[64,16384]{1,0:T(8,128)}, bf16[64,128]{1,0:T(8,128)(2,1)S(1)}, bf16[64,128]{1,0:T(8,128)(2,1)S(1)}, bf16[64,136,128]{2,1,0:T(8,128)(2,1)}) custom-call(s32[1]{0:T(128)} %bitcast.refs_0_, s32[1]{0:T(128)S(6)} %copy.19.count_ref.refs_1_, s32[1,512]{1,0:T(1,128)S(1)} %copy-done.2, s32[1,512]{1,0:T(1,128)S(1)} %copy-done.3, ...), custom_call_target="tpu_custom_call" | custom-call | tf_op jit(solution)/shard_map/finish/pallas_call | solution.py:445
  115.9 8.5 %all-to-all-start.3 = ((bf16[64,136,128]{2,1,0:T(8,128)(2,1)}), bf16[64,136,128]{2,1,0:T(8,128)(2,1)S(1)}, u32[]{:S(2)}, u32[]{:S(2)}) async-start(bf16[64,136,128]{2,1,0:T(8,128)(2,1)} %get-tuple-element.42), calls=%async_computation.3 | async-start | bytes 4456448 | tf_op jit(solution)/shard_map/all_to_all | solution.py:503
  124.4 2.9 %collective-permute-start.4 = (bf16[64,128]{1,0:T(8,128)(2,1)S(1)}, bf16[64,128]{1,0:T(8,128)(2,1)S(1)}, u32[]{:S(2)}, u32[]{:S(2)}) collective-permute-start(bf16[64,128]{1,0:T(8,128)(2,1)S(1)} %get-tuple-element.40), channel_id=1, source_target_pairs={{0,2},{2,4},{4,6},{6,8},{8,10},{10,12},{12,14},{14,16},{16,18},{18... | collective-permute-start | bytes 49160 | tf_op jit(solution)/shard_map/ppermute | solution.py:504
  127.3 1.5 collective-permute-start.5
  128.8 10.2 %band.5 = (f32[128,64,128]{2,1,0:T(8,128)}, f32[1,128]{1,0:T(1,128)S(1)}) custom-call(f32[64,16384]{1,0:T(8,128)} %get-tuple-element.43.rank_hbm.refs_13_, f32[64,16384]{1,0:T(8,128)} %get-tuple-element.38.rank_hbm.refs_0_, bf16[128,3,128,128]{3,2,1,0:T(8,128)(2,1)} %refs_12_.5, s32[128,128]{1,0:T(8,128)S(1)} %bitcast.15), custom_call_target="tpu_custom_call" | custom-call | tf_op jit(solution)/shard_map/band/pallas_call | solution.py:267
  139.1 12.8 %all-to-all-done.3.refs_9_ = bf16[64,136,128]{2,1,0:T(8,128)(2,1)S(1)} async-done(((bf16[64,136,128]{2,1,0:T(8,128)(2,1)}), bf16[64,136,128]{2,1,0:T(8,128)(2,1)S(1)}, u32[]{:S(2)}, u32[]{:S(2)}) %all-to-all-start.3) | async-done | bytes 2228256 | tf_op jit(solution)/shard_map/all_to_all | solution.py:503
  151.8 11.5 %finish.5 = (f32[64,16384]{1,0:T(8,128)}, f32[128,1,256]{2,1,0:T(1,128)}) custom-call(s32[1]{0:T(128)} %bitcast.refs_0_, s32[1]{0:T(128)S(6)} %copy.19.count_ref.refs_1_, s32[1,512]{1,0:T(1,128)S(1)} %copy-done.2, s32[1,512]{1,0:T(1,128)S(1)} %copy-done.3, s32[64,128]{1,0:T(8,128)S(1)} %bitcast.20, s32[64,1]{1,0:T(8,128)S(1)} %copy.18.refs_5_, ...), custom_call_target="tpu_custom_call" | custom-call | tf_op jit(solution)/shard_map/finish/pallas_call | solution.py:445
  163.3 11.1 %all-to-all-start.4 = ((f32[128,1,256]{2,1,0:T(1,128)}), f32[128,1,256]{2,1,0:T(1,128)S(1)}, u32[]{:S(2)}, u32[]{:S(2)}) async-start(f32[128,1,256]{2,1,0:T(1,128)} %get-tuple-element.48), calls=%async_computation.4 | async-start | bytes 262144 | tf_op jit(solution)/shard_map/all_to_all | solution.py:517
  174.4 9.8 %all-to-all-done.4.got_ref = f32[128,1,256]{2,1,0:T(1,128)S(1)} async-done(((f32[128,1,256]{2,1,0:T(1,128)}), f32[128,1,256]{2,1,0:T(1,128)S(1)}, u32[]{:S(2)}, u32[]{:S(2)}) %all-to-all-start.4) | async-done | bytes 131104 | tf_op jit(solution)/shard_map/all_to_all | solution.py:517
  184.9 1.6 stats.1
  (21 shorter events, 5.3 us)
Async XLA Ops:
  2.7 20.3 %all-to-all-start = ((s32[64,1,128]{2,1,0:T(1,128)}), s32[64,1,128]{2,1,0:T(1,128)S(1)}, u32[]{:S(2)}, u32[]{:S(2)}) async-start(s32[64,1,128]{2,1,0:T(1,128)} %bitcast.21), calls=%async_computation | async-start | bytes 65536 | tf_op jit(solution)/shard_map/all_to_all | solution.py:496
  14.7 0.8 copy-start
  23.0 11.5 %copy-start.5 = (s32[64]{0:T(128)S(1)}, s32[64]{0:T(128)}, u32[]{:S(2)}) copy-start(s32[64]{0:T(128)} %param.14) | copy-start | bytes 772
  23.0 11.6 %copy-start.1 = (s32[16384]{0:T(1024)S(1)}, s32[16384]{0:T(1024)}, u32[]{:S(2)}) copy-start(s32[16384]{0:T(1024)} %param.15) | copy-start | bytes 196612
  25.6 33.1 %all-to-all-start.1 = ((bf16[64,136,128]{2,1,0:T(8,128)(2,1)}), bf16[64,136,128]{2,1,0:T(8,128)(2,1)S(1)}, u32[]{:S(2)}, u32[]{:S(2)}) async-start(bf16[64,136,128]{2,1,0:T(8,128)(2,1)} %pack.1), calls=%async_computation.1 | async-start | bytes 4456448 | tf_op jit(solution)/shard_map/all_to_all | solution.py:503
  30.3 13.9 %collective-permute-start = (bf16[64,128]{1,0:T(8,128)(2,1)S(1)}, bf16[64,128]{1,0:T(8,128)(2,1)S(1)}, u32[]{:S(2)}, u32[]{:S(2)}) collective-permute-start(bf16[64,128]{1,0:T(8,128)(2,1)S(1)} %get-tuple-element.31), channel_id=1, source_target_pairs={{0,2},{2,4},{4,6},{6,8},{8,10},{10,12},{12,14},{14,16},{16,18},{18... | collective-permute-start | bytes 49160 | tf_op jit(solution)/shard_map/ppermute | solution.py:504
  33.2 11.9 %collective-permute-start.1 = (bf16[64,128]{1,0:T(8,128)(2,1)S(1)}, bf16[64,128]{1,0:T(8,128)(2,1)S(1)}, u32[]{:S(2)}, u32[]{:S(2)}) collective-permute-start(bf16[64,128]{1,0:T(8,128)(2,1)S(1)} %get-tuple-element.32), channel_id=1, source_target_pairs={{2,0},{4,2},{6,4},{8,6},{10,8},{12,10},{14,12},{16,14},{18,16},{20... | collective-permute-start | bytes 49160 | tf_op jit(solution)/shard_map/ppermute | solution.py:505
  34.6 24.0 %copy-start.2 = (s32[1,512]{1,0:T(1,128)S(1)}, s32[1,512]{1,0:T(1,128)}, u32[]{:S(2)}) copy-start(s32[1,512]{1,0:T(1,128)} %get-tuple-element.28.refs_2_) | copy-start | bytes 6148
  34.7 24.0 %copy-start.3 = (s32[1,512]{1,0:T(1,128)S(1)}, s32[1,512]{1,0:T(1,128)}, u32[]{:S(2)}) copy-start(s32[1,512]{1,0:T(1,128)} %get-tuple-element.29.refs_3_) | copy-start | bytes 6148
  69.0 36.6 %all-to-all-start.2 = ((bf16[64,136,128]{2,1,0:T(8,128)(2,1)}), bf16[64,136,128]{2,1,0:T(8,128)(2,1)S(1)}, u32[]{:S(2)}, u32[]{:S(2)}) async-start(bf16[64,136,128]{2,1,0:T(8,128)(2,1)} %get-tuple-element.37), calls=%async_computation.2 | async-start | bytes 4456448 | tf_op jit(solution)/shard_map/all_to_all | solution.py:503
  77.6 14.6 %collective-permute-start.2 = (bf16[64,128]{1,0:T(8,128)(2,1)S(1)}, bf16[64,128]{1,0:T(8,128)(2,1)S(1)}, u32[]{:S(2)}, u32[]{:S(2)}) collective-permute-start(bf16[64,128]{1,0:T(8,128)(2,1)S(1)} %get-tuple-element.35), channel_id=1, source_target_pairs={{0,2},{2,4},{4,6},{6,8},{8,10},{10,12},{12,14},{14,16},{16,18},{18... | collective-permute-start | bytes 49160 | tf_op jit(solution)/shard_map/ppermute | solution.py:504
  80.6 11.7 %collective-permute-start.3 = (bf16[64,128]{1,0:T(8,128)(2,1)S(1)}, bf16[64,128]{1,0:T(8,128)(2,1)S(1)}, u32[]{:S(2)}, u32[]{:S(2)}) collective-permute-start(bf16[64,128]{1,0:T(8,128)(2,1)S(1)} %get-tuple-element.36), channel_id=1, source_target_pairs={{2,0},{4,2},{6,4},{8,6},{10,8},{12,10},{14,12},{16,14},{18,16},{20... | collective-permute-start | bytes 49160 | tf_op jit(solution)/shard_map/ppermute | solution.py:505
  115.9 35.9 %all-to-all-start.3 = ((bf16[64,136,128]{2,1,0:T(8,128)(2,1)}), bf16[64,136,128]{2,1,0:T(8,128)(2,1)S(1)}, u32[]{:S(2)}, u32[]{:S(2)}) async-start(bf16[64,136,128]{2,1,0:T(8,128)(2,1)} %get-tuple-element.42), calls=%async_computation.3 | async-start | bytes 4456448 | tf_op jit(solution)/shard_map/all_to_all | solution.py:503
  124.4 14.7 %collective-permute-start.4 = (bf16[64,128]{1,0:T(8,128)(2,1)S(1)}, bf16[64,128]{1,0:T(8,128)(2,1)S(1)}, u32[]{:S(2)}, u32[]{:S(2)}) collective-permute-start(bf16[64,128]{1,0:T(8,128)(2,1)S(1)} %get-tuple-element.40), channel_id=1, source_target_pairs={{0,2},{2,4},{4,6},{6,8},{8,10},{10,12},{12,14},{14,16},{16,18},{18... | collective-permute-start | bytes 49160 | tf_op jit(solution)/shard_map/ppermute | solution.py:504
  127.3 11.8 %collective-permute-start.5 = (bf16[64,128]{1,0:T(8,128)(2,1)S(1)}, bf16[64,128]{1,0:T(8,128)(2,1)S(1)}, u32[]{:S(2)}, u32[]{:S(2)}) collective-permute-start(bf16[64,128]{1,0:T(8,128)(2,1)S(1)} %get-tuple-element.41), channel_id=1, source_target_pairs={{2,0},{4,2},{6,4},{8,6},{10,8},{12,10},{14,12},{16,14},{18,16},{20... | collective-permute-start | bytes 49160 | tf_op jit(solution)/shard_map/ppermute | solution.py:505
  163.3 20.9 %all-to-all-start.4 = ((f32[128,1,256]{2,1,0:T(1,128)}), f32[128,1,256]{2,1,0:T(1,128)S(1)}, u32[]{:S(2)}, u32[]{:S(2)}) async-start(f32[128,1,256]{2,1,0:T(1,128)} %get-tuple-element.48), calls=%async_computation.4 | async-start | bytes 262144 | tf_op jit(solution)/shard_map/all_to_all | solution.py:517
  184.3 0.7 copy-start.4

commit v4 on v3

--- a/solution.py
+++ b/solution.py
@@ -185,11 +185,17 @@
     )(wanted, source, slab)
 
 
-def band_kernel(gap_at, rank_hbm, *refs):
+def from_seed(seed_ref, first_ref, width):
+    seeds = seed_ref.shape[0]
+    here = jnp.broadcast_to(seed_ref[...] - first_ref[0], (seeds, width))
+    return here - lax.broadcasted_iota(I32, (seeds, width), 1)
+
+
+def band_kernel(gap_at, first_ref, rank_hbm, *refs):
     refs = list(refs)
     old_hbm = None if gap_at is None else refs.pop(0)
-    tiles_hbm, dangling_ref, out_hbm = refs[:3]
-    refs = refs[3:]
+    tiles_hbm, dangling_ref, seed_ref, out_hbm = refs[:4]
+    refs = refs[4:]
     gap_ref = None if gap_at is None else refs.pop(0)
     rank, source, tiles, banded, sem, rank_sem, out_sem = refs[:7]
     blocks, seeds, width = banded.shape
@@ -234,6 +240,7 @@
         return gap
 
     gap = prepare(0, gap)
+    away = from_seed(seed_ref, first_ref, width)
     zero = jnp.zeros((seeds, width), BF16)
     for c in range(chunks):
         if c + 1 < chunks:
@@ -244,7 +251,7 @@
             after = source[b + 1] if b + 1 < blocks else zero
             x = jnp.concatenate([before, source[b], after], axis=1)
             w = jnp.concatenate([tiles[b, 0], tiles[b, 1], tiles[b, 2]], axis=1)
-            banded[b] = dot_nt(x, w)
+            banded[b] = DAMP * dot_nt(x, w) + jnp.where(away == b * width, 1.0 - DAMP, 0.0)
         flush(c).start()
     if gap_at is not None:
         gap_ref[...] = to_row(jnp.sum(gap, axis=1, keepdims=True), gap_at)
@@ -252,7 +259,7 @@
         flush(c).wait()
 
 
-def band(gap_at, rank, old, tiles, dangling):
+def band(gap_at, first, rank, old, tiles, dangling, seeds_at):
     blocks, _, width, _ = tiles.shape
     seeds = rank.shape[0]
     shape = (blocks, seeds, width)
@@ -267,7 +274,7 @@
     return pl.pallas_call(
         functools.partial(band_kernel, gap_at),
         out_shape=tuple(out_shape),
-        in_specs=[hbm()] * (len(ranks) + 1) + [vmem()],
+        in_specs=[smem()] + [hbm()] * (len(ranks) + 1) + [vmem()] * 2,
         out_specs=tuple(out_specs),
         scratch_shapes=[
             VMEM(rank.shape, F32),
@@ -281,12 +288,10 @@
         + extra,
         compiler_params=MIDDLE,
         name="band",
-    )(*(off_chip(x) for x in ranks), off_chip(tiles), dangling)
+    )(first, *(off_chip(x) for x in ranks), off_chip(tiles), dangling, seeds_at)
 
 
 UNROLL = 64
-PIECE = 32
-AHEAD = 6
 DEPTH = 8
 
 
@@ -310,7 +315,7 @@
         return pltpu.make_async_copy(at, edges.at[k], edge_sem.at[k])
 
     def tile_copy(g):
-        at = pl.ds(g * PIECE, PIECE)
+        at = pl.ds(g * UNROLL, UNROLL)
         return pltpu.make_async_copy(tiles_hbm.at[at], tiles.at[at], tile_sem.at[g])
 
     def rank_store(c):
@@ -318,15 +323,21 @@
         return pltpu.make_async_copy(rank.at[:, cols], next_hbm.at[:, cols], out_sem.at[c])
 
     trips = (count_ref[0] + UNROLL - 1) // UNROLL
-    pieces = trips * (UNROLL // PIECE)
-    for g in range(AHEAD):
-
-        @pl.when(g < pieces)
+    for g in range(tile_sem.shape[0]):
+
+        @pl.when(g < trips)
         def _():
             tile_copy(g).start()
 
+    loads = [pltpu.make_async_copy(banded_hbm, banded, base_sem)]
+    if last:
+        loads.append(pltpu.make_async_copy(rank_hbm, rank, rank_sem))
+    for load in loads:
+        load.start()
+    for k in range(2):
+        edge_copy(k).start()
     mass_row = jnp.sum(jnp.sum(fetched[:, CAP * seeds :, :].astype(F32), axis=0), axis=0, keepdims=True)
-    share = jnp.broadcast_to(to_column(mass_row, seeds) / vertices, (seeds, width))
+    share = jnp.broadcast_to(DAMP * (to_column(mass_row, seeds) / vertices), (seeds, width))
     zero = jnp.zeros((seeds, width), BF16)
     acc[...] = jnp.zeros_like(acc)
 
@@ -336,14 +347,7 @@
         return fetched[slot // CAP, pl.ds(at, seeds), :]
 
     def group(g, carry):
-        for k in range(UNROLL // PIECE):
-            piece = g * (UNROLL // PIECE) + k
-            tile_copy(piece).wait()
-
-            @pl.when(piece + AHEAD < pieces)
-            def _():
-                tile_copy(piece + AHEAD).start()
-
+        tile_copy(g).wait()
         first = g * UNROLL
         waiting = []
 
@@ -368,16 +372,7 @@
         add(0)
         return carry
 
-    early = jnp.minimum(trips, 2)
-    lax.fori_loop(0, early, group, 0)
-    loads = [pltpu.make_async_copy(banded_hbm, banded, base_sem)]
-    if last:
-        loads.append(pltpu.make_async_copy(rank_hbm, rank, rank_sem))
-    for load in loads:
-        load.start()
-    for k in range(2):
-        edge_copy(k).start()
-    lax.fori_loop(early, trips, group, 0)
+    lax.fori_loop(0, trips, group, 0)
     for k in range(2):
         edge_copy(k).wait()
     acc[0] = acc[0] + dot_nt(left_ref[...], edges[0])
@@ -385,19 +380,17 @@
     for load in loads:
         load.wait()
 
-    away = jnp.broadcast_to(seed_ref[...] - first_ref[0], (seeds, width)) - lax.broadcasted_iota(
-        I32, (seeds, width), 1
-    )
+    if last:
+        away = from_seed(seed_ref, first_ref, width)
 
     def update(b, carry):
         cols = pl.ds(pl.multiple_of(b * width, width), width)
-        at_seed = away == b * width
-        new = DAMP * (banded[b] + acc[b] + share) + jnp.where(at_seed, 1.0 - DAMP, 0.0)
+        new = banded[b] + (DAMP * acc[b] + share)
         if last:
             gap, own = carry
             gap = gap + jnp.abs(new - rank[:, cols])
             rank[:, cols] = new
-            return gap, own + jnp.where(at_seed, new, 0.0)
+            return gap, own + jnp.where(away == b * width, new, 0.0)
         rank[:, cols] = new
         dead = jnp.broadcast_to(dangling_ref[pl.ds(b, 1), :], (seeds, width)) != 0
         kept = jnp.where(dead, 0.0, new)
@@ -458,7 +451,7 @@
             VMEM(shape, F32),
             VMEM((2, width, width), BF16),
             pltpu.SemaphoreType.DMA((2,)),
-            pltpu.SemaphoreType.DMA((tiles.shape[0] // PIECE,)),
+            pltpu.SemaphoreType.DMA((tiles.shape[0] // UNROLL,)),
             pltpu.SemaphoreType.DMA,
             pltpu.SemaphoreType.DMA((8,)),
         ],
@@ -504,7 +497,7 @@
         left = lax.ppermute(tail, "dom", [(i, i + 1) for i in range(peers - 1)])
         right = lax.ppermute(head, "dom", [(i + 1, i) for i in range(peers - 1)])
         gap_at = (iteration - 1) * seeds if iteration > 0 else None
-        banded, *gap = band(gap_at, rank, old, band_tiles, dangling)
+        banded, *gap = band(gap_at, first, rank, old, band_tiles, dangling, seeds_at)
         gaps += gap
         scalars = (first, tile_count, slot, target, wanted)
         vectors = (seeds_at, dangling, left, right, fetched)
@@ -520,6 +513,7 @@
         out_shape=(shaped((ITERS, seeds), F32), shaped((1, ITERS), F32), shaped((1, seeds), F32)),
         in_specs=[smem(), vmem()],
         out_specs=(vmem(),) * 3,
+        compiler_params=SMALL,
         name="stats",
     )(group, got)
     return (rank, change, total.reshape(ITERS), own.reshape(seeds))

time: 187 us -> 183 us (0.979)
  Pallas kernels: 70.1 us -> 67.3 us
  starting transfers between devices: 57.9 us -> 56 us
    all_to_all x1, starting transfers between devices: 11.1 us -> 9.07 us  [on_device(): lax.all_to_all(line, ('dom', 'seed'), split_axis=0, concat_axis=0, tiled=...]
    pallas_call x3, Pallas kernels: 32.1 us -> 30.2 us  [finish(): pl.pallas_call(functools.partial(finish_kernel, last, vertices), out_shap...]
  transfers between devices with their start and end apart: 11 -> 11, of which waited for: 6 -> 8; matrix products, arithmetic and copies ran while one was open for 0% -> 0% of each run, Pallas kernels for 17% -> 18%
where the time goes in v4:
time: 183 us
  Pallas kernels  67.3 us (37%)
  waiting for transfers between devices  56.8 us (31%)
  starting transfers between devices  56 us (31%)
    all_to_all x3, waiting for transfers between devices, on_device(): lax.all_to_all(message, 'dom', split_axis=0, concat_axis=0, tiled=True)  40.3 us
    pallas_call x3, Pallas kernels, finish(): pl.pallas_call(functools.partial(finish_kernel, last, vertices), out_shap...  30.2 us
    pallas_call x3, Pallas kernels, band(): pl.pallas_call(functools.partial(band_kernel, gap_at), out_shape=tuple(ou...  30 us
    all_to_all x3, starting transfers between devices, on_device(): lax.all_to_all(message, 'dom', split_axis=0, concat_axis=0, tiled=True)  22.2 us
    all_to_all x1, starting transfers between devices, on_device(): lax.all_to_all(request, 'dom', split_axis=0, concat_axis=0, tiled=True)  12 us
    all_to_all x1, waiting for transfers between devices, on_device(): lax.all_to_all(line, ('dom', 'seed'), split_axis=0, concat_axis=0, tiled=...  9.82 us
    all_to_all x1, starting transfers between devices, on_device(): lax.all_to_all(line, ('dom', 'seed'), split_axis=0, concat_axis=0, tiled=...  9.07 us
    ppermute x3, starting transfers between devices, on_device(): left = lax.ppermute(tail, 'dom', [(i, i + 1) for i in range(peers - 1)])  8.75 us
  transfers between devices with their start and end apart: 11, of which 8 were waited for; matrix products, arithmetic and copies ran while one was open for 0% of the time, Pallas kernels for 18%

profile of v4, /device:TPU:1, one launch (start us, length us, event | category | flops | bytes accessed | tf_op | source)
XLA Modules:
  0.0 182.5 jit_solution(14554453945729443769)
XLA Ops:
  1.3 1.4 plan.1
  2.7 12.0 %all-to-all-start = ((s32[64,1,128]{2,1,0:T(1,128)}), s32[64,1,128]{2,1,0:T(1,128)S(1)}, u32[]{:S(2)}, u32[]{:S(2)}) async-start(s32[64,1,128]{2,1,0:T(1,128)} %bitcast.21), calls=%async_computation | async-start | bytes 65536 | tf_op jit(solution)/shard_map/all_to_all | solution.py:489
  15.5 2.4 %prep.1 = (bf16[128,64,128]{2,1,0:T(8,128)(2,1)S(1)}, bf16[8,128]{1,0:T(8,128)(2,1)S(1)}, bf16[64,128]{1,0:T(8,128)(2,1)S(1)}, bf16[64,128]{1,0:T(8,128)(2,1)S(1)}) custom-call(f32[64,16384]{1,0:T(8,128)} %refs_0_.3, s32[128,128]{1,0:T(8,128)S(1)} %bitcast.10), custom_call_target="tpu_custom_call" | custom-call | tf_op jit(solution)/shard_map/prep/pallas_call | solution.py:136
  17.9 5.1 %all-to-all-done = s32[64,1,128]{2,1,0:T(1,128)S(1)} async-done(((s32[64,1,128]{2,1,0:T(1,128)}), s32[64,1,128]{2,1,0:T(1,128)S(1)}, u32[]{:S(2)}, u32[]{:S(2)}) %all-to-all-start) | async-done | bytes 32800 | tf_op jit(solution)/shard_map/all_to_all | solution.py:489
  23.0 2.5 %pack.1 = bf16[64,136,128]{2,1,0:T(8,128)(2,1)} custom-call(s32[64,128]{1,0:T(8,128)S(1)} %bitcast.17, bf16[128,64,128]{2,1,0:T(8,128)(2,1)S(1)} %get-tuple-element.33.source_ref, bf16[8,128]{1,0:T(8,128)(2,1)S(1)} %get-tuple-element.34.slab_ref), custom_call_target="tpu_custom_call" | custom-call | tf_op jit(solution)/shard_map/pack/pallas_call | solution.py:177
  25.6 4.7 %all-to-all-start.1 = ((bf16[64,136,128]{2,1,0:T(8,128)(2,1)}), bf16[64,136,128]{2,1,0:T(8,128)(2,1)S(1)}, u32[]{:S(2)}, u32[]{:S(2)}) async-start(bf16[64,136,128]{2,1,0:T(8,128)(2,1)} %pack.1), calls=%async_computation.1 | async-start | bytes 4456448 | tf_op jit(solution)/shard_map/all_to_all | solution.py:496
  30.3 2.9 %collective-permute-start = (bf16[64,128]{1,0:T(8,128)(2,1)S(1)}, bf16[64,128]{1,0:T(8,128)(2,1)S(1)}, u32[]{:S(2)}, u32[]{:S(2)}) collective-permute-start(bf16[64,128]{1,0:T(8,128)(2,1)S(1)} %get-tuple-element.31), channel_id=1, source_target_pairs={{0,2},{2,4},{4,6},{6,8},{8,10},{10,12},{12,14},{14,16},{16,18},{18... | collective-permute-start | bytes 49160 | tf_op jit(solution)/shard_map/ppermute | solution.py:497
  33.2 1.3 collective-permute-start.1
  34.7 9.5 %band.3.refs_10_ = f32[128,64,128]{2,1,0:T(8,128)} custom-call(s32[1]{0:T(128)} %bitcast.first_ref.refs_0_, f32[64,16384]{1,0:T(8,128)} %refs_0_.3, bf16[128,3,128,128]{3,2,1,0:T(8,128)(2,1)} %refs_12_.5, s32[128,128]{1,0:T(8,128)S(1)} %bitcast.11, s32[64,1]{1,0:T(8,128)S(1)} %copy.24.refs_2_.refs_5_.refs_3_), custom_call_target="tpu_custom_call" | custom-call | tf_op jit(solution)/shard_map/band/pallas_call | solution.py:274
  45.1 13.5 %all-to-all-done.1.refs_9_ = bf16[64,136,128]{2,1,0:T(8,128)(2,1)S(1)} async-done(((bf16[64,136,128]{2,1,0:T(8,128)(2,1)}), bf16[64,136,128]{2,1,0:T(8,128)(2,1)S(1)}, u32[]{:S(2)}, u32[]{:S(2)}) %all-to-all-start.1) | async-done | bytes 2228256 | tf_op jit(solution)/shard_map/all_to_all | solution.py:496
  58.6 9.8 %finish.3 = (f32[64,16384]{1,0:T(8,128)}, bf16[64,128]{1,0:T(8,128)(2,1)S(1)}, bf16[64,128]{1,0:T(8,128)(2,1)S(1)}, bf16[64,136,128]{2,1,0:T(8,128)(2,1)}) custom-call(s32[1]{0:T(128)} %bitcast.first_ref.refs_0_, s32[1]{0:T(128)S(6)} %copy.25.count_ref.refs_1_, s32[1,512]{1,0:T(1,128)S(1)} %copy-done.2, s32[1,512]{1,0:T(1,128)S(1)} %copy-done.3, ...), custom_call_target="tpu_custom_call" | custom-call | tf_op jit(solution)/shard_map/finish/pallas_call | solution.py:438
  68.4 8.7 %all-to-all-start.2 = ((bf16[64,136,128]{2,1,0:T(8,128)(2,1)}), bf16[64,136,128]{2,1,0:T(8,128)(2,1)S(1)}, u32[]{:S(2)}, u32[]{:S(2)}) async-start(bf16[64,136,128]{2,1,0:T(8,128)(2,1)} %get-tuple-element.37), calls=%async_computation.2 | async-start | bytes 4456448 | tf_op jit(solution)/shard_map/all_to_all | solution.py:496
  77.1 2.9 %collective-permute-start.2 = (bf16[64,128]{1,0:T(8,128)(2,1)S(1)}, bf16[64,128]{1,0:T(8,128)(2,1)S(1)}, u32[]{:S(2)}, u32[]{:S(2)}) collective-permute-start(bf16[64,128]{1,0:T(8,128)(2,1)S(1)} %get-tuple-element.35), channel_id=1, source_target_pairs={{0,2},{2,4},{4,6},{6,8},{8,10},{10,12},{12,14},{14,16},{16,18},{18... | collective-permute-start | bytes 49160 | tf_op jit(solution)/shard_map/ppermute | solution.py:497
  80.0 1.5 collective-permute-start.3
  81.5 10.3 %band.4 = (f32[128,64,128]{2,1,0:T(8,128)}, f32[1,128]{1,0:T(1,128)S(1)}) custom-call(s32[1]{0:T(128)} %bitcast.first_ref.refs_0_, f32[64,16384]{1,0:T(8,128)} %get-tuple-element.38.rank_hbm.refs_0_, f32[64,16384]{1,0:T(8,128)} %refs_0_.3, bf16[128,3,128,128]{3,2,1,0:T(8,128)(2,1)} %refs_12_.5, s32[128,128]{1,0:T(8,128)S(1)} %bitcast.13, ...), custom_call_target="tpu_custom_call" | custom-call | tf_op jit(solution)/shard_map/band/pallas_call | solution.py:274
  92.0 13.5 %all-to-all-done.2.refs_9_ = bf16[64,136,128]{2,1,0:T(8,128)(2,1)S(1)} async-done(((bf16[64,136,128]{2,1,0:T(8,128)(2,1)}), bf16[64,136,128]{2,1,0:T(8,128)(2,1)S(1)}, u32[]{:S(2)}, u32[]{:S(2)}) %all-to-all-start.2) | async-done | bytes 2228256 | tf_op jit(solution)/shard_map/all_to_all | solution.py:496
  105.4 9.8 %finish.4 = (f32[64,16384]{1,0:T(8,128)}, bf16[64,128]{1,0:T(8,128)(2,1)S(1)}, bf16[64,128]{1,0:T(8,128)(2,1)S(1)}, bf16[64,136,128]{2,1,0:T(8,128)(2,1)}) custom-call(s32[1]{0:T(128)} %bitcast.first_ref.refs_0_, s32[1]{0:T(128)S(6)} %copy.25.count_ref.refs_1_, s32[1,512]{1,0:T(1,128)S(1)} %copy-done.2, s32[1,512]{1,0:T(1,128)S(1)} %copy-done.3, ...), custom_call_target="tpu_custom_call" | custom-call | tf_op jit(solution)/shard_map/finish/pallas_call | solution.py:438
  115.2 8.7 %all-to-all-start.3 = ((bf16[64,136,128]{2,1,0:T(8,128)(2,1)}), bf16[64,136,128]{2,1,0:T(8,128)(2,1)S(1)}, u32[]{:S(2)}, u32[]{:S(2)}) async-start(bf16[64,136,128]{2,1,0:T(8,128)(2,1)} %get-tuple-element.42), calls=%async_computation.3 | async-start | bytes 4456448 | tf_op jit(solution)/shard_map/all_to_all | solution.py:496
  123.9 2.9 %collective-permute-start.4 = (bf16[64,128]{1,0:T(8,128)(2,1)S(1)}, bf16[64,128]{1,0:T(8,128)(2,1)S(1)}, u32[]{:S(2)}, u32[]{:S(2)}) collective-permute-start(bf16[64,128]{1,0:T(8,128)(2,1)S(1)} %get-tuple-element.40), channel_id=1, source_target_pairs={{0,2},{2,4},{4,6},{6,8},{8,10},{10,12},{12,14},{14,16},{16,18},{18... | collective-permute-start | bytes 49160 | tf_op jit(solution)/shard_map/ppermute | solution.py:497
  128.2 10.3 %band.5 = (f32[128,64,128]{2,1,0:T(8,128)}, f32[1,128]{1,0:T(1,128)S(1)}) custom-call(s32[1]{0:T(128)} %bitcast.first_ref.refs_0_, f32[64,16384]{1,0:T(8,128)} %get-tuple-element.43.rank_hbm.refs_13_, f32[64,16384]{1,0:T(8,128)} %get-tuple-element.38.rank_hbm.refs_0_, bf16[128,3,128,128]{3,2,1,0:T(8,128)(2,1)} %refs_12_.5, s32[128,128]{1,0:T(8,128)S(1)} %bitcast.15, ...), custom_call_target="tpu_custom_call" | custom-call | tf_op jit(solution)/shard_map/band/pallas_call | solution.py:274
  138.8 13.4 %all-to-all-done.3.refs_9_ = bf16[64,136,128]{2,1,0:T(8,128)(2,1)S(1)} async-done(((bf16[64,136,128]{2,1,0:T(8,128)(2,1)}), bf16[64,136,128]{2,1,0:T(8,128)(2,1)S(1)}, u32[]{:S(2)}, u32[]{:S(2)}) %all-to-all-start.3) | async-done | bytes 2228256 | tf_op jit(solution)/shard_map/all_to_all | solution.py:496
  152.2 10.7 %finish.5 = (f32[64,16384]{1,0:T(8,128)}, f32[128,1,256]{2,1,0:T(1,128)}) custom-call(s32[1]{0:T(128)} %bitcast.first_ref.refs_0_, s32[1]{0:T(128)S(6)} %copy.25.count_ref.refs_1_, s32[1,512]{1,0:T(1,128)S(1)} %copy-done.2, s32[1,512]{1,0:T(1,128)S(1)} %copy-done.3, s32[64,128]{1,0:T(8,128)S(1)} %bitcast.20, s32[64,1]{1,0:T(8,128)S(1)} %copy.24.refs_2_.refs_5_.refs_3_, ...), custom_call_target="tpu_custom_call" | custom-call | tf_op jit(solution)/shard_map/finish/pallas_call | solution.py:438
  162.9 9.1 %all-to-all-start.4 = ((f32[128,1,256]{2,1,0:T(1,128)}), f32[128,1,256]{2,1,0:T(1,128)S(1)}, u32[]{:S(2)}, u32[]{:S(2)}) async-start(f32[128,1,256]{2,1,0:T(1,128)} %get-tuple-element.48), calls=%async_computation.4 | async-start | bytes 262144 | tf_op jit(solution)/shard_map/all_to_all | solution.py:510
  172.0 9.8 %all-to-all-done.4.got_ref = f32[128,1,256]{2,1,0:T(1,128)S(1)} async-done(((f32[128,1,256]{2,1,0:T(1,128)}), f32[128,1,256]{2,1,0:T(1,128)S(1)}, u32[]{:S(2)}, u32[]{:S(2)}) %all-to-all-start.4) | async-done | bytes 131104 | tf_op jit(solution)/shard_map/all_to_all | solution.py:510
  (19 shorter events, 4.5 us)
Async XLA Ops:
  2.7 20.3 %all-to-all-start = ((s32[64,1,128]{2,1,0:T(1,128)}), s32[64,1,128]{2,1,0:T(1,128)S(1)}, u32[]{:S(2)}, u32[]{:S(2)}) async-start(s32[64,1,128]{2,1,0:T(1,128)} %bitcast.21), calls=%async_computation | async-start | bytes 65536 | tf_op jit(solution)/shard_map/all_to_all | solution.py:489
  14.7 0.8 copy-start
  23.0 11.5 %copy-start.4 = (s32[64]{0:T(128)S(1)}, s32[64]{0:T(128)}, u32[]{:S(2)}) copy-start(s32[64]{0:T(128)} %param.14) | copy-start | bytes 772
  23.0 11.6 %copy-start.1 = (s32[16384]{0:T(1024)S(1)}, s32[16384]{0:T(1024)}, u32[]{:S(2)}) copy-start(s32[16384]{0:T(1024)} %param.15) | copy-start | bytes 196612
  25.6 33.1 %all-to-all-start.1 = ((bf16[64,136,128]{2,1,0:T(8,128)(2,1)}), bf16[64,136,128]{2,1,0:T(8,128)(2,1)S(1)}, u32[]{:S(2)}, u32[]{:S(2)}) async-start(bf16[64,136,128]{2,1,0:T(8,128)(2,1)} %pack.1), calls=%async_computation.1 | async-start | bytes 4456448 | tf_op jit(solution)/shard_map/all_to_all | solution.py:496
  30.3 13.8 %collective-permute-start = (bf16[64,128]{1,0:T(8,128)(2,1)S(1)}, bf16[64,128]{1,0:T(8,128)(2,1)S(1)}, u32[]{:S(2)}, u32[]{:S(2)}) collective-permute-start(bf16[64,128]{1,0:T(8,128)(2,1)S(1)} %get-tuple-element.31), channel_id=1, source_target_pairs={{0,2},{2,4},{4,6},{6,8},{8,10},{10,12},{12,14},{14,16},{16,18},{18... | collective-permute-start | bytes 49160 | tf_op jit(solution)/shard_map/ppermute | solution.py:497
  33.2 11.9 %collective-permute-start.1 = (bf16[64,128]{1,0:T(8,128)(2,1)S(1)}, bf16[64,128]{1,0:T(8,128)(2,1)S(1)}, u32[]{:S(2)}, u32[]{:S(2)}) collective-permute-start(bf16[64,128]{1,0:T(8,128)(2,1)S(1)} %get-tuple-element.32), channel_id=1, source_target_pairs={{2,0},{4,2},{6,4},{8,6},{10,8},{12,10},{14,12},{16,14},{18,16},{20... | collective-permute-start | bytes 49160 | tf_op jit(solution)/shard_map/ppermute | solution.py:498
  34.6 24.0 %copy-start.2 = (s32[1,512]{1,0:T(1,128)S(1)}, s32[1,512]{1,0:T(1,128)}, u32[]{:S(2)}) copy-start(s32[1,512]{1,0:T(1,128)} %get-tuple-element.28.refs_2_) | copy-start | bytes 6148
  34.6 24.0 %copy-start.3 = (s32[1,512]{1,0:T(1,128)S(1)}, s32[1,512]{1,0:T(1,128)}, u32[]{:S(2)}) copy-start(s32[1,512]{1,0:T(1,128)} %get-tuple-element.29.refs_3_) | copy-start | bytes 6148
  68.4 37.0 %all-to-all-start.2 = ((bf16[64,136,128]{2,1,0:T(8,128)(2,1)}), bf16[64,136,128]{2,1,0:T(8,128)(2,1)S(1)}, u32[]{:S(2)}, u32[]{:S(2)}) async-start(bf16[64,136,128]{2,1,0:T(8,128)(2,1)} %get-tuple-element.37), calls=%async_computation.2 | async-start | bytes 4456448 | tf_op jit(solution)/shard_map/all_to_all | solution.py:496
  77.1 14.7 %collective-permute-start.2 = (bf16[64,128]{1,0:T(8,128)(2,1)S(1)}, bf16[64,128]{1,0:T(8,128)(2,1)S(1)}, u32[]{:S(2)}, u32[]{:S(2)}) collective-permute-start(bf16[64,128]{1,0:T(8,128)(2,1)S(1)} %get-tuple-element.35), channel_id=1, source_target_pairs={{0,2},{2,4},{4,6},{6,8},{8,10},{10,12},{12,14},{14,16},{16,18},{18... | collective-permute-start | bytes 49160 | tf_op jit(solution)/shard_map/ppermute | solution.py:497
  80.0 11.9 %collective-permute-start.3 = (bf16[64,128]{1,0:T(8,128)(2,1)S(1)}, bf16[64,128]{1,0:T(8,128)(2,1)S(1)}, u32[]{:S(2)}, u32[]{:S(2)}) collective-permute-start(bf16[64,128]{1,0:T(8,128)(2,1)S(1)} %get-tuple-element.36), channel_id=1, source_target_pairs={{2,0},{4,2},{6,4},{8,6},{10,8},{12,10},{14,12},{16,14},{18,16},{20... | collective-permute-start | bytes 49160 | tf_op jit(solution)/shard_map/ppermute | solution.py:498
  115.2 37.0 %all-to-all-start.3 = ((bf16[64,136,128]{2,1,0:T(8,128)(2,1)}), bf16[64,136,128]{2,1,0:T(8,128)(2,1)S(1)}, u32[]{:S(2)}, u32[]{:S(2)}) async-start(bf16[64,136,128]{2,1,0:T(8,128)(2,1)} %get-tuple-element.42), calls=%async_computation.3 | async-start | bytes 4456448 | tf_op jit(solution)/shard_map/all_to_all | solution.py:496
  123.9 14.5 %collective-permute-start.4 = (bf16[64,128]{1,0:T(8,128)(2,1)S(1)}, bf16[64,128]{1,0:T(8,128)(2,1)S(1)}, u32[]{:S(2)}, u32[]{:S(2)}) collective-permute-start(bf16[64,128]{1,0:T(8,128)(2,1)S(1)} %get-tuple-element.40), channel_id=1, source_target_pairs={{0,2},{2,4},{4,6},{6,8},{8,10},{10,12},{12,14},{14,16},{16,18},{18... | collective-permute-start | bytes 49160 | tf_op jit(solution)/shard_map/ppermute | solution.py:497
  126.9 12.0 %collective-permute-start.5 = (bf16[64,128]{1,0:T(8,128)(2,1)S(1)}, bf16[64,128]{1,0:T(8,128)(2,1)S(1)}, u32[]{:S(2)}, u32[]{:S(2)}) collective-permute-start(bf16[64,128]{1,0:T(8,128)(2,1)S(1)} %get-tuple-element.41), channel_id=1, source_target_pairs={{2,0},{4,2},{6,4},{8,6},{10,8},{12,10},{14,12},{16,14},{18,16},{20... | collective-permute-start | bytes 49160 | tf_op jit(solution)/shard_map/ppermute | solution.py:498
  162.9 18.9 %all-to-all-start.4 = ((f32[128,1,256]{2,1,0:T(1,128)}), f32[128,1,256]{2,1,0:T(1,128)S(1)}, u32[]{:S(2)}, u32[]{:S(2)}) async-start(f32[128,1,256]{2,1,0:T(1,128)} %get-tuple-element.48), calls=%async_computation.4 | async-start | bytes 262144 | tf_op jit(solution)/shard_map/all_to_all | solution.py:510

commit v5 on v4

--- a/solution.py
+++ b/solution.py
@@ -156,7 +156,7 @@
 
     def one(p, carry):
         for k in range(CAP):
-            message[p, k * seeds : (k + 1) * seeds, :] = source[wanted[p, k]]
+            message[p, k * seeds : (k + 1) * seeds, :] = source[wanted(p, k)]
         message[p, CAP * seeds :, :] = slab
         return carry
 
@@ -168,7 +168,7 @@
 
 
 def pack_kernel(wanted_ref, source_ref, slab_ref, out_hbm, message, sem):
-    pack(wanted_ref, source_ref, slab_ref[...], message, out_hbm, sem)
+    pack(lambda p, k: wanted_ref[p, k], source_ref, slab_ref[...], message, out_hbm, sem)
 
 
 def pack_first(wanted, source, slab, peers):
@@ -318,6 +318,14 @@
         at = pl.ds(g * UNROLL, UNROLL)
         return pltpu.make_async_copy(tiles_hbm.at[at], tiles.at[at], tile_sem.at[g])
 
+    def part_loads(c):
+        at = pl.ds(c * span, span)
+        loads = [pltpu.make_async_copy(banded_hbm.at[at], banded.at[at], base_sem.at[c])]
+        if last:
+            cols = pl.ds(c * span * width, span * width)
+            loads.append(pltpu.make_async_copy(rank_hbm.at[:, cols], rank.at[:, cols], rank_sem.at[c]))
+        return loads
+
     def rank_store(c):
         cols = pl.ds(c * span * width, span * width)
         return pltpu.make_async_copy(rank.at[:, cols], next_hbm.at[:, cols], out_sem.at[c])
@@ -329,13 +337,11 @@
         def _():
             tile_copy(g).start()
 
-    loads = [pltpu.make_async_copy(banded_hbm, banded, base_sem)]
-    if last:
-        loads.append(pltpu.make_async_copy(rank_hbm, rank, rank_sem))
-    for load in loads:
-        load.start()
     for k in range(2):
         edge_copy(k).start()
+    for c in range(parts):
+        for load in part_loads(c):
+            load.start()
     mass_row = jnp.sum(jnp.sum(fetched[:, CAP * seeds :, :].astype(F32), axis=0), axis=0, keepdims=True)
     share = jnp.broadcast_to(DAMP * (to_column(mass_row, seeds) / vertices), (seeds, width))
     zero = jnp.zeros((seeds, width), BF16)
@@ -377,9 +383,6 @@
         edge_copy(k).wait()
     acc[0] = acc[0] + dot_nt(left_ref[...], edges[0])
     acc[blocks - 1] = acc[blocks - 1] + dot_nt(right_ref[...], edges[1])
-    for load in loads:
-        load.wait()
-
     if last:
         away = from_seed(seed_ref, first_ref, width)
 
@@ -400,6 +403,8 @@
     nothing = jnp.zeros((seeds, width), F32)
     carry = (nothing, nothing) if last else nothing
     for c in range(parts):
+        for load in part_loads(c):
+            load.wait()
         carry = lax.fori_loop(c * span, (c + 1) * span, update, carry, unroll=8)
         rank_store(c).start()
     if last:
@@ -409,7 +414,7 @@
         )
         line_ref[...] = jnp.broadcast_to(line[:, None, :], line_ref.shape)
     else:
-        pack(wanted_ref, source, mass_slab(carry), message, message_hbm, send_sem)
+        pack(lambda p, k: wanted_ref[k, p], source, mass_slab(carry), message, message_hbm, send_sem)
         head_ref[...] = source[0]
         tail_ref[...] = source[blocks - 1]
     for c in range(parts):
@@ -425,7 +430,7 @@
     if last:
         out_shape = (in_hbm(shape, F32), shaped((devices, 1, 256), F32))
         out_specs = (hbm(), vmem())
-        scratch = [pltpu.SemaphoreType.DMA]
+        scratch = [pltpu.SemaphoreType.DMA((8,))]
     else:
         edge = shaped((seeds, width), BF16)
         out_shape = (in_hbm(shape, F32), edge, edge, in_hbm(fetched.shape, BF16))
@@ -452,7 +457,7 @@
             VMEM((2, width, width), BF16),
             pltpu.SemaphoreType.DMA((2,)),
             pltpu.SemaphoreType.DMA((tiles.shape[0] // UNROLL,)),
-            pltpu.SemaphoreType.DMA,
+            pltpu.SemaphoreType.DMA((8,)),
             pltpu.SemaphoreType.DMA((8,)),
         ],
         compiler_params=PARAMS,
@@ -489,6 +494,7 @@
     wanted = lax.all_to_all(request, "dom", split_axis=0, concat_axis=0, tiled=True)
     source, slab, head, tail = prep(rank_in, dangling, blocks)
     message = pack_first(wanted, source, slab, peers)
+    asked = jnp.transpose(wanted[:, :CAP])
     old, rank = None, rank_in
     gaps = []
     for iteration in range(ITERS):
@@ -499,7 +505,7 @@
         gap_at = (iteration - 1) * seeds if iteration > 0 else None
         banded, *gap = band(gap_at, first, rank, old, band_tiles, dangling, seeds_at)
         gaps += gap
-        scalars = (first, tile_count, slot, target, wanted)
+        scalars = (first, tile_count, slot, target, asked)
         vectors = (seeds_at, dangling, left, right, fetched)
         arrays = (banded, off_tiles, band_tiles)
         if last:

time: 183 us -> 182 us (level)
  starting transfers between devices: 56 us -> 52.1 us
  Pallas kernels: 67.3 us -> 70.6 us
    pallas_call x3, Pallas kernels: 30.2 us -> 33.6 us  [finish(): pl.pallas_call(functools.partial(finish_kernel, last, vertices), out_shap...]
    all_to_all x3, starting transfers between devices: 22.2 us -> 19.1 us  [on_device(): lax.all_to_all(message, 'dom', split_axis=0, concat_axis=0, tiled=True)]
where the time goes in v5:
time: 182 us
  Pallas kernels  70.6 us (39%)
  waiting for transfers between devices  56.7 us (31%)
  starting transfers between devices  52.1 us (29%)
    all_to_all x3, waiting for transfers between devices, on_device(): lax.all_to_all(message, 'dom', split_axis=0, concat_axis=0, tiled=True)  40.5 us
    pallas_call x3, Pallas kernels, finish(): pl.pallas_call(functools.partial(finish_kernel, last, vertices), out_shap...  33.6 us
    pallas_call x3, Pallas kernels, band(): pl.pallas_call(functools.partial(band_kernel, gap_at), out_shape=tuple(ou...  30 us
    all_to_all x3, starting transfers between devices, on_device(): lax.all_to_all(message, 'dom', split_axis=0, concat_axis=0, tiled=True)  19.1 us
    all_to_all x1, starting transfers between devices, on_device(): lax.all_to_all(request, 'dom', split_axis=0, concat_axis=0, tiled=True)  12 us
    all_to_all x1, waiting for transfers between devices, on_device(): lax.all_to_all(line, ('dom', 'seed'), split_axis=0, concat_axis=0, tiled=...  9.82 us
    ppermute x3, starting transfers between devices, on_device(): left = lax.ppermute(tail, 'dom', [(i, i + 1) for i in range(peers - 1)])  8.75 us
    all_to_all x1, starting transfers between devices, on_device(): lax.all_to_all(line, ('dom', 'seed'), split_axis=0, concat_axis=0, tiled=...  8.23 us
  transfers between devices with their start and end apart: 11, of which 8 were waited for; matrix products, arithmetic and copies ran while one was open for 0% of the time, Pallas kernels for 18%

profile of v5, /device:TPU:1, one launch (start us, length us, event | category | flops | bytes accessed | tf_op | source)
XLA Modules:
  0.0 182.0 jit_solution(17941201064392262707)
XLA Ops:
  1.3 1.4 plan.1
  2.7 12.0 %all-to-all-start = ((s32[64,1,128]{2,1,0:T(1,128)}), s32[64,1,128]{2,1,0:T(1,128)S(1)}, u32[]{:S(2)}, u32[]{:S(2)}) async-start(s32[64,1,128]{2,1,0:T(1,128)} %bitcast.24), calls=%async_computation | async-start | bytes 65536 | tf_op jit(solution)/shard_map/all_to_all | solution.py:494
  15.5 2.4 %prep.1 = (bf16[128,64,128]{2,1,0:T(8,128)(2,1)S(1)}, bf16[8,128]{1,0:T(8,128)(2,1)S(1)}, bf16[64,128]{1,0:T(8,128)(2,1)S(1)}, bf16[64,128]{1,0:T(8,128)(2,1)S(1)}) custom-call(f32[64,16384]{1,0:T(8,128)} %refs_0_.3, s32[128,128]{1,0:T(8,128)S(1)} %bitcast.15), custom_call_target="tpu_custom_call" | custom-call | tf_op jit(solution)/shard_map/prep/pallas_call | solution.py:136
  17.9 5.1 %all-to-all-done = s32[64,1,128]{2,1,0:T(1,128)S(1)} async-done(((s32[64,1,128]{2,1,0:T(1,128)}), s32[64,1,128]{2,1,0:T(1,128)S(1)}, u32[]{:S(2)}, u32[]{:S(2)}) %all-to-all-start) | async-done | bytes 32800 | tf_op jit(solution)/shard_map/all_to_all | solution.py:494
  23.0 2.5 %pack.1 = bf16[64,136,128]{2,1,0:T(8,128)(2,1)} custom-call(s32[64,128]{1,0:T(8,128)S(1)} %bitcast.22, bf16[128,64,128]{2,1,0:T(8,128)(2,1)S(1)} %get-tuple-element.33.source_ref, bf16[8,128]{1,0:T(8,128)(2,1)S(1)} %get-tuple-element.34.slab_ref), custom_call_target="tpu_custom_call" | custom-call | tf_op jit(solution)/shard_map/pack/pallas_call | solution.py:177
  25.6 4.7 %all-to-all-start.1 = ((bf16[64,136,128]{2,1,0:T(8,128)(2,1)}), bf16[64,136,128]{2,1,0:T(8,128)(2,1)S(1)}, u32[]{:S(2)}, u32[]{:S(2)}) async-start(bf16[64,136,128]{2,1,0:T(8,128)(2,1)} %pack.1), calls=%async_computation.1 | async-start | bytes 4456448 | tf_op jit(solution)/shard_map/all_to_all | solution.py:502
  30.3 2.9 %collective-permute-start = (bf16[64,128]{1,0:T(8,128)(2,1)S(1)}, bf16[64,128]{1,0:T(8,128)(2,1)S(1)}, u32[]{:S(2)}, u32[]{:S(2)}) collective-permute-start(bf16[64,128]{1,0:T(8,128)(2,1)S(1)} %get-tuple-element.31), channel_id=1, source_target_pairs={{0,2},{2,4},{4,6},{6,8},{8,10},{10,12},{12,14},{14,16},{16,18},{18... | collective-permute-start | bytes 49160 | tf_op jit(solution)/shard_map/ppermute | solution.py:503
  33.2 1.3 collective-permute-start.1
  34.7 9.5 %band.3.refs_10_ = f32[128,64,128]{2,1,0:T(8,128)} custom-call(s32[1]{0:T(128)} %bitcast.first_ref.refs_0_, f32[64,16384]{1,0:T(8,128)} %refs_0_.3, bf16[128,3,128,128]{3,2,1,0:T(8,128)(2,1)} %refs_12_.5, s32[128,128]{1,0:T(8,128)S(1)} %bitcast.16, s32[64,1]{1,0:T(8,128)S(1)} %copy.28.refs_2_.refs_5_.refs_3_), custom_call_target="tpu_custom_call" | custom-call | tf_op jit(solution)/shard_map/band/pallas_call | solution.py:274
  45.1 13.5 %all-to-all-done.1.refs_9_ = bf16[64,136,128]{2,1,0:T(8,128)(2,1)S(1)} async-done(((bf16[64,136,128]{2,1,0:T(8,128)(2,1)}), bf16[64,136,128]{2,1,0:T(8,128)(2,1)S(1)}, u32[]{:S(2)}, u32[]{:S(2)}) %all-to-all-start.1) | async-done | bytes 2228256 | tf_op jit(solution)/shard_map/all_to_all | solution.py:502
  58.6 10.9 %finish.3 = (f32[64,16384]{1,0:T(8,128)}, bf16[64,128]{1,0:T(8,128)(2,1)S(1)}, bf16[64,128]{1,0:T(8,128)(2,1)S(1)}, bf16[64,136,128]{2,1,0:T(8,128)(2,1)}) custom-call(s32[1]{0:T(128)} %bitcast.first_ref.refs_0_, s32[1]{0:T(128)S(6)} %copy.30.count_ref.refs_1_, s32[1,512]{1,0:T(1,128)S(1)} %copy-done.2, s32[1,512]{1,0:T(1,128)S(1)} %copy-done.3, ...), custom_call_target="tpu_custom_call" | custom-call | tf_op jit(solution)/shard_map/finish/pallas_call | solution.py:443
  69.5 7.2 %all-to-all-start.2 = ((bf16[64,136,128]{2,1,0:T(8,128)(2,1)}), bf16[64,136,128]{2,1,0:T(8,128)(2,1)S(1)}, u32[]{:S(2)}, u32[]{:S(2)}) async-start(bf16[64,136,128]{2,1,0:T(8,128)(2,1)} %get-tuple-element.37), calls=%async_computation.2 | async-start | bytes 4456448 | tf_op jit(solution)/shard_map/all_to_all | solution.py:502
  76.7 2.9 %collective-permute-start.2 = (bf16[64,128]{1,0:T(8,128)(2,1)S(1)}, bf16[64,128]{1,0:T(8,128)(2,1)S(1)}, u32[]{:S(2)}, u32[]{:S(2)}) collective-permute-start(bf16[64,128]{1,0:T(8,128)(2,1)S(1)} %get-tuple-element.35), channel_id=1, source_target_pairs={{0,2},{2,4},{4,6},{6,8},{8,10},{10,12},{12,14},{14,16},{16,18},{18... | collective-permute-start | bytes 49160 | tf_op jit(solution)/shard_map/ppermute | solution.py:503
  79.6 1.5 collective-permute-start.3
  81.1 10.2 %band.4 = (f32[128,64,128]{2,1,0:T(8,128)}, f32[1,128]{1,0:T(1,128)S(1)}) custom-call(s32[1]{0:T(128)} %bitcast.first_ref.refs_0_, f32[64,16384]{1,0:T(8,128)} %get-tuple-element.38.rank_hbm.refs_0_, f32[64,16384]{1,0:T(8,128)} %refs_0_.3, bf16[128,3,128,128]{3,2,1,0:T(8,128)(2,1)} %refs_12_.5, s32[128,128]{1,0:T(8,128)S(1)} %bitcast.18, ...), custom_call_target="tpu_custom_call" | custom-call | tf_op jit(solution)/shard_map/band/pallas_call | solution.py:274
  91.5 13.5 %all-to-all-done.2.refs_9_ = bf16[64,136,128]{2,1,0:T(8,128)(2,1)S(1)} async-done(((bf16[64,136,128]{2,1,0:T(8,128)(2,1)}), bf16[64,136,128]{2,1,0:T(8,128)(2,1)S(1)}, u32[]{:S(2)}, u32[]{:S(2)}) %all-to-all-start.2) | async-done | bytes 2228256 | tf_op jit(solution)/shard_map/all_to_all | solution.py:502
  105.0 10.9 %finish.4 = (f32[64,16384]{1,0:T(8,128)}, bf16[64,128]{1,0:T(8,128)(2,1)S(1)}, bf16[64,128]{1,0:T(8,128)(2,1)S(1)}, bf16[64,136,128]{2,1,0:T(8,128)(2,1)}) custom-call(s32[1]{0:T(128)} %bitcast.first_ref.refs_0_, s32[1]{0:T(128)S(6)} %copy.30.count_ref.refs_1_, s32[1,512]{1,0:T(1,128)S(1)} %copy-done.2, s32[1,512]{1,0:T(1,128)S(1)} %copy-done.3, ...), custom_call_target="tpu_custom_call" | custom-call | tf_op jit(solution)/shard_map/finish/pallas_call | solution.py:443
  115.9 7.2 %all-to-all-start.3 = ((bf16[64,136,128]{2,1,0:T(8,128)(2,1)}), bf16[64,136,128]{2,1,0:T(8,128)(2,1)S(1)}, u32[]{:S(2)}, u32[]{:S(2)}) async-start(bf16[64,136,128]{2,1,0:T(8,128)(2,1)} %get-tuple-element.42), calls=%async_computation.3 | async-start | bytes 4456448 | tf_op jit(solution)/shard_map/all_to_all | solution.py:502
  123.1 2.9 %collective-permute-start.4 = (bf16[64,128]{1,0:T(8,128)(2,1)S(1)}, bf16[64,128]{1,0:T(8,128)(2,1)S(1)}, u32[]{:S(2)}, u32[]{:S(2)}) collective-permute-start(bf16[64,128]{1,0:T(8,128)(2,1)S(1)} %get-tuple-element.40), channel_id=1, source_target_pairs={{0,2},{2,4},{4,6},{6,8},{8,10},{10,12},{12,14},{14,16},{16,18},{18... | collective-permute-start | bytes 49160 | tf_op jit(solution)/shard_map/ppermute | solution.py:503
  127.3 10.3 %band.5 = (f32[128,64,128]{2,1,0:T(8,128)}, f32[1,128]{1,0:T(1,128)S(1)}) custom-call(s32[1]{0:T(128)} %bitcast.first_ref.refs_0_, f32[64,16384]{1,0:T(8,128)} %get-tuple-element.43.rank_hbm.refs_13_, f32[64,16384]{1,0:T(8,128)} %get-tuple-element.38.rank_hbm.refs_0_, bf16[128,3,128,128]{3,2,1,0:T(8,128)(2,1)} %refs_12_.5, s32[128,128]{1,0:T(8,128)S(1)} %bitcast.20, ...), custom_call_target="tpu_custom_call" | custom-call | tf_op jit(solution)/shard_map/band/pallas_call | solution.py:274
  137.9 13.5 %all-to-all-done.3.refs_9_ = bf16[64,136,128]{2,1,0:T(8,128)(2,1)S(1)} async-done(((bf16[64,136,128]{2,1,0:T(8,128)(2,1)}), bf16[64,136,128]{2,1,0:T(8,128)(2,1)S(1)}, u32[]{:S(2)}, u32[]{:S(2)}) %all-to-all-start.3) | async-done | bytes 2228256 | tf_op jit(solution)/shard_map/all_to_all | solution.py:502
  151.4 11.8 %finish.5 = (f32[64,16384]{1,0:T(8,128)}, f32[128,1,256]{2,1,0:T(1,128)}) custom-call(s32[1]{0:T(128)} %bitcast.first_ref.refs_0_, s32[1]{0:T(128)S(6)} %copy.30.count_ref.refs_1_, s32[1,512]{1,0:T(1,128)S(1)} %copy-done.2, s32[1,512]{1,0:T(1,128)S(1)} %copy-done.3, s32[2,64]{1,0:T(2,128)S(1)} %slice_bitcast_fusion.refs_4_, ...), custom_call_target="tpu_custom_call" | custom-call | tf_op jit(solution)/shard_map/finish/pallas_call | solution.py:443
  163.2 8.2 %all-to-all-start.4 = ((f32[128,1,256]{2,1,0:T(1,128)}), f32[128,1,256]{2,1,0:T(1,128)S(1)}, u32[]{:S(2)}, u32[]{:S(2)}) async-start(f32[128,1,256]{2,1,0:T(1,128)} %get-tuple-element.48), calls=%async_computation.4 | async-start | bytes 262144 | tf_op jit(solution)/shard_map/all_to_all | solution.py:516
  171.4 9.8 %all-to-all-done.4.got_ref = f32[128,1,256]{2,1,0:T(1,128)S(1)} async-done(((f32[128,1,256]{2,1,0:T(1,128)}), f32[128,1,256]{2,1,0:T(1,128)S(1)}, u32[]{:S(2)}, u32[]{:S(2)}) %all-to-all-start.4) | async-done | bytes 131104 | tf_op jit(solution)/shard_map/all_to_all | solution.py:516
  (21 shorter events, 4.4 us)
Async XLA Ops:
  2.7 20.3 %all-to-all-start = ((s32[64,1,128]{2,1,0:T(1,128)}), s32[64,1,128]{2,1,0:T(1,128)S(1)}, u32[]{:S(2)}, u32[]{:S(2)}) async-start(s32[64,1,128]{2,1,0:T(1,128)} %bitcast.24), calls=%async_computation | async-start | bytes 65536 | tf_op jit(solution)/shard_map/all_to_all | solution.py:494
  14.7 0.8 copy-start
  23.0 11.5 %copy-start.4 = (s32[64]{0:T(128)S(1)}, s32[64]{0:T(128)}, u32[]{:S(2)}) copy-start(s32[64]{0:T(128)} %param.14) | copy-start | bytes 772
  23.0 11.6 %copy-start.1 = (s32[16384]{0:T(1024)S(1)}, s32[16384]{0:T(1024)}, u32[]{:S(2)}) copy-start(s32[16384]{0:T(1024)} %param.15) | copy-start | bytes 196612
  25.6 33.1 %all-to-all-start.1 = ((bf16[64,136,128]{2,1,0:T(8,128)(2,1)}), bf16[64,136,128]{2,1,0:T(8,128)(2,1)S(1)}, u32[]{:S(2)}, u32[]{:S(2)}) async-start(bf16[64,136,128]{2,1,0:T(8,128)(2,1)} %pack.1), calls=%async_computation.1 | async-start | bytes 4456448 | tf_op jit(solution)/shard_map/all_to_all | solution.py:502
  30.3 13.9 %collective-permute-start = (bf16[64,128]{1,0:T(8,128)(2,1)S(1)}, bf16[64,128]{1,0:T(8,128)(2,1)S(1)}, u32[]{:S(2)}, u32[]{:S(2)}) collective-permute-start(bf16[64,128]{1,0:T(8,128)(2,1)S(1)} %get-tuple-element.31), channel_id=1, source_target_pairs={{0,2},{2,4},{4,6},{6,8},{8,10},{10,12},{12,14},{14,16},{16,18},{18... | collective-permute-start | bytes 49160 | tf_op jit(solution)/shard_map/ppermute | solution.py:503
  33.2 11.9 %collective-permute-start.1 = (bf16[64,128]{1,0:T(8,128)(2,1)S(1)}, bf16[64,128]{1,0:T(8,128)(2,1)S(1)}, u32[]{:S(2)}, u32[]{:S(2)}) collective-permute-start(bf16[64,128]{1,0:T(8,128)(2,1)S(1)} %get-tuple-element.32), channel_id=1, source_target_pairs={{2,0},{4,2},{6,4},{8,6},{10,8},{12,10},{14,12},{16,14},{18,16},{20... | collective-permute-start | bytes 49160 | tf_op jit(solution)/shard_map/ppermute | solution.py:504
  34.6 24.0 %copy-start.2 = (s32[1,512]{1,0:T(1,128)S(1)}, s32[1,512]{1,0:T(1,128)}, u32[]{:S(2)}) copy-start(s32[1,512]{1,0:T(1,128)} %get-tuple-element.28.refs_2_) | copy-start | bytes 6148
  34.6 24.0 %copy-start.3 = (s32[1,512]{1,0:T(1,128)S(1)}, s32[1,512]{1,0:T(1,128)}, u32[]{:S(2)}) copy-start(s32[1,512]{1,0:T(1,128)} %get-tuple-element.29.refs_3_) | copy-start | bytes 6148
  69.5 35.5 %all-to-all-start.2 = ((bf16[64,136,128]{2,1,0:T(8,128)(2,1)}), bf16[64,136,128]{2,1,0:T(8,128)(2,1)S(1)}, u32[]{:S(2)}, u32[]{:S(2)}) async-start(bf16[64,136,128]{2,1,0:T(8,128)(2,1)} %get-tuple-element.37), calls=%async_computation.2 | async-start | bytes 4456448 | tf_op jit(solution)/shard_map/all_to_all | solution.py:502
  76.7 14.7 %collective-permute-start.2 = (bf16[64,128]{1,0:T(8,128)(2,1)S(1)}, bf16[64,128]{1,0:T(8,128)(2,1)S(1)}, u32[]{:S(2)}, u32[]{:S(2)}) collective-permute-start(bf16[64,128]{1,0:T(8,128)(2,1)S(1)} %get-tuple-element.35), channel_id=1, source_target_pairs={{0,2},{2,4},{4,6},{6,8},{8,10},{10,12},{12,14},{14,16},{16,18},{18... | collective-permute-start | bytes 49160 | tf_op jit(solution)/shard_map/ppermute | solution.py:503
  79.6 11.9 %collective-permute-start.3 = (bf16[64,128]{1,0:T(8,128)(2,1)S(1)}, bf16[64,128]{1,0:T(8,128)(2,1)S(1)}, u32[]{:S(2)}, u32[]{:S(2)}) collective-permute-start(bf16[64,128]{1,0:T(8,128)(2,1)S(1)} %get-tuple-element.36), channel_id=1, source_target_pairs={{2,0},{4,2},{6,4},{8,6},{10,8},{12,10},{14,12},{16,14},{18,16},{20... | collective-permute-start | bytes 49160 | tf_op jit(solution)/shard_map/ppermute | solution.py:504
  115.9 35.5 %all-to-all-start.3 = ((bf16[64,136,128]{2,1,0:T(8,128)(2,1)}), bf16[64,136,128]{2,1,0:T(8,128)(2,1)S(1)}, u32[]{:S(2)}, u32[]{:S(2)}) async-start(bf16[64,136,128]{2,1,0:T(8,128)(2,1)} %get-tuple-element.42), calls=%async_computation.3 | async-start | bytes 4456448 | tf_op jit(solution)/shard_map/all_to_all | solution.py:502
  123.1 14.5 %collective-permute-start.4 = (bf16[64,128]{1,0:T(8,128)(2,1)S(1)}, bf16[64,128]{1,0:T(8,128)(2,1)S(1)}, u32[]{:S(2)}, u32[]{:S(2)}) collective-permute-start(bf16[64,128]{1,0:T(8,128)(2,1)S(1)} %get-tuple-element.40), channel_id=1, source_target_pairs={{0,2},{2,4},{4,6},{6,8},{8,10},{10,12},{12,14},{14,16},{16,18},{18... | collective-permute-start | bytes 49160 | tf_op jit(solution)/shard_map/ppermute | solution.py:503
  126.0 11.9 %collective-permute-start.5 = (bf16[64,128]{1,0:T(8,128)(2,1)S(1)}, bf16[64,128]{1,0:T(8,128)(2,1)S(1)}, u32[]{:S(2)}, u32[]{:S(2)}) collective-permute-start(bf16[64,128]{1,0:T(8,128)(2,1)S(1)} %get-tuple-element.41), channel_id=1, source_target_pairs={{2,0},{4,2},{6,4},{8,6},{10,8},{12,10},{14,12},{16,14},{18,16},{20... | collective-permute-start | bytes 49160 | tf_op jit(solution)/shard_map/ppermute | solution.py:504
  163.2 18.1 %all-to-all-start.4 = ((f32[128,1,256]{2,1,0:T(1,128)}), f32[128,1,256]{2,1,0:T(1,128)S(1)}, u32[]{:S(2)}, u32[]{:S(2)}) async-start(f32[128,1,256]{2,1,0:T(1,128)} %get-tuple-element.48), calls=%async_computation.4 | async-start | bytes 262144 | tf_op jit(solution)/shard_map/all_to_all | solution.py:516

commit v6 on v5

--- a/solution.py
+++ b/solution.py
@@ -36,6 +36,10 @@
 
 def in_hbm(shape, dtype):
     return pltpu.HBM(shape, dtype)
+
+
+def on_chip(shape, dtype):
+    return pltpu.VMEM(shape, dtype)
 
 
 def off_chip(x):
@@ -185,6 +189,9 @@
     )(wanted, source, slab)
 
 
+KEPT = 32
+
+
 def from_seed(seed_ref, first_ref, width):
     seeds = seed_ref.shape[0]
     here = jnp.broadcast_to(seed_ref[...] - first_ref[0], (seeds, width))
@@ -194,8 +201,8 @@
 def band_kernel(gap_at, first_ref, rank_hbm, *refs):
     refs = list(refs)
     old_hbm = None if gap_at is None else refs.pop(0)
-    tiles_hbm, dangling_ref, seed_ref, out_hbm = refs[:4]
-    refs = refs[4:]
+    tiles_hbm, dangling_ref, seed_ref, out_hbm, kept_ref = refs[:5]
+    refs = refs[5:]
     gap_ref = None if gap_at is None else refs.pop(0)
     rank, source, tiles, banded, sem, rank_sem, out_sem = refs[:7]
     blocks, seeds, width = banded.shape
@@ -208,7 +215,7 @@
 
     def flush(c):
         span = pl.ds(c * per, per)
-        return pltpu.make_async_copy(banded.at[span], out_hbm.at[span], out_sem.at[c])
+        return pltpu.make_async_copy(banded.at[span], out_hbm.at[pl.ds(c * per - KEPT, per)], out_sem.at[c])
 
     def fetch_rank(c):
         cols = pl.ds(c * per * width, per * width)
@@ -251,11 +258,13 @@
             after = source[b + 1] if b + 1 < blocks else zero
             x = jnp.concatenate([before, source[b], after], axis=1)
             w = jnp.concatenate([tiles[b, 0], tiles[b, 1], tiles[b, 2]], axis=1)
-            banded[b] = DAMP * dot_nt(x, w) + jnp.where(away == b * width, 1.0 - DAMP, 0.0)
-        flush(c).start()
+            into = kept_ref if b < KEPT else banded
+            into[b] = DAMP * dot_nt(x, w) + jnp.where(away == b * width, 1.0 - DAMP, 0.0)
+        if c * per >= KEPT:
+            flush(c).start()
     if gap_at is not None:
         gap_ref[...] = to_row(jnp.sum(gap, axis=1, keepdims=True), gap_at)
-    for c in range(chunks):
+    for c in range(KEPT // per, chunks):
         flush(c).wait()
 
 
@@ -264,8 +273,8 @@
     seeds = rank.shape[0]
     shape = (blocks, seeds, width)
     ranks = [rank] if gap_at is None else [rank, old]
-    out_shape = [in_hbm(shape, F32)]
-    out_specs = [hbm()]
+    out_shape = [in_hbm((blocks - KEPT, seeds, width), F32), on_chip((KEPT, seeds, width), F32)]
+    out_specs = [hbm(), vmem()]
     extra = []
     if gap_at is not None:
         out_shape.append(shaped((1, 128), F32))
@@ -297,16 +306,17 @@
 
 def finish_kernel(last, vertices, *refs):
     (first_ref, count_ref, slot_ref, target_ref, wanted_ref) = refs[:5]
-    (seed_ref, dangling_ref, left_ref, right_ref, fetched) = refs[5:10]
-    banded_hbm, tiles_hbm, band_hbm = refs[10:13]
+    (seed_ref, dangling_ref, left_ref, right_ref, kept_ref, fetched) = refs[5:11]
+    banded_hbm, tiles_hbm, band_hbm = refs[11:14]
     if last:
-        rank_hbm, gap_one_ref, gap_two_ref, next_hbm, line_ref, rank_sem = refs[13:19]
-        scratch = refs[19:]
+        rank_hbm, gap_one_ref, gap_two_ref, next_hbm, line_ref, rank_sem = refs[14:20]
+        scratch = refs[20:]
     else:
-        next_hbm, head_ref, tail_ref, message_hbm, source, message, send_sem = refs[13:20]
-        scratch = refs[20:]
+        next_hbm, head_ref, tail_ref, message_hbm, source, message, send_sem = refs[14:21]
+        scratch = refs[21:]
     tiles, acc, banded, rank, edges, edge_sem, tile_sem, base_sem, out_sem = scratch
-    blocks, seeds, width = banded.shape
+    seeds, width = banded.shape[1:]
+    blocks = banded.shape[0] + KEPT
     parts = out_sem.shape[0]
     span = blocks // parts
 
@@ -319,8 +329,10 @@
         return pltpu.make_async_copy(tiles_hbm.at[at], tiles.at[at], tile_sem.at[g])
 
     def part_loads(c):
-        at = pl.ds(c * span, span)
-        loads = [pltpu.make_async_copy(banded_hbm.at[at], banded.at[at], base_sem.at[c])]
+        loads = []
+        if c * span >= KEPT:
+            at = pl.ds(c * span - KEPT, span)
+            loads.append(pltpu.make_async_copy(banded_hbm.at[at], banded.at[at], base_sem.at[c]))
         if last:
             cols = pl.ds(c * span * width, span * width)
             loads.append(pltpu.make_async_copy(rank_hbm.at[:, cols], rank.at[:, cols], rank_sem.at[c]))
@@ -386,9 +398,10 @@
     if last:
         away = from_seed(seed_ref, first_ref, width)
 
-    def update(b, carry):
+    def update(kept_here, b, carry):
         cols = pl.ds(pl.multiple_of(b * width, width), width)
-        new = banded[b] + (DAMP * acc[b] + share)
+        base = kept_ref[b] if kept_here else banded[b - KEPT]
+        new = base + (DAMP * acc[b] + share)
         if last:
             gap, own = carry
             gap = gap + jnp.abs(new - rank[:, cols])
@@ -405,7 +418,9 @@
     for c in range(parts):
         for load in part_loads(c):
             load.wait()
-        carry = lax.fori_loop(c * span, (c + 1) * span, update, carry, unroll=8)
+        carry = lax.fori_loop(
+            c * span, (c + 1) * span, functools.partial(update, c * span < KEPT), carry, unroll=8
+        )
         rank_store(c).start()
     if last:
         gap, own = (jnp.sum(x, axis=1, keepdims=True) for x in carry)
@@ -424,7 +439,8 @@
 def finish(last, vertices, devices, scalars, vectors, arrays, old=(), gaps=()):
     fetched = vectors[-1]
     banded, tiles, _ = arrays
-    blocks, seeds, width = banded.shape
+    seeds, width = banded.shape[1:]
+    blocks = banded.shape[0] + KEPT
     shape = (seeds, blocks * width)
     operands = tuple(scalars) + tuple(vectors) + tuple(off_chip(x) for x in tuple(arrays) + tuple(old)) + tuple(gaps)
     if last:
@@ -452,7 +468,7 @@
         + [
             VMEM(tiles.shape, BF16),
             VMEM((blocks + 1, seeds, width), F32),
-            VMEM((blocks, seeds, width), F32),
+            VMEM(banded.shape, F32),
             VMEM(shape, F32),
             VMEM((2, width, width), BF16),
             pltpu.SemaphoreType.DMA((2,)),
@@ -503,10 +519,10 @@
         left = lax.ppermute(tail, "dom", [(i, i + 1) for i in range(peers - 1)])
         right = lax.ppermute(head, "dom", [(i + 1, i) for i in range(peers - 1)])
         gap_at = (iteration - 1) * seeds if iteration > 0 else None
-        banded, *gap = band(gap_at, first, rank, old, band_tiles, dangling, seeds_at)
+        banded, kept, *gap = band(gap_at, first, rank, old, band_tiles, dangling, seeds_at)
         gaps += gap
         scalars = (first, tile_count, slot, target, asked)
-        vectors = (seeds_at, dangling, left, right, fetched)
+        vectors = (seeds_at, dangling, left, right, kept, fetched)
         arrays = (banded, off_tiles, band_tiles)
         if last:
             rank, line = finish(last, vertices, devices, scalars, vectors, arrays, (rank,), gaps)

time: 182 us -> 181 us (level)
  Pallas kernels: 70.6 us -> 67.9 us
  starting transfers between devices: 52.1 us -> 54.3 us
    pallas_call x3, Pallas kernels: 33.6 us -> 30.9 us  [finish(): pl.pallas_call(functools.partial(finish_kernel, last, vertices), out_shap...]
  transfers between devices with their start and end apart: 11 -> 11, of which waited for: 8 -> 6; matrix products, arithmetic and copies ran while one was open for 0% -> 0% of each run, Pallas kernels for 18% -> 18%
where the time goes in v6:
time: 181 us; the launch traced here: 180 us
  Pallas kernels  67.9 us (38%)
  waiting for transfers between devices  55.5 us (31%)
  starting transfers between devices  54.3 us (30%)
    all_to_all x3, waiting for transfers between devices, on_device(): lax.all_to_all(message, 'dom', split_axis=0, concat_axis=0, tiled=True)  39.8 us
    pallas_call x3, Pallas kernels, finish(): pl.pallas_call(functools.partial(finish_kernel, last, vertices), out_shap...  30.9 us
    pallas_call x3, Pallas kernels, band(): pl.pallas_call(functools.partial(band_kernel, gap_at), out_shape=tuple(ou...  30 us
    all_to_all x3, starting transfers between devices, on_device(): lax.all_to_all(message, 'dom', split_axis=0, concat_axis=0, tiled=True)  19.7 us
    all_to_all x1, starting transfers between devices, on_device(): lax.all_to_all(request, 'dom', split_axis=0, concat_axis=0, tiled=True)  12 us
    all_to_all x1, starting transfers between devices, on_device(): lax.all_to_all(line, ('dom', 'seed'), split_axis=0, concat_axis=0, tiled=...  9.85 us
    all_to_all x1, waiting for transfers between devices, on_device(): lax.all_to_all(line, ('dom', 'seed'), split_axis=0, concat_axis=0, tiled=...  9.82 us
    ppermute x3, starting transfers between devices, on_device(): left = lax.ppermute(tail, 'dom', [(i, i + 1) for i in range(peers - 1)])  8.74 us
  transfers between devices with their start and end apart: 11, of which 6 were waited for; matrix products, arithmetic and copies ran while one was open for 0% of the time, Pallas kernels for 18%

profile of v6, /device:TPU:1, one launch (start us, length us, event | category | flops | bytes accessed | tf_op | source)
XLA Modules:
  0.0 180.3 jit_solution(8418955856415247687)
XLA Ops:
  1.3 1.4 plan.1
  2.7 12.0 %all-to-all-start = ((s32[64,1,128]{2,1,0:T(1,128)}), s32[64,1,128]{2,1,0:T(1,128)S(1)}, u32[]{:S(2)}, u32[]{:S(2)}) async-start(s32[64,1,128]{2,1,0:T(1,128)} %bitcast.24), calls=%async_computation | async-start | bytes 65536 | tf_op jit(solution)/shard_map/all_to_all | solution.py:510
  15.5 2.4 %prep.1 = (bf16[128,64,128]{2,1,0:T(8,128)(2,1)S(1)}, bf16[8,128]{1,0:T(8,128)(2,1)S(1)}, bf16[64,128]{1,0:T(8,128)(2,1)S(1)}, bf16[64,128]{1,0:T(8,128)(2,1)S(1)}) custom-call(f32[64,16384]{1,0:T(8,128)} %refs_0_.3, s32[128,128]{1,0:T(8,128)S(1)} %bitcast.15), custom_call_target="tpu_custom_call" | custom-call | tf_op jit(solution)/shard_map/prep/pallas_call | solution.py:140
  17.9 5.1 %all-to-all-done = s32[64,1,128]{2,1,0:T(1,128)S(1)} async-done(((s32[64,1,128]{2,1,0:T(1,128)}), s32[64,1,128]{2,1,0:T(1,128)S(1)}, u32[]{:S(2)}, u32[]{:S(2)}) %all-to-all-start) | async-done | bytes 32800 | tf_op jit(solution)/shard_map/all_to_all | solution.py:510
  23.0 2.5 %pack.1 = bf16[64,136,128]{2,1,0:T(8,128)(2,1)} custom-call(s32[64,128]{1,0:T(8,128)S(1)} %bitcast.22, bf16[128,64,128]{2,1,0:T(8,128)(2,1)S(1)} %get-tuple-element.38.source_ref, bf16[8,128]{1,0:T(8,128)(2,1)S(1)} %get-tuple-element.39.slab_ref), custom_call_target="tpu_custom_call" | custom-call | tf_op jit(solution)/shard_map/pack/pallas_call | solution.py:181
  25.6 4.8 %all-to-all-start.1 = ((bf16[64,136,128]{2,1,0:T(8,128)(2,1)}), bf16[64,136,128]{2,1,0:T(8,128)(2,1)S(1)}, u32[]{:S(2)}, u32[]{:S(2)}) async-start(bf16[64,136,128]{2,1,0:T(8,128)(2,1)} %pack.1), calls=%async_computation.1 | async-start | bytes 4456448 | tf_op jit(solution)/shard_map/all_to_all | solution.py:518
  30.4 2.9 %collective-permute-start = (bf16[64,128]{1,0:T(8,128)(2,1)S(1)}, bf16[64,128]{1,0:T(8,128)(2,1)S(1)}, u32[]{:S(2)}, u32[]{:S(2)}) collective-permute-start(bf16[64,128]{1,0:T(8,128)(2,1)S(1)} %get-tuple-element.35), channel_id=1, source_target_pairs={{0,2},{2,4},{4,6},{6,8},{8,10},{10,12},{12,14},{14,16},{16,18},{18... | collective-permute-start | bytes 49160 | tf_op jit(solution)/shard_map/ppermute | solution.py:519
  33.3 1.3 collective-permute-start.1
  34.8 9.5 %band.3 = (f32[96,64,128]{2,1,0:T(8,128)}, f32[32,64,128]{2,1,0:T(8,128)S(1)}) custom-call(s32[1]{0:T(128)} %bitcast.first_ref.refs_0_, f32[64,16384]{1,0:T(8,128)} %refs_0_.3, bf16[128,3,128,128]{3,2,1,0:T(8,128)(2,1)} %refs_13_.5, s32[128,128]{1,0:T(8,128)S(1)} %bitcast.16, s32[64,1]{1,0:T(8,128)S(1)} %copy.28.refs_2_.refs_5_.refs_3_), custom_call_target="tpu_custom_call" | custom-call | tf_op jit(solution)/shard_map/band/pallas_call | solution.py:283
  45.2 13.5 %all-to-all-done.1.refs_10_ = bf16[64,136,128]{2,1,0:T(8,128)(2,1)S(1)} async-done(((bf16[64,136,128]{2,1,0:T(8,128)(2,1)}), bf16[64,136,128]{2,1,0:T(8,128)(2,1)S(1)}, u32[]{:S(2)}, u32[]{:S(2)}) %all-to-all-start.1) | async-done | bytes 2228256 | tf_op jit(solution)/shard_map/all_to_all | solution.py:518
  58.7 10.1 %finish.3 = (f32[64,16384]{1,0:T(8,128)}, bf16[64,128]{1,0:T(8,128)(2,1)S(1)}, bf16[64,128]{1,0:T(8,128)(2,1)S(1)}, bf16[64,136,128]{2,1,0:T(8,128)(2,1)}) custom-call(s32[1]{0:T(128)} %bitcast.first_ref.refs_0_, s32[1]{0:T(128)S(6)} %copy.30.count_ref.refs_1_, s32[1,512]{1,0:T(1,128)S(1)} %copy-done.2, s32[1,512]{1,0:T(1,128)S(1)} %copy-done.3, ...), custom_call_target="tpu_custom_call" | custom-call | tf_op jit(solution)/shard_map/finish/pallas_call | solution.py:459
  68.8 7.2 %all-to-all-start.2 = ((bf16[64,136,128]{2,1,0:T(8,128)(2,1)}), bf16[64,136,128]{2,1,0:T(8,128)(2,1)S(1)}, u32[]{:S(2)}, u32[]{:S(2)}) async-start(bf16[64,136,128]{2,1,0:T(8,128)(2,1)} %get-tuple-element.45), calls=%async_computation.2 | async-start | bytes 4456448 | tf_op jit(solution)/shard_map/all_to_all | solution.py:518
  76.0 2.9 %collective-permute-start.2 = (bf16[64,128]{1,0:T(8,128)(2,1)S(1)}, bf16[64,128]{1,0:T(8,128)(2,1)S(1)}, u32[]{:S(2)}, u32[]{:S(2)}) collective-permute-start(bf16[64,128]{1,0:T(8,128)(2,1)S(1)} %get-tuple-element.41), channel_id=1, source_target_pairs={{0,2},{2,4},{4,6},{6,8},{8,10},{10,12},{12,14},{14,16},{16,18},{18... | collective-permute-start | bytes 49160 | tf_op jit(solution)/shard_map/ppermute | solution.py:519
  79.0 1.5 collective-permute-start.3
  80.4 10.3 %band.4 = (f32[96,64,128]{2,1,0:T(8,128)}, f32[32,64,128]{2,1,0:T(8,128)S(1)}, f32[1,128]{1,0:T(1,128)S(1)}) custom-call(s32[1]{0:T(128)} %bitcast.first_ref.refs_0_, f32[64,16384]{1,0:T(8,128)} %get-tuple-element.43.rank_hbm.refs_0_, f32[64,16384]{1,0:T(8,128)} %refs_0_.3, bf16[128,3,128,128]{3,2,1,0:T(8,128)(2,1)} %refs_13_.5, s32[128,128]{1,0:T(8,128)S(1)} %bitcast.18, ...), custom_call_target="tpu_custom_call" | custom-call | tf_op jit(solution)/shard_map/band/pallas_call | solution.py:283
  90.7 13.1 %all-to-all-done.2.refs_10_ = bf16[64,136,128]{2,1,0:T(8,128)(2,1)S(1)} async-done(((bf16[64,136,128]{2,1,0:T(8,128)(2,1)}), bf16[64,136,128]{2,1,0:T(8,128)(2,1)S(1)}, u32[]{:S(2)}, u32[]{:S(2)}) %all-to-all-start.2) | async-done | bytes 2228256 | tf_op jit(solution)/shard_map/all_to_all | solution.py:518
  103.8 10.2 %finish.4 = (f32[64,16384]{1,0:T(8,128)}, bf16[64,128]{1,0:T(8,128)(2,1)S(1)}, bf16[64,128]{1,0:T(8,128)(2,1)S(1)}, bf16[64,136,128]{2,1,0:T(8,128)(2,1)}) custom-call(s32[1]{0:T(128)} %bitcast.first_ref.refs_0_, s32[1]{0:T(128)S(6)} %copy.30.count_ref.refs_1_, s32[1,512]{1,0:T(1,128)S(1)} %copy-done.2, s32[1,512]{1,0:T(1,128)S(1)} %copy-done.3, ...), custom_call_target="tpu_custom_call" | custom-call | tf_op jit(solution)/shard_map/finish/pallas_call | solution.py:459
  114.0 7.6 %all-to-all-start.3 = ((bf16[64,136,128]{2,1,0:T(8,128)(2,1)}), bf16[64,136,128]{2,1,0:T(8,128)(2,1)S(1)}, u32[]{:S(2)}, u32[]{:S(2)}) async-start(bf16[64,136,128]{2,1,0:T(8,128)(2,1)} %get-tuple-element.51), calls=%async_computation.3 | async-start | bytes 4456448 | tf_op jit(solution)/shard_map/all_to_all | solution.py:518
  121.7 2.9 %collective-permute-start.4 = (bf16[64,128]{1,0:T(8,128)(2,1)S(1)}, bf16[64,128]{1,0:T(8,128)(2,1)S(1)}, u32[]{:S(2)}, u32[]{:S(2)}) collective-permute-start(bf16[64,128]{1,0:T(8,128)(2,1)S(1)} %get-tuple-element.47), channel_id=1, source_target_pairs={{0,2},{2,4},{4,6},{6,8},{8,10},{10,12},{12,14},{14,16},{16,18},{18... | collective-permute-start | bytes 49160 | tf_op jit(solution)/shard_map/ppermute | solution.py:519
  125.9 10.3 %band.5 = (f32[96,64,128]{2,1,0:T(8,128)}, f32[32,64,128]{2,1,0:T(8,128)S(1)}, f32[1,128]{1,0:T(1,128)S(1)}) custom-call(s32[1]{0:T(128)} %bitcast.first_ref.refs_0_, f32[64,16384]{1,0:T(8,128)} %get-tuple-element.49.rank_hbm.refs_14_, f32[64,16384]{1,0:T(8,128)} %get-tuple-element.43.rank_hbm.refs_0_, bf16[128,3,128,128]{3,2,1,0:T(8,128)(2,1)} %refs_13_.5, ...), custom_call_target="tpu_custom_call" | custom-call | tf_op jit(solution)/shard_map/band/pallas_call | solution.py:283
  136.2 13.1 %all-to-all-done.3.refs_10_ = bf16[64,136,128]{2,1,0:T(8,128)(2,1)S(1)} async-done(((bf16[64,136,128]{2,1,0:T(8,128)(2,1)}), bf16[64,136,128]{2,1,0:T(8,128)(2,1)S(1)}, u32[]{:S(2)}, u32[]{:S(2)}) %all-to-all-start.3) | async-done | bytes 2228256 | tf_op jit(solution)/shard_map/all_to_all | solution.py:518
  149.3 10.6 %finish.5 = (f32[64,16384]{1,0:T(8,128)}, f32[128,1,256]{2,1,0:T(1,128)}) custom-call(s32[1]{0:T(128)} %bitcast.first_ref.refs_0_, s32[1]{0:T(128)S(6)} %copy.30.count_ref.refs_1_, s32[1,512]{1,0:T(1,128)S(1)} %copy-done.2, s32[1,512]{1,0:T(1,128)S(1)} %copy-done.3, s32[2,64]{1,0:T(2,128)S(1)} %slice_bitcast_fusion.refs_4_, ...), custom_call_target="tpu_custom_call" | custom-call | tf_op jit(solution)/shard_map/finish/pallas_call | solution.py:459
  159.9 9.9 %all-to-all-start.4 = ((f32[128,1,256]{2,1,0:T(1,128)}), f32[128,1,256]{2,1,0:T(1,128)S(1)}, u32[]{:S(2)}, u32[]{:S(2)}) async-start(f32[128,1,256]{2,1,0:T(1,128)} %get-tuple-element.56), calls=%async_computation.4 | async-start | bytes 262144 | tf_op jit(solution)/shard_map/all_to_all | solution.py:532
  169.7 9.8 %all-to-all-done.4.got_ref = f32[128,1,256]{2,1,0:T(1,128)S(1)} async-done(((f32[128,1,256]{2,1,0:T(1,128)}), f32[128,1,256]{2,1,0:T(1,128)S(1)}, u32[]{:S(2)}, u32[]{:S(2)}) %all-to-all-start.4) | async-done | bytes 131104 | tf_op jit(solution)/shard_map/all_to_all | solution.py:532
  (21 shorter events, 3.9 us)
Async XLA Ops:
  2.7 20.3 %all-to-all-start = ((s32[64,1,128]{2,1,0:T(1,128)}), s32[64,1,128]{2,1,0:T(1,128)S(1)}, u32[]{:S(2)}, u32[]{:S(2)}) async-start(s32[64,1,128]{2,1,0:T(1,128)} %bitcast.24), calls=%async_computation | async-start | bytes 65536 | tf_op jit(solution)/shard_map/all_to_all | solution.py:510
  14.7 0.8 copy-start
  25.5 9.1 %copy-start.4 = (s32[64]{0:T(128)S(1)}, s32[64]{0:T(128)}, u32[]{:S(2)}) copy-start(s32[64]{0:T(128)} %param.14) | copy-start | bytes 772
  25.5 9.2 %copy-start.1 = (s32[16384]{0:T(1024)S(1)}, s32[16384]{0:T(1024)}, u32[]{:S(2)}) copy-start(s32[16384]{0:T(1024)} %param.15) | copy-start | bytes 196612
  25.6 33.2 %all-to-all-start.1 = ((bf16[64,136,128]{2,1,0:T(8,128)(2,1)}), bf16[64,136,128]{2,1,0:T(8,128)(2,1)S(1)}, u32[]{:S(2)}, u32[]{:S(2)}) async-start(bf16[64,136,128]{2,1,0:T(8,128)(2,1)} %pack.1), calls=%async_computation.1 | async-start | bytes 4456448 | tf_op jit(solution)/shard_map/all_to_all | solution.py:518
  30.4 14.0 %collective-permute-start = (bf16[64,128]{1,0:T(8,128)(2,1)S(1)}, bf16[64,128]{1,0:T(8,128)(2,1)S(1)}, u32[]{:S(2)}, u32[]{:S(2)}) collective-permute-start(bf16[64,128]{1,0:T(8,128)(2,1)S(1)} %get-tuple-element.35), channel_id=1, source_target_pairs={{0,2},{2,4},{4,6},{6,8},{8,10},{10,12},{12,14},{14,16},{16,18},{18... | collective-permute-start | bytes 49160 | tf_op jit(solution)/shard_map/ppermute | solution.py:519
  33.3 11.9 %collective-permute-start.1 = (bf16[64,128]{1,0:T(8,128)(2,1)S(1)}, bf16[64,128]{1,0:T(8,128)(2,1)S(1)}, u32[]{:S(2)}, u32[]{:S(2)}) collective-permute-start(bf16[64,128]{1,0:T(8,128)(2,1)S(1)} %get-tuple-element.36), channel_id=1, source_target_pairs={{2,0},{4,2},{6,4},{8,6},{10,8},{12,10},{14,12},{16,14},{18,16},{20... | collective-permute-start | bytes 49160 | tf_op jit(solution)/shard_map/ppermute | solution.py:520
  34.7 24.0 %copy-start.2 = (s32[1,512]{1,0:T(1,128)S(1)}, s32[1,512]{1,0:T(1,128)}, u32[]{:S(2)}) copy-start(s32[1,512]{1,0:T(1,128)} %get-tuple-element.32.refs_2_) | copy-start | bytes 6148
  34.7 24.0 %copy-start.3 = (s32[1,512]{1,0:T(1,128)S(1)}, s32[1,512]{1,0:T(1,128)}, u32[]{:S(2)}) copy-start(s32[1,512]{1,0:T(1,128)} %get-tuple-element.33.refs_3_) | copy-start | bytes 6148
  68.8 35.0 %all-to-all-start.2 = ((bf16[64,136,128]{2,1,0:T(8,128)(2,1)}), bf16[64,136,128]{2,1,0:T(8,128)(2,1)S(1)}, u32[]{:S(2)}, u32[]{:S(2)}) async-start(bf16[64,136,128]{2,1,0:T(8,128)(2,1)} %get-tuple-element.45), calls=%async_computation.2 | async-start | bytes 4456448 | tf_op jit(solution)/shard_map/all_to_all | solution.py:518
  76.0 14.7 %collective-permute-start.2 = (bf16[64,128]{1,0:T(8,128)(2,1)S(1)}, bf16[64,128]{1,0:T(8,128)(2,1)S(1)}, u32[]{:S(2)}, u32[]{:S(2)}) collective-permute-start(bf16[64,128]{1,0:T(8,128)(2,1)S(1)} %get-tuple-element.41), channel_id=1, source_target_pairs={{0,2},{2,4},{4,6},{6,8},{8,10},{10,12},{12,14},{14,16},{16,18},{18... | collective-permute-start | bytes 49160 | tf_op jit(solution)/shard_map/ppermute | solution.py:519
  79.0 11.8 %collective-permute-start.3 = (bf16[64,128]{1,0:T(8,128)(2,1)S(1)}, bf16[64,128]{1,0:T(8,128)(2,1)S(1)}, u32[]{:S(2)}, u32[]{:S(2)}) collective-permute-start(bf16[64,128]{1,0:T(8,128)(2,1)S(1)} %get-tuple-element.42), channel_id=1, source_target_pairs={{2,0},{4,2},{6,4},{8,6},{10,8},{12,10},{14,12},{16,14},{18,16},{20... | collective-permute-start | bytes 49160 | tf_op jit(solution)/shard_map/ppermute | solution.py:520
  114.0 35.3 %all-to-all-start.3 = ((bf16[64,136,128]{2,1,0:T(8,128)(2,1)}), bf16[64,136,128]{2,1,0:T(8,128)(2,1)S(1)}, u32[]{:S(2)}, u32[]{:S(2)}) async-start(bf16[64,136,128]{2,1,0:T(8,128)(2,1)} %get-tuple-element.51), calls=%async_computation.3 | async-start | bytes 4456448 | tf_op jit(solution)/shard_map/all_to_all | solution.py:518
  121.7 14.5 %collective-permute-start.4 = (bf16[64,128]{1,0:T(8,128)(2,1)S(1)}, bf16[64,128]{1,0:T(8,128)(2,1)S(1)}, u32[]{:S(2)}, u32[]{:S(2)}) collective-permute-start(bf16[64,128]{1,0:T(8,128)(2,1)S(1)} %get-tuple-element.47), channel_id=1, source_target_pairs={{0,2},{2,4},{4,6},{6,8},{8,10},{10,12},{12,14},{14,16},{16,18},{18... | collective-permute-start | bytes 49160 | tf_op jit(solution)/shard_map/ppermute | solution.py:519
  124.6 11.6 %collective-permute-start.5 = (bf16[64,128]{1,0:T(8,128)(2,1)S(1)}, bf16[64,128]{1,0:T(8,128)(2,1)S(1)}, u32[]{:S(2)}, u32[]{:S(2)}) collective-permute-start(bf16[64,128]{1,0:T(8,128)(2,1)S(1)} %get-tuple-element.48), channel_id=1, source_target_pairs={{2,0},{4,2},{6,4},{8,6},{10,8},{12,10},{14,12},{16,14},{18,16},{20... | collective-permute-start | bytes 49160 | tf_op jit(solution)/shard_map/ppermute | solution.py:520
  159.9 19.7 %all-to-all-start.4 = ((f32[128,1,256]{2,1,0:T(1,128)}), f32[128,1,256]{2,1,0:T(1,128)S(1)}, u32[]{:S(2)}, u32[]{:S(2)}) async-start(f32[128,1,256]{2,1,0:T(1,128)} %get-tuple-element.56), calls=%async_computation.4 | async-start | bytes 262144 | tf_op jit(solution)/shard_map/all_to_all | solution.py:532
